TPU v7x, 256 devices: a whole 4x4x8 slice. The times are simulated.
256 devices in a mesh: seq: 64 (over x, z, core), head: 4 (over y).
Axes of the slice: x: 4, y: 4, z: 8, core: 2. Of those that a mesh axis runs over, the one named last changes fastest.
Arguments:
- q_latent: bfloat16 [16384, 1536], P('seq', 'head'), may hold values from -6 to 6
- kv_latent: bfloat16 [16384, 512], P('seq', 'head'), may hold values from -6 to 6
- k_rope: bfloat16 [16384, 64], P('seq'), may hold values from -6 to 6
- segment_ids: int32 [16384], P('seq'), may hold values from 0 to 63, as said below
- w_q_nope: bfloat16 [1536, 16384], P('seq', 'head'), may hold values from -6 to 6
- w_q_rope: bfloat16 [1536, 8192], P('seq', 'head'), may hold values from -6 to 6
- w_kv_nope: bfloat16 [512, 16384], P('seq', 'head'), may hold values from -6 to 6
- threshold: float32 [1], replicated, may hold values from 3.5 to 5.5
Outputs:
- new_q_nope: bfloat16 [1536, 16384], P('seq', 'head')
- new_q_rope: bfloat16 [1536, 8192], P('seq', 'head')
- new_kv_nope: bfloat16 [512, 16384], P('seq', 'head')
- head_max: float32 [128], P('head')
- row_max: float32 [16384, 128], P('seq', 'head')
Inputs may be any that keep to these rules, and one draw needn't show every extreme that they name: segment_ids never fall along the tokens and each document has 1 to 768 tokens.
All inputs are finite; a program needn't handle non-finite values.
Results may differ from a plain program's by a relative error of at most 0.0034.
Values may be sent and summed in bfloat16 or wider, within the bound.
No kernel may reach another device: no remote copies, remote signals or barrier semaphores. Data moves between devices by JAX's collectives and lax.ppermute only.
A program may use at most 128 MiB of HBM per device.

v0:
```python
import math

import jax
import jax.numpy as jnp
from jax import lax
from jax.sharding import PartitionSpec as P

D_NOPE = 128
D_ROPE = 64
QLORA = 1536
KVLORA = 512
REACH = 3


def joined_along(blocks, dim):
    blocks = jnp.moveaxis(blocks, 0, dim)
    lengths = blocks.shape
    return blocks.reshape(*lengths[:dim], lengths[dim] * lengths[dim + 1], *lengths[dim + 2 :])


def one_gather(arrays, axis, dims):
    ravelled = jnp.concatenate([a.reshape(-1) for a in arrays])
    lines, at, finished = (lax.all_gather(ravelled, axis), 0, [])
    for a, dim in zip(arrays, dims):
        blocks = lines[:, at : at + a.size].reshape(-1, *a.shape)
        finished.append(joined_along(blocks, dim))
        at += a.size
    return tuple(finished)


def side_by_side(arrays, axis, dim, along):
    both = jnp.concatenate(arrays, axis=along)
    result, at, finished = (lax.all_gather(both, axis, axis=dim, tiled=True), 0, [])
    for a in arrays:
        finished.append(lax.slice_in_dim(result, at, at + a.shape[along], axis=along))
        at += a.shape[along]
    return tuple(finished)


def shifted(block, axis, distance):
    devices = range(lax.axis_size(axis))
    route = [(i - distance, i) for i in devices if i - distance in devices]
    return lax.ppermute(block, axis, route)


def sent_to_all(value, axis):
    devices = lax.axis_size(axis)
    return lax.all_to_all(
        jnp.broadcast_to(value[None], (devices, *value.shape)), axis, 0, 0, tiled=True
    )


def over_copies(value, axis):
    everything = sent_to_all(value, axis)
    return jnp.max(everything, axis=0)


def score_max(query_nope, query_rope, key_nope, key_rope, allowed):
    nope = jnp.einsum("qhd,khd->hqk", query_nope, key_nope, preferred_element_type=jnp.float32)
    rope = jnp.einsum("qhd,kd->hqk", query_rope, key_rope, preferred_element_type=jnp.float32)
    scores = (nope + rope) * (1.0 / math.sqrt(D_NOPE + D_ROPE))
    return jnp.max(jnp.where(allowed[None], scores, jnp.float32(-1e30)), axis=2)


def masked_max(compute, operands):
    return compute(*operands)


def local(q_latent, kv_latent, k_rope, segment_ids, w_q_nope, w_q_rope, w_kv_nope, threshold):
    q_whole, kv_whole = one_gather((q_latent, kv_latent), "head", (1, 1))
    rows = q_whole.shape[0]
    heads = w_q_nope.shape[1] // D_NOPE
    q_scale = 1.0 / math.sqrt(QLORA)
    k_scale = 1.0 / math.sqrt(KVLORA)
    place = lax.axis_index("seq")
    full_nope, full_rope, full_kv = (
        *side_by_side((w_q_nope, w_q_rope), "seq", 0, 1),
        lax.all_gather(w_kv_nope, "seq", axis=0, tiled=True),
    )
    query_nope = (
        (jnp.dot(q_whole, full_nope, preferred_element_type=jnp.float32) * q_scale)
        .astype(jnp.bfloat16)
        .reshape(rows, heads, D_NOPE)
    )
    query_rope = (
        (jnp.dot(q_whole, full_rope, preferred_element_type=jnp.float32) * q_scale)
        .astype(jnp.bfloat16)
        .reshape(rows, heads, D_ROPE)
    )

    def expand(latent):
        return (
            (jnp.dot(latent, full_kv, preferred_element_type=jnp.float32) * k_scale)
            .astype(jnp.bfloat16)
            .reshape(rows, heads, D_NOPE)
        )

    def tokens_max(moving_first, moving_rope, allowed):
        key_nope = expand(moving_first)
        return score_max(query_nope, query_rope, key_nope, moving_rope, allowed)

    query_pos = place * rows + jnp.arange(rows, dtype=jnp.int32)
    moving = (kv_whole, k_rope)
    moving_seg = segment_ids
    running = jnp.full((heads, rows), -1e30, jnp.float32)
    for back in range(REACH + 1):
        if back > 0:
            moving = shifted((moving[0], moving[1]), "seq", 1)
            moving_seg = shifted(moving_seg, "seq", 1)
        key_pos = (place - back) * rows + jnp.arange(rows, dtype=jnp.int32)
        allowed = (
            (segment_ids[:, None] == moving_seg[None, :])
            & (key_pos[None, :] <= query_pos[:, None])
            & (key_pos[None, :] >= 0)
        )
        found = masked_max(tokens_max, (moving[0], moving[1], allowed))
        running = jnp.maximum(running, found)
    row_max = running.T
    local_heads = jnp.max(running, axis=1)
    head_max = over_copies(local_heads, "seq")
    clip = threshold[0] / jnp.maximum(head_max, threshold[0])
    root = jnp.sqrt(clip)
    new_q_nope = (w_q_nope.astype(jnp.float32) * jnp.repeat(root, D_NOPE)[None, :]).astype(
        jnp.bfloat16
    )
    new_q_rope = (w_q_rope.astype(jnp.float32) * jnp.repeat(clip, D_ROPE)[None, :]).astype(
        jnp.bfloat16
    )
    new_kv_nope = (w_kv_nope.astype(jnp.float32) * jnp.repeat(root, D_NOPE)[None, :]).astype(
        jnp.bfloat16
    )
    return (new_q_nope, new_q_rope, new_kv_nope, head_max, row_max)


def solution(mesh):
    in_specs = (
        P("seq", "head"),
        P("seq", "head"),
        P("seq", None),
        P("seq"),
        P("seq", "head"),
        P("seq", "head"),
        P("seq", "head"),
        P(),
    )
    out_specs = (P("seq", "head"), P("seq", "head"), P("seq", "head"), P("head"), P("seq", "head"))
    return jax.shard_map(local, mesh=mesh, in_specs=in_specs, out_specs=out_specs, check_vma=False)
```

profile of v0, /device:TPU:1, one launch (start us, length us, event | category | flops | bytes accessed | tf_op | source)
XLA Modules:
  0.0 283.7 jit_solution(593446844976654654)
XLA Ops:
  8.3 1.6 pad_maximum_fusion.1
  10.6 1.7 pad_maximum_fusion
  12.4 4.9 %collective-permute-start = (s32[256]{0:T(256)}, s32[256]{0:T(256)S(1)}, u32[]{:S(2)}, u32[]{:S(2)}) collective-permute-start(s32[256]{0:T(256)} %param.11), channel_id=1, source_target_pairs={{0,4},{4,8},{8,12},{12,16},{16,20},{20,24},{24,28},{28,32},{32,36}... | collective-permute-start | bytes 3080 | tf_op jit(solution)/shard_map/ppermute | solution.py:43
  17.3 1.9 collective-permute-start.2
  19.3 20.2 %all-gather.9.cloned.1.call-done = bf16[524288]{0:T(1024)(128)(2,1)} async-done(((bf16[131072]{0:T(1024)(128)(2,1)}), bf16[524288]{0:T(1024)(128)(2,1)}) %all-gather.9.cloned.1.call-update) | async-done | bytes 1048592 | tf_op jit(solution)/shard_map/all_gather | solution.py:23
  39.4 1.6 reshape.376
  41.3 4.6 %collective-permute-start.1 = (bf16[256,512]{0,1:T(8,128)(2,1)S(1)}, bf16[256,512]{0,1:T(8,128)(2,1)S(1)}, u32[]{:S(2)}, u32[]{:S(2)}) collective-permute-start(bf16[256,512]{0,1:T(8,128)(2,1)S(1)} %bitcast.115), channel_id=1, source_target_pairs={{0,4},{4,8},{8,12},{12,16},{16,20},{20,24},{24,28},{28,32},{32,36}... | collective-permute-start | bytes 786440 | tf_op jit(solution)/shard_map/ppermute | solution.py:43
  46.0 1.9 collective-permute-start.3
  48.0 1.3 collective-permute-done.3
  49.3 4.4 %collective-permute-start.6 = (s32[256]{0:T(256)S(1)}, s32[256]{0:T(256)S(1)}, u32[]{:S(2)}, u32[]{:S(2)}) collective-permute-start(s32[256]{0:T(256)S(1)} %collective-permute-done.3), channel_id=1, source_target_pairs={{0,4},{4,8},{8,12},{12,16},{16,20},{20,24},{24,28},{28,32},{32,36}... | collective-permute-start | bytes 3080 | tf_op jit(solution)/shard_map/ppermute | solution.py:43
  53.7 1.9 collective-permute-start.4
  55.7 3.6 %collective-permute-start.5 = (bf16[256,64]{0,1:T(8,128)(2,1)S(1)}, bf16[256,64]{0,1:T(8,128)(2,1)S(1)}, u32[]{:S(2)}, u32[]{:S(2)}) collective-permute-start(bf16[256,64]{0,1:T(8,128)(2,1)S(1)} %collective-permute-done.2), channel_id=1, source_target_pairs={{0,4},{4,8},{8,12},{12,16},{16,20},{20,24},{24,28},{28,32},{32,36}... | collective-permute-start | bytes 98312 | tf_op jit(solution)/shard_map/ppermute | solution.py:43
  60.3 4.2 %collective-permute-start.8 = (bf16[256,64]{0,1:T(8,128)(2,1)S(1)}, bf16[256,64]{0,1:T(8,128)(2,1)S(1)}, u32[]{:S(2)}, u32[]{:S(2)}) collective-permute-start(bf16[256,64]{0,1:T(8,128)(2,1)S(1)} %collective-permute-done.5), channel_id=1, source_target_pairs={{0,4},{4,8},{8,12},{12,16},{16,20},{20,24},{24,28},{28,32},{32,36}... | collective-permute-start | bytes 98312 | tf_op jit(solution)/shard_map/ppermute | solution.py:43
  65.2 1.9 collective-permute-start.7
  67.1 55.8 %all-gather.7.cloned.1.call-done = bf16[512,4096]{1,0:T(8,128)(2,1)} async-done(((bf16[8,4096]{1,0:T(8,128)(2,1)}), bf16[512,4096]{1,0:T(8,128)(2,1)}) %all-gather.7.cloned.1.call-update) | async-done | bytes 4194320 | tf_op jit(solution)/shard_map/all_gather | solution.py:78
  122.9 5.1 %fusion.52 = bf16[32,32,8,128]{3,2,1,0:T(8,128)(2,1)} fusion(bf16[256,512]{0,1:T(8,128)(2,1)S(1)} %collective-permute-done.4, bf16[512,4096]{1,0:T(8,128)(2,1)} %all-gather.7.cloned.1.call-done), kind=kOutput, calls=%fused_computation.50 | convolution fusion | flops 1075838976 | bytes 6553600 | tf_op jit(solution)/shard_map/dot_general | solution.py:93
  128.0 2.8 fusion.53
  130.8 2.8 fusion.54
  133.6 1.4 fusion.51
  135.0 92.9 %all-gather.5.cloned.1.call-done = bf16[1536,6144]{1,0:T(8,128)(2,1)} async-done(((bf16[24,6144]{1,0:T(8,128)(2,1)}), bf16[1536,6144]{1,0:T(8,128)(2,1)}) %all-gather.5.cloned.1.call-update) | async-done | bytes 18874384 | tf_op jit(solution)/shard_map/all_gather | solution.py:33
  227.9 5.7 %fusion.29 = bf16[256,2048]{1,0:T(8,128)(2,1)} fusion(bf16[256,1536]{0,1:T(8,128)(2,1)S(1)} %bitcast.122, bf16[1536,6144]{1,0:T(8,128)(2,1)} %all-gather.5.cloned.1.call-done), kind=kOutput, calls=%fused_computation.31 | convolution fusion | flops 1611661312 | bytes 8126464 | tf_op jit(solution)/shard_map/dot_general | solution.py:86
  233.6 1.7 copy.71
  235.2 8.6 %fusion.48 = bf16[32,32,8,128]{3,2,1,0:T(8,128)(2,1)S(1)} fusion(bf16[256,1536]{0,1:T(8,128)(2,1)} %bitcast.123, bf16[1536,6144]{1,0:T(8,128)(2,1)} %all-gather.5.cloned.1.call-done), kind=kOutput, calls=%fused_computation.48 | convolution fusion | flops 3223322624 | bytes 15466496 | tf_op jit(solution)/shard_map/dot_general | solution.py:81
  243.9 1.3 fusion.41
  246.7 2.9 %fusion.35 = f32[32,256,256]{1,2,0:T(8,128)S(1)} fusion(bf16[32,32,8,128]{3,2,1,0:T(8,128)(2,1)} %fusion.52, bf16[32,32,8,128]{3,2,1,0:T(8,128)(2,1)S(1)} %fusion.48), kind=kOutput, calls=%fused_computation.35 | convolution fusion | flops 536870912 | bytes 12582912 | tf_op jit(solution)/shard_map/qhd,khd->hqk/dot_general | solution.py:59
  249.7 1.7 fusion.13
  251.4 1.7 fusion.10
  253.1 1.8 fusion.7
  254.9 1.6 fusion.32
  256.5 1.8 fusion.4
  259.7 6.0 %all-to-all-start = ((f32[64,1,32]{2,1,0:T(1,128)}), f32[64,1,32]{2,1,0:T(1,128)S(1)}, u32[]{:S(2)}, u32[]{:S(2)}) async-start(f32[64,1,32]{2,1,0:T(1,128)} %broadcast_in_dim.76), calls=%async_computation | async-start | bytes 65536 | tf_op jit(solution)/shard_map/all_to_all | solution.py:48
  266.3 8.6 %all-to-all-done = f32[64,1,32]{2,1,0:T(1,128)S(1)} async-done(((f32[64,1,32]{2,1,0:T(1,128)}), f32[64,1,32]{2,1,0:T(1,128)S(1)}, u32[]{:S(2)}, u32[]{:S(2)}) %all-to-all-start) | async-done | bytes 8224 | tf_op jit(solution)/shard_map/all_to_all | solution.py:48
  (57 shorter events, 9.2 us)
Async XLA Ops:
  7.2 52.1 %copy-start.7 = (s32[256]{0:T(256)S(1)}, s32[256]{0:T(256)}, u32[]{:S(2)}) copy-start(s32[256]{0:T(256)} %param.11) | copy-start | bytes 3076
  7.2 32.2 %all-gather.9.cloned.1.call-start = ((), (), s32[]{:S(2)}) async-start(), calls=%async_computation.3 | async-start | bytes 1310720 | tf_op jit(solution)/shard_map/all_gather | solution.py:23
  9.8 113.0 %all-gather.7.cloned.1.call-start = ((), (), s32[]{:S(2)}) async-start(), calls=%async_computation.2 | async-start | bytes 4259840 | tf_op jit(solution)/shard_map/all_gather | solution.py:78
  10.6 217.3 %all-gather.5.cloned.1.call-start = ((), (), s32[]{:S(2)}) async-start(), calls=%async_computation.1 | async-start | bytes 19169280 | tf_op jit(solution)/shard_map/all_gather | solution.py:33
  12.4 33.7 %collective-permute-start = (s32[256]{0:T(256)}, s32[256]{0:T(256)S(1)}, u32[]{:S(2)}, u32[]{:S(2)}) collective-permute-start(s32[256]{0:T(256)} %param.11), channel_id=1, source_target_pairs={{0,4},{4,8},{8,12},{12,16},{16,20},{20,24},{24,28},{28,32},{32,36}... | collective-permute-start | bytes 3080 | tf_op jit(solution)/shard_map/ppermute | solution.py:43
  17.3 38.4 %collective-permute-start.2 = (bf16[256,64]{0,1:T(8,128)(2,1)}, bf16[256,64]{0,1:T(8,128)(2,1)S(1)}, u32[]{:S(2)}, u32[]{:S(2)}) collective-permute-start(bf16[256,64]{0,1:T(8,128)(2,1)} %param.10), channel_id=1, source_target_pairs={{0,4},{4,8},{8,12},{12,16},{16,20},{20,24},{24,28},{28,32},{32,36}... | collective-permute-start | bytes 98312 | tf_op jit(solution)/shard_map/ppermute | solution.py:43
  41.3 12.4 %collective-permute-start.1 = (bf16[256,512]{0,1:T(8,128)(2,1)S(1)}, bf16[256,512]{0,1:T(8,128)(2,1)S(1)}, u32[]{:S(2)}, u32[]{:S(2)}) collective-permute-start(bf16[256,512]{0,1:T(8,128)(2,1)S(1)} %bitcast.115), channel_id=1, source_target_pairs={{0,4},{4,8},{8,12},{12,16},{16,20},{20,24},{24,28},{28,32},{32,36}... | collective-permute-start | bytes 786440 | tf_op jit(solution)/shard_map/ppermute | solution.py:43
  46.0 3.3 %collective-permute-start.3 = (s32[256]{0:T(256)S(1)}, s32[256]{0:T(256)S(1)}, u32[]{:S(2)}, u32[]{:S(2)}) collective-permute-start(s32[256]{0:T(256)S(1)} %collective-permute-done), channel_id=1, source_target_pairs={{0,4},{4,8},{8,12},{12,16},{16,20},{20,24},{24,28},{28,32},{32,36}... | collective-permute-start | bytes 3080 | tf_op jit(solution)/shard_map/ppermute | solution.py:43
  49.3 9.9 %collective-permute-start.6 = (s32[256]{0:T(256)S(1)}, s32[256]{0:T(256)S(1)}, u32[]{:S(2)}, u32[]{:S(2)}) collective-permute-start(s32[256]{0:T(256)S(1)} %collective-permute-done.3), channel_id=1, source_target_pairs={{0,4},{4,8},{8,12},{12,16},{16,20},{20,24},{24,28},{28,32},{32,36}... | collective-permute-start | bytes 3080 | tf_op jit(solution)/shard_map/ppermute | solution.py:43
  53.7 11.4 %collective-permute-start.4 = (bf16[256,512]{0,1:T(8,128)(2,1)S(1)}, bf16[256,512]{0,1:T(8,128)(2,1)S(1)}, u32[]{:S(2)}, u32[]{:S(2)}) collective-permute-start(bf16[256,512]{0,1:T(8,128)(2,1)S(1)} %collective-permute-done.1), channel_id=1, source_target_pairs={{0,4},{4,8},{8,12},{12,16},{16,20},{20,24},{24,28},{28,32},{32,36}... | collective-permute-start | bytes 786440 | tf_op jit(solution)/shard_map/ppermute | solution.py:43
  55.7 4.6 %collective-permute-start.5 = (bf16[256,64]{0,1:T(8,128)(2,1)S(1)}, bf16[256,64]{0,1:T(8,128)(2,1)S(1)}, u32[]{:S(2)}, u32[]{:S(2)}) collective-permute-start(bf16[256,64]{0,1:T(8,128)(2,1)S(1)} %collective-permute-done.2), channel_id=1, source_target_pairs={{0,4},{4,8},{8,12},{12,16},{16,20},{20,24},{24,28},{28,32},{32,36}... | collective-permute-start | bytes 98312 | tf_op jit(solution)/shard_map/ppermute | solution.py:43
  60.3 196.2 %collective-permute-start.8 = (bf16[256,64]{0,1:T(8,128)(2,1)S(1)}, bf16[256,64]{0,1:T(8,128)(2,1)S(1)}, u32[]{:S(2)}, u32[]{:S(2)}) collective-permute-start(bf16[256,64]{0,1:T(8,128)(2,1)S(1)} %collective-permute-done.5), channel_id=1, source_target_pairs={{0,4},{4,8},{8,12},{12,16},{16,20},{20,24},{24,28},{28,32},{32,36}... | collective-permute-start | bytes 98312 | tf_op jit(solution)/shard_map/ppermute | solution.py:43
  65.1 162.8 %copy-start.3 = (bf16[256,4,384]{0,2,1:T(8,128)(2,1)}, bf16[256,4,384]{0,2,1:T(8,128)(2,1)S(1)}, u32[]{:S(2)}) copy-start(bf16[256,4,384]{0,2,1:T(8,128)(2,1)S(1)} %copy.67) | copy-start | bytes 2359300
  65.2 68.4 %collective-permute-start.7 = (bf16[256,512]{0,1:T(8,128)(2,1)S(1)}, bf16[256,512]{0,1:T(8,128)(2,1)S(1)}, u32[]{:S(2)}, u32[]{:S(2)}) collective-permute-start(bf16[256,512]{0,1:T(8,128)(2,1)S(1)} %collective-permute-done.4), channel_id=1, source_target_pairs={{0,4},{4,8},{8,12},{12,16},{16,20},{20,24},{24,28},{28,32},{32,36}... | collective-permute-start | bytes 786440 | tf_op jit(solution)/shard_map/ppermute | solution.py:43
  122.9 5.1 %copy-start = (bf16[512,4096]{1,0:T(8,128)(2,1)S(1)}, bf16[512,4096]{1,0:T(8,128)(2,1)}, u32[]{:S(2)}) copy-start(bf16[512,4096]{1,0:T(8,128)(2,1)} %all-gather.7.cloned.1.call-done) | copy-start | bytes 12582916
  235.2 8.6 %copy-start.2 = (bf16[32,32,8,128]{3,2,1,0:T(8,128)(2,1)S(1)}, bf16[32,32,8,128]{3,2,1,0:T(8,128)(2,1)}, u32[]{:S(2)}) copy-start(bf16[32,32,8,128]{3,2,1,0:T(8,128)(2,1)} %fusion.54) | copy-start | bytes 6291460
  243.9 1.6 copy-start.1
  246.7 2.9 %copy-start.9 = (bf16[256,64]{0,1:T(8,128)(2,1)S(1)}, bf16[256,64]{0,1:T(8,128)(2,1)}, u32[]{:S(2)}) copy-start(bf16[256,64]{0,1:T(8,128)(2,1)} %param.10) | copy-start | bytes 98308
  256.5 18.5 %copy-start.6 = (bf16[8,4096]{1,0:T(8,128)(2,1)S(1)}, bf16[8,4096]{1,0:T(8,128)(2,1)}, u32[]{:S(2)}) copy-start(bf16[8,4096]{1,0:T(8,128)(2,1)} %param.14) | copy-start | bytes 196612
  256.5 19.2 %copy-start.4 = (bf16[24,4096]{1,0:T(8,128)(2,1)S(1)}, bf16[24,4096]{1,0:T(8,128)(2,1)}, u32[]{:S(2)}) copy-start(bf16[24,4096]{1,0:T(8,128)(2,1)} %param.12) | copy-start | bytes 589828
  256.5 20.0 %copy-start.5 = (bf16[24,2048]{1,0:T(8,128)(2,1)S(1)}, bf16[24,2048]{1,0:T(8,128)(2,1)}, u32[]{:S(2)}) copy-start(bf16[24,2048]{1,0:T(8,128)(2,1)} %param.13) | copy-start | bytes 294916
  259.7 15.2 %all-to-all-start = ((f32[64,1,32]{2,1,0:T(1,128)}), f32[64,1,32]{2,1,0:T(1,128)S(1)}, u32[]{:S(2)}, u32[]{:S(2)}) async-start(f32[64,1,32]{2,1,0:T(1,128)} %broadcast_in_dim.76), calls=%async_computation | async-start | bytes 65536 | tf_op jit(solution)/shard_map/all_to_all | solution.py:48
  274.9 2.3 copy-start.8
Sparse Core Ops, SparseCore 0:
  9.9 29.4 all-gather.8
  42.2 80.6 all-gather.6
  125.6 102.2 all-gather.4
where the time goes:
time: 284 us
  waiting for transfers between devices  180 us (63%)
  matrix products  40.4 us (14%)
  starting transfers between devices  35.5 us (12%)
  between operations  14.8 us (5%)
  other arithmetic  6.78 us (2%)
  local copies, waits for them, and re-layouts  6.44 us (2%)
    all_gather x1, waiting for transfers between devices, side_by_side(): lax.all_gather(both, axis, axis=dim, tiled=True)  92.9 us
    all_gather x1, waiting for transfers between devices, local(): lax.all_gather(w_kv_nope, 'seq', axis=0, tiled=True)  55.8 us
    ppermute x9, starting transfers between devices, shifted(): return lax.ppermute(block, axis, route)  29.4 us
    all_gather x1, waiting for transfers between devices, one_gather(): lines, at, finished = (lax.all_gather(ravelled, axis), 0, [])  20.2 us
    dot_general x4, matrix products, expand(): jnp.dot(latent, full_kv, preferred_element_type=jnp.float32) * k_scale  12.1 us
    dot_general x1, matrix products, local(): jnp.dot(q_whole, full_nope, preferred_element_type=jnp.float32) * q_scale  8.62 us
    all_to_all x1, waiting for transfers between devices, sent_to_all(): lax.all_to_all(jnp.broadcast_to(value[None], (devices, *value.shape)), ax...  8.56 us
    dot_general x4, matrix products, score_max(): jnp.einsum('qhd,khd->hqk', query_nope, key_nope, preferred_element_type=j...  7 us
  transfers between devices with their start and end apart: 13, of which 6 were waited for; matrix products, arithmetic and copies ran while one was open for 16% of the time, Pallas kernels for 0%

commit v1 on v0

v1 whole, which is shorter than its diff:
```python
import math

import jax
import jax.numpy as jnp
from jax import lax
from jax.experimental import pallas as pl
from jax.experimental.pallas import tpu as pltpu
from jax.sharding import Mesh
from jax.sharding import PartitionSpec as P

D_NOPE = 128
D_ROPE = 64
QLORA = 1536
KVLORA = 512
BLK = 256
HEADS = 8
NX = 4
Q_COLS = HEADS * (D_NOPE + D_ROPE)
W_COLS = 3 * Q_COLS + HEADS * D_NOPE
NEG = -1e30
SEQ = ("x", "z", "c")


def place_of(block, shift=0):
    group, i = divmod(block, 4)
    group = (group + shift) % 16
    xo, zh = divmod(group, 4)
    x, z, c = (i + xo) % 4, zh * 2 + (xo & 1), xo >> 1
    return (x * 8 + z) * 2 + c


OWN_ROUTE = [(b, place_of(b)) for b in range(64)]
HALO_ROUTE = [(b, place_of(b, 1)) for b in range(60) if b % 4]


def home_route(slot):
    route = []
    for b in range(64):
        xzc = place_of(b)
        x, zc = divmod(xzc, 16)
        route.append((((x + slot) % 4) * 16 + zc, b))
    return route


HOME_ROUTES = [home_route(d) for d in range(4)]


def ring(value, axis, distance):
    n = lax.axis_size(axis)
    return lax.ppermute(value, axis, [(i, (i + distance) % n) for i in range(n)])


def pack_weights_kernel(x_ref, wn_ref, wr_ref, wk_ref, *out_refs):
    for d in range(4):
        to = lax.rem(x_ref[0] + d, 4)
        out = out_refs[d]
        for t in range(3):
            rows = pl.ds(t * 8, 8)
            at = t * Q_COLS
            out[:, at : at + 1024] = wn_ref[rows, pl.ds(pl.multiple_of(to * 1024, 1024), 1024)]
            out[:, at + 1024 : at + 1536] = wr_ref[rows, pl.ds(pl.multiple_of(to * 512, 512), 512)]
        out[:, 3 * Q_COLS :] = wk_ref[:, pl.ds(pl.multiple_of(to * 1024, 1024), 1024)]


def pack_weights(x, wn, wr, wk):
    vmem = pl.BlockSpec(memory_space=pltpu.VMEM)
    return pl.pallas_call(
        pack_weights_kernel,
        out_shape=[jax.ShapeDtypeStruct((8, W_COLS), jnp.bfloat16)] * 4,
        in_specs=[pl.BlockSpec(memory_space=pltpu.SMEM), vmem, vmem, vmem],
        out_specs=[vmem] * 4,
        name="pack_weights",
    )(x, wn, wr, wk)


def pack_latents_kernel(q_ref, kv_ref, rope_ref, seg_ref, own_ref, halo_ref):
    old = lax.broadcasted_iota(jnp.int32, (384, 384), 0)
    new = lax.broadcasted_iota(jnp.int32, (384, 384), 1)
    t, rest = new // 128, new % 128
    pick = old == (rest // 8) * 24 + t * 8 + rest % 8
    chosen = jnp.where(pick, 1.0, 0.0).astype(jnp.bfloat16)
    own_ref[:, :384] = jnp.dot(q_ref[...], chosen, preferred_element_type=jnp.float32).astype(
        jnp.bfloat16
    )
    kv = kv_ref[...]
    own_ref[:, 384:512] = kv
    halo_ref[:, :128] = kv
    seg = jnp.broadcast_to((seg_ref[...] + 1).astype(jnp.float32), (128, BLK))
    column = jnp.transpose(seg).astype(jnp.bfloat16)
    rope = rope_ref[...]
    for ref, at in ((own_ref, 512), (halo_ref, 128)):
        ref[:, at : at + 128] = column
        ref[:, at : at + 64] = rope


def pack_latents(q, kv, rope, seg):
    vmem = pl.BlockSpec(memory_space=pltpu.VMEM)
    return pl.pallas_call(
        pack_latents_kernel,
        out_shape=[
            jax.ShapeDtypeStruct((BLK, 640), jnp.bfloat16),
            jax.ShapeDtypeStruct((BLK, 256), jnp.bfloat16),
        ],
        in_specs=[vmem] * 4,
        out_specs=[vmem] * 2,
        name="pack_latents",
    )(q, kv, rope, seg.reshape(1, BLK))


def main_kernel(
    place_ref, w_ref, ql_ref, kv_ref, rs_ref, rm_ref, hm_ref,
    wn, wr, wk, kn, kr, qn, qr, bias, sems,
):
    i_own, delta = place_ref[0], place_ref[1]
    copies = []
    for e in range(4):
        slot = lax.rem(delta + e, 4)
        copies.append(
            pltpu.make_async_copy(
                w_ref.at[slot, :, pl.ds(3 * Q_COLS, 1024)], wk.at[pl.ds(e * 128, 128), :], sems.at[e]
            )
        )
    for e in range(4):
        slot = lax.rem(delta + e, 4)
        for t in range(3):
            rows = pl.ds((e * 3 + t) * 128, 128)
            n = 4 + 2 * (e * 3 + t)
            copies.append(
                pltpu.make_async_copy(
                    w_ref.at[slot, :, pl.ds(t * Q_COLS, 1024)], wn.at[rows, :], sems.at[n]
                )
            )
            copies.append(
                pltpu.make_async_copy(
                    w_ref.at[slot, :, pl.ds(t * Q_COLS + 1024, 512)], wr.at[rows, :], sems.at[n + 1]
                )
            )
    for copy in copies:
        copy.start()

    lane = lax.broadcasted_iota(jnp.int32, (BLK, 128), 1)
    seg_rows = []
    for d in range(8):
        rs = rs_ref[pl.ds(d * BLK, BLK), :].astype(jnp.float32)
        kr[0, d] = jnp.where(lane < 64, rs, 0.0).astype(jnp.bfloat16)
        kr[1, d] = jnp.where(lane >= 64, pltpu.roll(rs, 64, 1), 0.0).astype(jnp.bfloat16)
        if d < 4:
            seg_rows.append(jnp.transpose(rs)[64:65, :])
    k_iota = lax.broadcasted_iota(jnp.int32, (BLK, BLK), 0)
    q_iota = lax.broadcasted_iota(jnp.int32, (BLK, BLK), 1)
    which = []
    for d in range(4):
        i_q = lax.rem(i_own - d + 4, 4)
        for f in range(4):
            i_k = lax.rem(i_own - f + 4, 4)
            at = jnp.where(i_k > i_q, f + 4, f)
            which.append(at)
            seg_k = rs_ref[pl.ds(pl.multiple_of(at * BLK, BLK), BLK), 64:65].astype(jnp.float32)
            allowed = seg_k == seg_rows[d]
            if d == f:
                allowed = allowed & (k_iota <= q_iota)
            bias[d, f] = jnp.where(allowed, 0.0, NEG)

    for copy in copies[:4]:
        copy.wait()
    k_scale = 1.0 / math.sqrt(KVLORA)
    for b in range(8):
        kv = kv_ref[pl.ds(b * BLK, BLK), :]
        kn[b] = (jnp.dot(kv, wk[...], preferred_element_type=jnp.float32) * k_scale).astype(
            jnp.bfloat16
        )
    for copy in copies[4:]:
        copy.wait()
    q_scale = 1.0 / math.sqrt(QLORA)
    for d in range(4):
        ql = ql_ref[pl.ds(d * BLK, BLK), :]
        qn[d] = (jnp.dot(ql, wn[...], preferred_element_type=jnp.float32) * q_scale).astype(
            jnp.bfloat16
        )
        qr[d] = (jnp.dot(ql, wr[...], preferred_element_type=jnp.float32) * q_scale).astype(
            jnp.bfloat16
        )

    score_scale = 1.0 / math.sqrt(D_NOPE + D_ROPE)
    head_best = []
    for h in range(HEADS):
        best_h = None
        for d in range(4):
            query = jnp.concatenate(
                [qn[d, :, h * 128 : h * 128 + 128], qr[d, :, (h // 2) * 128 : (h // 2) * 128 + 128]],
                axis=1,
            )
            best = None
            for f in range(4):
                at = which[d * 4 + f]
                keys = jnp.concatenate([kn[at, :, h * 128 : h * 128 + 128], kr[h % 2, at]], axis=1)
                s = lax.dot_general(
                    keys, query, (((1,), (1,)), ((), ())), preferred_element_type=jnp.float32
                )
                s = jnp.max((s + bias[d, f]).reshape(BLK // 8, 8, BLK), axis=0)
                best = s if best is None else jnp.maximum(best, s)
            row = jnp.max(best, axis=0, keepdims=True) * score_scale
            rm_ref[d, h : h + 1, :] = row
            best_h = row if best_h is None else jnp.maximum(best_h, row)
        head_best.append(jnp.max(best_h, axis=1, keepdims=True))
    hm_lane = lax.broadcasted_iota(jnp.int32, (1, 128), 1)
    line = jnp.zeros((1, 128), jnp.float32)
    for h in range(HEADS):
        line = jnp.where(hm_lane == h, head_best[h], line)
    hm_ref[...] = jnp.broadcast_to(line, hm_ref.shape)


def main(place, w, ql, kv, rs):
    vmem = pl.BlockSpec(memory_space=pltpu.VMEM)
    bf16, f32 = jnp.bfloat16, jnp.float32
    return pl.pallas_call(
        main_kernel,
        out_shape=[
            jax.ShapeDtypeStruct((4, HEADS, BLK), f32),
            jax.ShapeDtypeStruct((64, 128), f32),
        ],
        in_specs=[
            pl.BlockSpec(memory_space=pltpu.SMEM),
            pl.BlockSpec(memory_space=pl.ANY),
            vmem,
            vmem,
            vmem,
        ],
        out_specs=[vmem, vmem],
        scratch_shapes=[
            pltpu.VMEM((QLORA, 1024), bf16),
            pltpu.VMEM((QLORA, 512), bf16),
            pltpu.VMEM((KVLORA, 1024), bf16),
            pltpu.VMEM((8, BLK, 1024), bf16),
            pltpu.VMEM((2, 8, BLK, 128), bf16),
            pltpu.VMEM((4, BLK, 1024), bf16),
            pltpu.VMEM((4, BLK, 512), bf16),
            pltpu.VMEM((4, 4, BLK, BLK), f32),
            pltpu.SemaphoreType.DMA((28,)),
        ],
        compiler_params=pltpu.CompilerParams(vmem_limit_bytes=48 * 2**20),
        cost_estimate=pl.CostEstimate(
            flops=2 * 2048 * 512 * 1024 + 2 * 1024 * 1536 * 1536 + 2 * 128 * 256**3,
            bytes_accessed=12 * 2**20,
            transcendentals=0,
        ),
        name="row_maxima",
    )(place, w, ql, kv, rs)


def gathered_weights(wn, wr, wk):
    x = lax.axis_index("x")
    parts = pack_weights(x.reshape(1).astype(jnp.int32), wn, wr, wk)
    moved = [parts[0], ring(parts[1], "x", 1), ring(parts[2], "x", 2), ring(parts[3], "x", -1)]
    return lax.all_gather(jnp.stack(moved), ("z", "c"), axis=1, tiled=True)


def gathered_latents(q_latent, kv_latent, k_rope, segment_ids):
    own, halo = pack_latents(q_latent, kv_latent, k_rope, segment_ids)
    own = lax.ppermute(own, SEQ, OWN_ROUTE)
    halo = lax.ppermute(halo, SEQ, HALO_ROUTE)
    first = jnp.concatenate([own[:128, :512], halo[:128, :128]], axis=1)
    rest = [
        own[128:, :512], halo[128:, :128],
        own[:128, 512:], halo[:128, 128:], own[128:, 512:], halo[128:, 128:],
    ]
    rest = jnp.concatenate(rest, axis=1)
    by_y = [first, ring(first, "y", 1), ring(first, "y", 2), ring(first, "y", -1)]
    by_x = [rest, ring(rest, "x", 1), ring(rest, "x", 2), ring(rest, "x", -1)]
    by_y = jnp.stack(by_y)
    far = jnp.stack([r[:, :640] for r in by_x])

    def both_ways(value, axis):
        up, down = ring(value, axis, 1), ring(value, axis, -1)
        two = [ring(up[:2], axis, 1), ring(down[2:], axis, -1)]
        return [list(value), list(up), list(two[0]) + list(two[1]), list(down)]

    a = both_ways(by_y, "x")
    b = both_ways(far, "y")
    ql, kv_own, kv_halo = [], [], []
    for d in range(4):
        ra = jnp.concatenate
        ql.append(ra([a[d][e][:, :384] for e in range(4)], axis=1))
        ql.append(ra([b[e][d][:, :384] for e in range(4)], axis=1))
        kv_own.append(ra([a[d][e][:, 384:512] for e in range(4)], axis=1))
        kv_own.append(ra([b[e][d][:, 384:512] for e in range(4)], axis=1))
        kv_halo.append(ra([a[d][e][:, 512:] for e in range(4)], axis=1))
        kv_halo.append(ra([b[e][d][:, 512:] for e in range(4)], axis=1))
    ql = jnp.concatenate(ql, axis=0)
    kv = jnp.concatenate(kv_own + kv_halo, axis=0)
    rs = [r[:, at : at + 128] for r in by_x for at in (640, 896)]
    rs += [r[:, at : at + 128] for r in by_x for at in (768, 1024)]
    return ql, kv, jnp.concatenate(rs, axis=0)


def local(q_latent, kv_latent, k_rope, segment_ids, w_q_nope, w_q_rope, w_kv_nope, threshold):
    x, z, c, y = (lax.axis_index(a).astype(jnp.int32) for a in ("x", "z", "c", "y"))
    w = gathered_weights(w_q_nope, w_q_rope, w_kv_nope)
    ql, kv, rs = gathered_latents(q_latent, kv_latent, k_rope, segment_ids)
    xo = lax.rem(z, 2) + 2 * c
    place = jnp.stack([lax.rem(x - xo + 4, 4), lax.rem(x - y + 4, 4)])
    rm, hm = main(place, w, ql, kv, rs)

    everything = lax.all_to_all(hm, SEQ, 0, 0, tiled=True)
    head_max = jnp.max(everything.reshape(4, 16, 128), axis=1)[:, :HEADS].reshape(32)
    back = [lax.ppermute(rm[d], SEQ, HOME_ROUTES[d]) for d in range(4)]
    first = lax.rem(lax.rem(z, 2) * 2 + c + x, 4)
    twice = jnp.concatenate(back + back[:3], axis=0)
    row_max = lax.dynamic_slice_in_dim(twice, 8 * lax.rem(4 - first, 4), 32, axis=0).T

    clip = threshold[0] / jnp.maximum(head_max, threshold[0])
    root = jnp.sqrt(clip)
    new_q_nope = (w_q_nope.astype(jnp.float32) * jnp.repeat(root, D_NOPE)[None, :]).astype(
        jnp.bfloat16
    )
    new_q_rope = (w_q_rope.astype(jnp.float32) * jnp.repeat(clip, D_ROPE)[None, :]).astype(
        jnp.bfloat16
    )
    new_kv_nope = (w_kv_nope.astype(jnp.float32) * jnp.repeat(root, D_NOPE)[None, :]).astype(
        jnp.bfloat16
    )
    return (new_q_nope, new_q_rope, new_kv_nope, head_max, row_max)


def solution(mesh):
    fine = Mesh(mesh.devices.reshape(4, 8, 2, 4), ("x", "z", "c", "y"))
    in_specs = (
        P(SEQ, "y"),
        P(SEQ, "y"),
        P(SEQ, None),
        P(SEQ),
        P(SEQ, "y"),
        P(SEQ, "y"),
        P(SEQ, "y"),
        P(),
    )
    out_specs = (P(SEQ, "y"), P(SEQ, "y"), P(SEQ, "y"), P("y"), P(SEQ, "y"))
    return jax.shard_map(local, mesh=fine, in_specs=in_specs, out_specs=out_specs, check_vma=False)
```

time: 284 us -> 143 us (0.50)
  waiting for transfers between devices: 180 us -> 32.6 us
  matrix products: 40.4 us -> 0 us
  starting transfers between devices: 35.5 us -> 62.4 us
  Pallas kernels: 0 us -> 19 us
    all_gather x3 -> x1, waiting for transfers between devices: 169 us -> 0.02 us  [gathered_weights(): return lax.all_gather(jnp.stack(moved), ('z', 'c'), axis=1, tiled=True)]
    dot_general x14 -> x0, matrix products: 40.4 us -> none  [the longest x4 12.1 us: expand(): jnp.dot(latent, full_kv, preferred_element_type=jnp.float32) * k_scale]
    ppermute x9 -> x23, starting transfers between devices: 29.4 us -> 54.4 us  [the longest x17 27 us: ring(): lax.ppermute(value, axis, [(i, (i + distance) % n) for i in range(n)])]
    ppermute x9 -> x23, waiting for transfers between devices: 1.7 us -> 24.1 us  [the longest x17 24.1 us: ring(): lax.ppermute(value, axis, [(i, (i + distance) % n) for i in range(n)])]
    pallas_call x0 -> x3, Pallas kernels: none -> 19 us  [the longest x1 15.2 us: main(): pl.pallas_call(main_kernel, out_shape=[jax.ShapeDtypeStruct((4, HEADS, BL...]
    unnamed x23 -> x44, local copies, waits for them, and re-layouts: 0.6 us -> 4.89 us
    concatenate x2, other arithmetic: 3.27 us -> 0.05 us  [the longest x1 0.03 us: gathered_latents(): ql = jnp.concatenate(ql, axis=0)]
  transfers between devices with their start and end apart: 13 -> 25, of which waited for: 6 -> 12; matrix products, arithmetic and copies ran while one was open for 16% -> 3% of each run, Pallas kernels for 0% -> 1%
where the time goes in v1:
time: 143 us; the launch traced here: 142 us
  starting transfers between devices  62.4 us (44%)
  waiting for transfers between devices  32.6 us (23%)
  Pallas kernels  19 us (13%)
  between operations  15.8 us (11%)
  local copies, waits for them, and re-layouts  7.71 us (5%)
  other arithmetic  4.63 us (3%)
    ppermute x17, starting transfers between devices, ring(): lax.ppermute(value, axis, [(i, (i + distance) % n) for i in range(n)])  27 us
    ppermute x17, waiting for transfers between devices, ring(): lax.ppermute(value, axis, [(i, (i + distance) % n) for i in range(n)])  24.1 us
    ppermute x4, starting transfers between devices, local(): back = [lax.ppermute(rm[d], SEQ, HOME_ROUTES[d]) for d in range(4)]  16.4 us
    pallas_call x1, Pallas kernels, main(): pl.pallas_call(main_kernel, out_shape=[jax.ShapeDtypeStruct((4, HEADS, BL...  15.2 us
    all_to_all x1, waiting for transfers between devices, local(): everything = lax.all_to_all(hm, SEQ, 0, 0, tiled=True)  8.47 us
    all_to_all x1, starting transfers between devices, local(): everything = lax.all_to_all(hm, SEQ, 0, 0, tiled=True)  7.91 us
    ppermute x1, starting transfers between devices, gathered_latents(): halo = lax.ppermute(halo, SEQ, HALO_ROUTE)  6.53 us
    unnamed x44, local copies, waits for them, and re-layouts  4.89 us
  transfers between devices with their start and end apart: 25, of which 12 were waited for; matrix products, arithmetic and copies ran while one was open for 3% of the time, Pallas kernels for 1%

profile of v1, /device:TPU:1, one launch (start us, length us, event | category | flops | bytes accessed | tf_op | source)
XLA Modules:
  0.0 142.1 jit_solution(5177797367977951978)
XLA Ops:
  7.2 1.5 %copy.14.rope_ref = bf16[256,64]{1,0:T(8,128)(2,1)} copy(bf16[256,64]{0,1:T(8,128)(2,1)} %param.10) | data formatting | bytes 65536 | tf_op args[2]
  8.7 2.0 %pack_latents.1 = (bf16[256,640]{1,0:T(8,128)(2,1)}, bf16[256,256]{1,0:T(8,128)(2,1)}) custom-call(bf16[256,384]{1,0:T(8,128)(2,1)} %q_ref.1, bf16[256,128]{1,0:T(8,128)(2,1)} %kv_ref.1, bf16[256,64]{1,0:T(8,128)(2,1)} %copy.14.rope_ref, s32[1,256]{1,0:T(1,128)} %bitcast.99), custom_call_target="tpu_custom_call" | custom-call | tf_op jit(solution)/shard_map/pack_latents/pallas_call | solution.py:98
  10.7 4.5 %collective-permute-start.3 = (bf16[256,640]{1,0:T(8,128)(2,1)}, bf16[256,640]{1,0:T(8,128)(2,1)S(1)}, u32[]{:S(2)}, u32[]{:S(2)}) collective-permute-start(bf16[256,640]{1,0:T(8,128)(2,1)} %get-tuple-element.17), channel_id=1, source_target_pairs={{0,0},{4,64},{8,128},{12,192},{16,16},{20,80},{24,144},{28,208},{3... | collective-permute-start | bytes 983048 | tf_op jit(solution)/shard_map/ppermute | solution.py:260
  15.2 6.5 %collective-permute-start.4 = (bf16[256,256]{1,0:T(8,128)(2,1)}, bf16[256,256]{1,0:T(8,128)(2,1)S(1)}, u32[]{:S(2)}, u32[]{:S(2)}) collective-permute-start(bf16[256,256]{1,0:T(8,128)(2,1)} %get-tuple-element.18), channel_id=1, source_target_pairs={{4,80},{8,144},{12,208},{20,96},{24,160},{28,224},{36,112},{40,176... | collective-permute-start | bytes 393224 | tf_op jit(solution)/shard_map/ppermute | solution.py:261
  21.8 1.7 %pack_weights.1 = (bf16[8,5632]{1,0:T(8,128)(2,1)}, bf16[8,5632]{1,0:T(8,128)(2,1)}, bf16[8,5632]{1,0:T(8,128)(2,1)}, bf16[8,5632]{1,0:T(8,128)(2,1)}) custom-call(s32[1]{0:T(128)} %bitcast.3.x_ref, bf16[24,4096]{1,0:T(8,128)(2,1)} %wn_ref.1, bf16[24,2048]{1,0:T(8,128)(2,1)} %wr_ref.1, bf16[8,4096]{1,0:T(8,128)(2,1)} %wk_ref.1), custom_call_target="tpu_custom_call" | custom-call | tf_op jit(solution)/shard_map/pack_weights/pallas_call | solution.py:67
  24.1 3.4 %collective-permute-start.1 = (bf16[8,5632]{1,0:T(8,128)(2,1)}, bf16[8,5632]{1,0:T(8,128)(2,1)S(1)}, u32[]{:S(2)}, u32[]{:S(2)}) collective-permute-start(bf16[8,5632]{1,0:T(8,128)(2,1)} %get-tuple-element.15), channel_id=1, source_target_pairs={{0,128},{64,192},{128,0},{192,64},{1,129},{65,193},{129,1},{193,65... | collective-permute-start | bytes 270344 | tf_op jit(solution)/shard_map/ppermute | solution.py:50
  28.5 2.1 %collective-permute-done.1 = bf16[8,5632]{1,0:T(8,128)(2,1)S(1)} collective-permute-done((bf16[8,5632]{1,0:T(8,128)(2,1)}, bf16[8,5632]{1,0:T(8,128)(2,1)S(1)}, u32[]{:S(2)}, u32[]{:S(2)}) %collective-permute-start.1) | collective-permute-done | bytes 90144 | tf_op jit(solution)/shard_map/ppermute | solution.py:50
  31.2 1.7 %pad_maximum_fusion.2 = bf16[4,8,5632]{2,1,0:T(8,128)(2,1)} fusion(bf16[1,8,5632]{2,1,0:T(8,128)(2,1)S(1)} %bitcast.97, bf16[1,8,5632]{2,1,0:T(8,128)(2,1)S(1)} %bitcast.96, bf16[1,8,5632]{2,1,0:T(8,128)(2,1)S(1)} %bitcast.95, bf16[1,8,5632]{2,1,0:T(8,128)(2,1)} %bitcast.94), kind=kLoop, calls=%fused_computation.11 | loop fusion | flops 540672 | bytes 720896 | tf_op jit(solution)/shard_map/stack | solution.py:255
  33.1 6.8 %collective-permute-start.9 = (bf16[128,1152]{1,0:T(8,128)(2,1)S(1)}, bf16[128,1152]{1,0:T(8,128)(2,1)S(1)}, u32[]{:S(2)}, u32[]{:S(2)}) collective-permute-start(bf16[128,1152]{1,0:T(8,128)(2,1)S(1)} %constant_dynamic-update-slice_fusion), channel_id=1, source_target_pairs={{0,128},{64,192},{128,0},{192,64},{1,129},{65,193},{129,1},{193,65... | collective-permute-start | bytes 884744 | tf_op jit(solution)/shard_map/ppermute | solution.py:50
  39.9 1.4 collective-permute-start.5
  41.3 2.6 %collective-permute-start.6 = (bf16[128,640]{1,0:T(8,128)(2,1)S(1)}, bf16[128,640]{1,0:T(8,128)(2,1)S(1)}, u32[]{:S(2)}, u32[]{:S(2)}) collective-permute-start(bf16[128,640]{1,0:T(8,128)(2,1)S(1)} %get-tuple-element.119), channel_id=1, source_target_pairs={{0,2},{1,3},{2,0},{3,1},{4,6},{5,7},{6,4},{7,5},{8,10},{9,11},{10,... | collective-permute-start | bytes 491528 | tf_op jit(solution)/shard_map/ppermute | solution.py:50
  43.9 1.1 collective-permute-start.7
  45.5 2.9 %collective-permute-done.6 = bf16[128,640]{1,0:T(8,128)(2,1)S(1)} collective-permute-done((bf16[128,640]{1,0:T(8,128)(2,1)S(1)}, bf16[128,640]{1,0:T(8,128)(2,1)S(1)}, u32[]{:S(2)}, u32[]{:S(2)}) %collective-permute-start.6) | collective-permute-done | bytes 163872 | tf_op jit(solution)/shard_map/ppermute | solution.py:50
  48.6 2.7 %collective-permute-start.16 = (bf16[4,128,640]{2,1,0:T(8,128)(2,1)S(1)}, bf16[4,128,640]{2,1,0:T(8,128)(2,1)S(1)}, u32[]{:S(2)}, u32[]{:S(2)}) collective-permute-start(bf16[4,128,640]{2,1,0:T(8,128)(2,1)S(1)} %pad_maximum_fusion.1), channel_id=1, source_target_pairs={{0,192},{64,0},{128,64},{192,128},{1,193},{65,1},{129,65},{193,129... | collective-permute-start | bytes 1966088 | tf_op jit(solution)/shard_map/ppermute | solution.py:50
  51.4 3.2 %collective-permute-done.10 = bf16[128,1152]{1,0:T(8,128)(2,1)S(1)} collective-permute-done((bf16[128,1152]{1,0:T(8,128)(2,1)S(1)}, bf16[128,1152]{1,0:T(8,128)(2,1)S(1)}, u32[]{:S(2)}, u32[]{:S(2)}) %collective-permute-start.10) | collective-permute-done | bytes 294944 | tf_op jit(solution)/shard_map/ppermute | solution.py:50
  55.1 2.5 %collective-permute-start.13 = (bf16[4,128,640]{2,1,0:T(8,128)(2,1)S(1)}, bf16[4,128,640]{2,1,0:T(8,128)(2,1)S(1)}, u32[]{:S(2)}, u32[]{:S(2)}) collective-permute-start(bf16[4,128,640]{2,1,0:T(8,128)(2,1)S(1)} %pad_maximum_fusion), channel_id=1, source_target_pairs={{0,3},{1,0},{2,1},{3,2},{4,7},{5,4},{6,5},{7,6},{8,11},{9,8},{10,9... | collective-permute-start | bytes 1966088 | tf_op jit(solution)/shard_map/ppermute | solution.py:50
  57.8 7.1 %collective-permute-done.16 = bf16[4,128,640]{2,1,0:T(8,128)(2,1)S(1)} collective-permute-done((bf16[4,128,640]{2,1,0:T(8,128)(2,1)S(1)}, bf16[4,128,640]{2,1,0:T(8,128)(2,1)S(1)}, u32[]{:S(2)}, u32[]{:S(2)}) %collective-permute-start.16) | collective-permute-done | bytes 655392 | tf_op jit(solution)/shard_map/ppermute | solution.py:50
  64.9 2.0 %collective-permute-start.17 = (bf16[2,128,640]{2,1,0:T(8,128)(2,1)S(1)}, bf16[2,128,640]{2,1,0:T(8,128)(2,1)S(1)}, u32[]{:S(2)}, u32[]{:S(2)}) collective-permute-start(bf16[2,128,640]{2,1,0:T(8,128)(2,1)S(1)} %slice.562), channel_id=1, source_target_pairs={{0,192},{64,0},{128,64},{192,128},{1,193},{65,1},{129,65},{193,129... | collective-permute-start | bytes 983048 | tf_op jit(solution)/shard_map/ppermute | solution.py:50
  67.9 1.6 %collective-permute-start.12 = (bf16[2,128,640]{2,1,0:T(8,128)(2,1)S(1)}, bf16[2,128,640]{2,1,0:T(8,128)(2,1)S(1)}, u32[]{:S(2)}, u32[]{:S(2)}) collective-permute-start(bf16[2,128,640]{2,1,0:T(8,128)(2,1)S(1)} %slice.548), channel_id=1, source_target_pairs={{0,1},{1,2},{2,3},{3,0},{4,5},{5,6},{6,7},{7,4},{8,9},{9,10},{10,1... | collective-permute-start | bytes 983048 | tf_op jit(solution)/shard_map/ppermute | solution.py:50
  69.5 1.7 %collective-permute-start.18 = (bf16[2,128,640]{2,1,0:T(8,128)(2,1)S(1)}, bf16[2,128,640]{2,1,0:T(8,128)(2,1)S(1)}, u32[]{:S(2)}, u32[]{:S(2)}) collective-permute-start(bf16[2,128,640]{2,1,0:T(8,128)(2,1)S(1)} %slice.567), channel_id=1, source_target_pairs={{0,3},{1,0},{2,1},{3,2},{4,7},{5,4},{6,5},{7,6},{8,11},{9,8},{10,9... | collective-permute-start | bytes 983048 | tf_op jit(solution)/shard_map/ppermute | solution.py:50
  71.3 1.1 collective-permute-done.17
  72.4 3.9 %collective-permute-done.15 = bf16[2,128,640]{2,1,0:T(8,128)(2,1)S(1)} collective-permute-done((bf16[2,128,640]{2,1,0:T(8,128)(2,1)S(1)}, bf16[2,128,640]{2,1,0:T(8,128)(2,1)S(1)}, u32[]{:S(2)}, u32[]{:S(2)}) %collective-permute-start.15) | collective-permute-done | bytes 327712 | tf_op jit(solution)/shard_map/ppermute | solution.py:50
  76.5 1.3 collective-permute-done.12
  80.7 1.6 %copy-done.1 = bf16[2048,512]{1,0:T(8,128)(2,1)S(1)} copy-done((bf16[2048,512]{1,0:T(8,128)(2,1)S(1)}, bf16[2048,512]{1,0:T(8,128)(2,1)}, u32[]{:S(2)}) %copy-start.1) | copy-done | bytes 2097176
  82.3 1.0 copy-done.3
  83.3 15.2 %row_maxima.1 = (f32[4,8,256]{2,1,0:T(8,128)S(1)}, f32[64,128]{1,0:T(8,128)}) custom-call(s32[2]{0:T(128)S(1)} %pad_add_fusion.place_ref, bf16[4,128,5632]{2,1,0:T(8,128)(2,1)} %all-gather.2.cloned.1.call-done.w_ref, bf16[1024,1536]{1,0:T(8,128)(2,1)S(1)} %maximum_dynamic-update-slice_fusion.ql_ref, bf16[2048,512]{1,0:T(8,128)(2,1)S(1)} %copy-done.1, ...), custom_call_target="tpu_custom_call" | custom-call | flops 11274289152 | bytes 12582912 | tf_op jit(solution)/shard_map/row_maxima/pallas_call | solution.py:216
  98.6 6.3 %collective-permute-start.19 = (f32[8,256]{1,0:T(8,128)S(1)}, f32[8,256]{1,0:T(8,128)S(1)}, u32[]{:S(2)}, u32[]{:S(2)}) collective-permute-start(f32[8,256]{1,0:T(8,128)S(1)} %get-tuple-element.126), channel_id=1, source_target_pairs={{0,0},{64,4},{128,8},{192,12},{16,16},{80,20},{144,24},{208,28},{3... | collective-permute-start | bytes 24584 | tf_op jit(solution)/shard_map/ppermute | solution.py:306
  105.6 1.9 %collective-permute-start.20 = (f32[8,256]{1,0:T(8,128)S(1)}, f32[8,256]{1,0:T(8,128)S(1)}, u32[]{:S(2)}, u32[]{:S(2)}) collective-permute-start(f32[8,256]{1,0:T(8,128)S(1)} %get-tuple-element.125), channel_id=1, source_target_pairs={{64,0},{128,4},{192,8},{0,12},{80,16},{144,20},{208,24},{16,28},{9... | collective-permute-start | bytes 24584 | tf_op jit(solution)/shard_map/ppermute | solution.py:306
  107.5 5.1 %collective-permute-start.21 = (f32[8,256]{1,0:T(8,128)S(1)}, f32[8,256]{1,0:T(8,128)S(1)}, u32[]{:S(2)}, u32[]{:S(2)}) collective-permute-start(f32[8,256]{1,0:T(8,128)S(1)} %get-tuple-element.124), channel_id=1, source_target_pairs={{128,0},{192,4},{0,8},{64,12},{144,16},{208,20},{16,24},{80,28},{1... | collective-permute-start | bytes 24584 | tf_op jit(solution)/shard_map/ppermute | solution.py:306
  112.7 3.1 %collective-permute-start.22 = (f32[8,256]{1,0:T(8,128)S(1)}, f32[8,256]{1,0:T(8,128)S(1)}, u32[]{:S(2)}, u32[]{:S(2)}) collective-permute-start(f32[8,256]{1,0:T(8,128)S(1)} %get-tuple-element.123), channel_id=1, source_target_pairs={{192,0},{0,4},{64,8},{128,12},{208,16},{16,20},{80,24},{144,28},{2... | collective-permute-start | bytes 24584 | tf_op jit(solution)/shard_map/ppermute | solution.py:306
  115.7 7.9 %all-to-all-start = ((f32[64,1,128]{2,1,0:T(1,128)}), f32[64,1,128]{2,1,0:T(1,128)S(1)}, u32[]{:S(2)}, u32[]{:S(2)}) async-start(f32[64,1,128]{2,1,0:T(1,128)} %bitcast.42), calls=%async_computation | async-start | bytes 65536 | tf_op jit(solution)/shard_map/all_to_all | solution.py:304
  124.4 8.5 %all-to-all-done = f32[64,1,128]{2,1,0:T(1,128)S(1)} async-done(((f32[64,1,128]{2,1,0:T(1,128)}), f32[64,1,128]{2,1,0:T(1,128)S(1)}, u32[]{:S(2)}, u32[]{:S(2)}) %all-to-all-start) | async-done | bytes 32800 | tf_op jit(solution)/shard_map/all_to_all | solution.py:304
  (178 shorter events, 10.4 us)
Async XLA Ops:
  7.2 73.5 %all-gather.2.cloned.1.call-start = ((), (), s32[]{:S(2)}) async-start(), calls=%async_computation.1 | async-start | bytes 6127616 | tf_op jit(solution)/shard_map/all_gather | solution.py:255
  10.7 22.2 %collective-permute-start.3 = (bf16[256,640]{1,0:T(8,128)(2,1)}, bf16[256,640]{1,0:T(8,128)(2,1)S(1)}, u32[]{:S(2)}, u32[]{:S(2)}) collective-permute-start(bf16[256,640]{1,0:T(8,128)(2,1)} %get-tuple-element.17), channel_id=1, source_target_pairs={{0,0},{4,64},{8,128},{12,192},{16,16},{20,80},{24,144},{28,208},{3... | collective-permute-start | bytes 983048 | tf_op jit(solution)/shard_map/ppermute | solution.py:260
  15.2 17.7 %collective-permute-start.4 = (bf16[256,256]{1,0:T(8,128)(2,1)}, bf16[256,256]{1,0:T(8,128)(2,1)S(1)}, u32[]{:S(2)}, u32[]{:S(2)}) collective-permute-start(bf16[256,256]{1,0:T(8,128)(2,1)} %get-tuple-element.18), channel_id=1, source_target_pairs={{4,80},{8,144},{12,208},{20,96},{24,160},{28,224},{36,112},{40,176... | collective-permute-start | bytes 393224 | tf_op jit(solution)/shard_map/ppermute | solution.py:261
  23.5 5.1 %collective-permute-start = (bf16[8,5632]{1,0:T(8,128)(2,1)}, bf16[8,5632]{1,0:T(8,128)(2,1)S(1)}, u32[]{:S(2)}, u32[]{:S(2)}) collective-permute-start(bf16[8,5632]{1,0:T(8,128)(2,1)} %get-tuple-element.14), channel_id=1, source_target_pairs={{0,64},{64,128},{128,192},{192,0},{1,65},{65,129},{129,193},{193,1... | collective-permute-start | bytes 270344 | tf_op jit(solution)/shard_map/ppermute | solution.py:50
  24.1 6.5 %collective-permute-start.1 = (bf16[8,5632]{1,0:T(8,128)(2,1)}, bf16[8,5632]{1,0:T(8,128)(2,1)S(1)}, u32[]{:S(2)}, u32[]{:S(2)}) collective-permute-start(bf16[8,5632]{1,0:T(8,128)(2,1)} %get-tuple-element.15), channel_id=1, source_target_pairs={{0,128},{64,192},{128,0},{192,64},{1,129},{65,193},{129,1},{193,65... | collective-permute-start | bytes 270344 | tf_op jit(solution)/shard_map/ppermute | solution.py:50
  27.6 3.6 %collective-permute-start.2 = (bf16[8,5632]{1,0:T(8,128)(2,1)}, bf16[8,5632]{1,0:T(8,128)(2,1)S(1)}, u32[]{:S(2)}, u32[]{:S(2)}) collective-permute-start(bf16[8,5632]{1,0:T(8,128)(2,1)} %get-tuple-element.16), channel_id=1, source_target_pairs={{0,192},{64,0},{128,64},{192,128},{1,193},{65,1},{129,65},{193,129... | collective-permute-start | bytes 270344 | tf_op jit(solution)/shard_map/ppermute | solution.py:50
  33.0 21.6 %collective-permute-start.8 = (bf16[128,1152]{1,0:T(8,128)(2,1)S(1)}, bf16[128,1152]{1,0:T(8,128)(2,1)S(1)}, u32[]{:S(2)}, u32[]{:S(2)}) collective-permute-start(bf16[128,1152]{1,0:T(8,128)(2,1)S(1)} %constant_dynamic-update-slice_fusion), channel_id=1, source_target_pairs={{0,64},{64,128},{128,192},{192,0},{1,65},{65,129},{129,193},{193,1... | collective-permute-start | bytes 884744 | tf_op jit(solution)/shard_map/ppermute | solution.py:50
  33.1 21.5 %collective-permute-start.9 = (bf16[128,1152]{1,0:T(8,128)(2,1)S(1)}, bf16[128,1152]{1,0:T(8,128)(2,1)S(1)}, u32[]{:S(2)}, u32[]{:S(2)}) collective-permute-start(bf16[128,1152]{1,0:T(8,128)(2,1)S(1)} %constant_dynamic-update-slice_fusion), channel_id=1, source_target_pairs={{0,128},{64,192},{128,0},{192,64},{1,129},{65,193},{129,1},{193,65... | collective-permute-start | bytes 884744 | tf_op jit(solution)/shard_map/ppermute | solution.py:50
  39.9 5.5 %collective-permute-start.5 = (bf16[128,640]{1,0:T(8,128)(2,1)S(1)}, bf16[128,640]{1,0:T(8,128)(2,1)S(1)}, u32[]{:S(2)}, u32[]{:S(2)}) collective-permute-start(bf16[128,640]{1,0:T(8,128)(2,1)S(1)} %get-tuple-element.119), channel_id=1, source_target_pairs={{0,1},{1,2},{2,3},{3,0},{4,5},{5,6},{6,7},{7,4},{8,9},{9,10},{10,1... | collective-permute-start | bytes 491528 | tf_op jit(solution)/shard_map/ppermute | solution.py:50
  41.3 7.1 %collective-permute-start.6 = (bf16[128,640]{1,0:T(8,128)(2,1)S(1)}, bf16[128,640]{1,0:T(8,128)(2,1)S(1)}, u32[]{:S(2)}, u32[]{:S(2)}) collective-permute-start(bf16[128,640]{1,0:T(8,128)(2,1)S(1)} %get-tuple-element.119), channel_id=1, source_target_pairs={{0,2},{1,3},{2,0},{3,1},{4,6},{5,7},{6,4},{7,5},{8,10},{9,11},{10,... | collective-permute-start | bytes 491528 | tf_op jit(solution)/shard_map/ppermute | solution.py:50
  43.9 4.5 %collective-permute-start.7 = (bf16[128,640]{1,0:T(8,128)(2,1)S(1)}, bf16[128,640]{1,0:T(8,128)(2,1)S(1)}, u32[]{:S(2)}, u32[]{:S(2)}) collective-permute-start(bf16[128,640]{1,0:T(8,128)(2,1)S(1)} %get-tuple-element.119), channel_id=1, source_target_pairs={{0,3},{1,0},{2,1},{3,2},{4,7},{5,4},{6,5},{7,6},{8,11},{9,8},{10,9... | collective-permute-start | bytes 491528 | tf_op jit(solution)/shard_map/ppermute | solution.py:50
  45.5 9.1 %collective-permute-start.10 = (bf16[128,1152]{1,0:T(8,128)(2,1)S(1)}, bf16[128,1152]{1,0:T(8,128)(2,1)S(1)}, u32[]{:S(2)}, u32[]{:S(2)}) collective-permute-start(bf16[128,1152]{1,0:T(8,128)(2,1)S(1)} %constant_dynamic-update-slice_fusion), channel_id=1, source_target_pairs={{0,192},{64,0},{128,64},{192,128},{1,193},{65,1},{129,65},{193,129... | collective-permute-start | bytes 884744 | tf_op jit(solution)/shard_map/ppermute | solution.py:50
  48.5 18.5 %collective-permute-start.14 = (bf16[4,128,640]{2,1,0:T(8,128)(2,1)S(1)}, bf16[4,128,640]{2,1,0:T(8,128)(2,1)S(1)}, u32[]{:S(2)}, u32[]{:S(2)}) collective-permute-start(bf16[4,128,640]{2,1,0:T(8,128)(2,1)S(1)} %pad_maximum_fusion.1), channel_id=1, source_target_pairs={{0,64},{64,128},{128,192},{192,0},{1,65},{65,129},{129,193},{193,1... | collective-permute-start | bytes 1966088 | tf_op jit(solution)/shard_map/ppermute | solution.py:50
  48.6 16.3 %collective-permute-start.16 = (bf16[4,128,640]{2,1,0:T(8,128)(2,1)S(1)}, bf16[4,128,640]{2,1,0:T(8,128)(2,1)S(1)}, u32[]{:S(2)}, u32[]{:S(2)}) collective-permute-start(bf16[4,128,640]{2,1,0:T(8,128)(2,1)S(1)} %pad_maximum_fusion.1), channel_id=1, source_target_pairs={{0,192},{64,0},{128,64},{192,128},{1,193},{65,1},{129,65},{193,129... | collective-permute-start | bytes 1966088 | tf_op jit(solution)/shard_map/ppermute | solution.py:50
  54.6 3.2 %copy-start.7 = (bf16[128,1152]{1,0:T(8,128)(2,1)}, bf16[128,1152]{1,0:T(8,128)(2,1)S(1)}, u32[]{:S(2)}) copy-start(bf16[128,1152]{1,0:T(8,128)(2,1)S(1)} %collective-permute-done.10) | copy-start | bytes 884740
  54.6 10.3 %copy-start.5 = (bf16[128,1152]{1,0:T(8,128)(2,1)}, bf16[128,1152]{1,0:T(8,128)(2,1)S(1)}, u32[]{:S(2)}) copy-start(bf16[128,1152]{1,0:T(8,128)(2,1)S(1)} %collective-permute-done.9) | copy-start | bytes 884740
  54.6 10.3 %copy-start.6 = (bf16[128,1152]{1,0:T(8,128)(2,1)}, bf16[128,1152]{1,0:T(8,128)(2,1)S(1)}, u32[]{:S(2)}) copy-start(bf16[128,1152]{1,0:T(8,128)(2,1)S(1)} %collective-permute-done.8) | copy-start | bytes 884740
  54.8 12.8 %collective-permute-start.11 = (bf16[4,128,640]{2,1,0:T(8,128)(2,1)S(1)}, bf16[4,128,640]{2,1,0:T(8,128)(2,1)S(1)}, u32[]{:S(2)}, u32[]{:S(2)}) collective-permute-start(bf16[4,128,640]{2,1,0:T(8,128)(2,1)S(1)} %pad_maximum_fusion), channel_id=1, source_target_pairs={{0,1},{1,2},{2,3},{3,0},{4,5},{5,6},{6,7},{7,4},{8,9},{9,10},{10,1... | collective-permute-start | bytes 1966088 | tf_op jit(solution)/shard_map/ppermute | solution.py:50
  55.1 12.5 %collective-permute-start.13 = (bf16[4,128,640]{2,1,0:T(8,128)(2,1)S(1)}, bf16[4,128,640]{2,1,0:T(8,128)(2,1)S(1)}, u32[]{:S(2)}, u32[]{:S(2)}) collective-permute-start(bf16[4,128,640]{2,1,0:T(8,128)(2,1)S(1)} %pad_maximum_fusion), channel_id=1, source_target_pairs={{0,3},{1,0},{2,1},{3,2},{4,7},{5,4},{6,5},{7,6},{8,11},{9,8},{10,9... | collective-permute-start | bytes 1966088 | tf_op jit(solution)/shard_map/ppermute | solution.py:50
  57.8 9.5 %copy-start.2 = (bf16[2048,128]{1,0:T(8,128)(2,1)}, bf16[2048,128]{1,0:T(8,128)(2,1)S(1)}, u32[]{:S(2)}) copy-start(bf16[2048,128]{1,0:T(8,128)(2,1)S(1)} %get-tuple-element.55.rs_ref) | copy-start | bytes 1572868
  64.9 7.5 %collective-permute-start.17 = (bf16[2,128,640]{2,1,0:T(8,128)(2,1)S(1)}, bf16[2,128,640]{2,1,0:T(8,128)(2,1)S(1)}, u32[]{:S(2)}, u32[]{:S(2)}) collective-permute-start(bf16[2,128,640]{2,1,0:T(8,128)(2,1)S(1)} %slice.562), channel_id=1, source_target_pairs={{0,192},{64,0},{128,64},{192,128},{1,193},{65,1},{129,65},{193,129... | collective-permute-start | bytes 983048 | tf_op jit(solution)/shard_map/ppermute | solution.py:50
  67.0 9.3 %collective-permute-start.15 = (bf16[2,128,640]{2,1,0:T(8,128)(2,1)S(1)}, bf16[2,128,640]{2,1,0:T(8,128)(2,1)S(1)}, u32[]{:S(2)}, u32[]{:S(2)}) collective-permute-start(bf16[2,128,640]{2,1,0:T(8,128)(2,1)S(1)} %slice.559), channel_id=1, source_target_pairs={{0,64},{64,128},{128,192},{192,0},{1,65},{65,129},{129,193},{193,1... | collective-permute-start | bytes 983048 | tf_op jit(solution)/shard_map/ppermute | solution.py:50
  67.9 9.8 %collective-permute-start.12 = (bf16[2,128,640]{2,1,0:T(8,128)(2,1)S(1)}, bf16[2,128,640]{2,1,0:T(8,128)(2,1)S(1)}, u32[]{:S(2)}, u32[]{:S(2)}) collective-permute-start(bf16[2,128,640]{2,1,0:T(8,128)(2,1)S(1)} %slice.548), channel_id=1, source_target_pairs={{0,1},{1,2},{2,3},{3,0},{4,5},{5,6},{6,7},{7,4},{8,9},{9,10},{10,1... | collective-permute-start | bytes 983048 | tf_op jit(solution)/shard_map/ppermute | solution.py:50
  69.5 9.1 %collective-permute-start.18 = (bf16[2,128,640]{2,1,0:T(8,128)(2,1)S(1)}, bf16[2,128,640]{2,1,0:T(8,128)(2,1)S(1)}, u32[]{:S(2)}, u32[]{:S(2)}) collective-permute-start(bf16[2,128,640]{2,1,0:T(8,128)(2,1)S(1)} %slice.567), channel_id=1, source_target_pairs={{0,3},{1,0},{2,1},{3,2},{4,7},{5,4},{6,5},{7,6},{8,11},{9,8},{10,9... | collective-permute-start | bytes 983048 | tf_op jit(solution)/shard_map/ppermute | solution.py:50
  83.3 49.7 %copy-start.4 = (bf16[24,4096]{1,0:T(8,128)(2,1)S(1)}, bf16[24,4096]{1,0:T(8,128)(2,1)}, u32[]{:S(2)}) copy-start(bf16[24,4096]{1,0:T(8,128)(2,1)} %wn_ref.1) | copy-start | bytes 589828
  83.3 50.5 %copy-start.9 = (bf16[8,4096]{1,0:T(8,128)(2,1)S(1)}, bf16[8,4096]{1,0:T(8,128)(2,1)}, u32[]{:S(2)}) copy-start(bf16[8,4096]{1,0:T(8,128)(2,1)} %wk_ref.1) | copy-start | bytes 196612
  83.3 51.2 %copy-start.8 = (bf16[24,2048]{1,0:T(8,128)(2,1)S(1)}, bf16[24,2048]{1,0:T(8,128)(2,1)}, u32[]{:S(2)}) copy-start(bf16[24,2048]{1,0:T(8,128)(2,1)} %wr_ref.1) | copy-start | bytes 294916
  98.6 25.1 %collective-permute-start.19 = (f32[8,256]{1,0:T(8,128)S(1)}, f32[8,256]{1,0:T(8,128)S(1)}, u32[]{:S(2)}, u32[]{:S(2)}) collective-permute-start(f32[8,256]{1,0:T(8,128)S(1)} %get-tuple-element.126), channel_id=1, source_target_pairs={{0,0},{64,4},{128,8},{192,12},{16,16},{80,20},{144,24},{208,28},{3... | collective-permute-start | bytes 24584 | tf_op jit(solution)/shard_map/ppermute | solution.py:306
  105.6 18.1 %collective-permute-start.20 = (f32[8,256]{1,0:T(8,128)S(1)}, f32[8,256]{1,0:T(8,128)S(1)}, u32[]{:S(2)}, u32[]{:S(2)}) collective-permute-start(f32[8,256]{1,0:T(8,128)S(1)} %get-tuple-element.125), channel_id=1, source_target_pairs={{64,0},{128,4},{192,8},{0,12},{80,16},{144,20},{208,24},{16,28},{9... | collective-permute-start | bytes 24584 | tf_op jit(solution)/shard_map/ppermute | solution.py:306
  107.5 16.2 %collective-permute-start.21 = (f32[8,256]{1,0:T(8,128)S(1)}, f32[8,256]{1,0:T(8,128)S(1)}, u32[]{:S(2)}, u32[]{:S(2)}) collective-permute-start(f32[8,256]{1,0:T(8,128)S(1)} %get-tuple-element.124), channel_id=1, source_target_pairs={{128,0},{192,4},{0,8},{64,12},{144,16},{208,20},{16,24},{80,28},{1... | collective-permute-start | bytes 24584 | tf_op jit(solution)/shard_map/ppermute | solution.py:306
  112.7 11.1 %collective-permute-start.22 = (f32[8,256]{1,0:T(8,128)S(1)}, f32[8,256]{1,0:T(8,128)S(1)}, u32[]{:S(2)}, u32[]{:S(2)}) collective-permute-start(f32[8,256]{1,0:T(8,128)S(1)} %get-tuple-element.123), channel_id=1, source_target_pairs={{192,0},{0,4},{64,8},{128,12},{208,16},{16,20},{80,24},{144,28},{2... | collective-permute-start | bytes 24584 | tf_op jit(solution)/shard_map/ppermute | solution.py:306
  115.7 17.1 %all-to-all-start = ((f32[64,1,128]{2,1,0:T(1,128)}), f32[64,1,128]{2,1,0:T(1,128)S(1)}, u32[]{:S(2)}, u32[]{:S(2)}) async-start(f32[64,1,128]{2,1,0:T(1,128)} %bitcast.42), calls=%async_computation | async-start | bytes 65536 | tf_op jit(solution)/shard_map/all_to_all | solution.py:304
  (7 other events, 9.5 us)
Sparse Core Ops, SparseCore 0:
  33.0 47.3 all-gather.1

commit v2 on v1

v2 whole, which is shorter than its diff:
```python
import math

import jax
import jax.numpy as jnp
from jax import lax
from jax.experimental import pallas as pl
from jax.experimental.pallas import tpu as pltpu
from jax.sharding import Mesh
from jax.sharding import PartitionSpec as P

D_NOPE = 128
D_ROPE = 64
QLORA = 1536
KVLORA = 512
BLK = 256
HEADS = 8
NX = 4
Q_COLS = HEADS * (D_NOPE + D_ROPE)
W_COLS = 3 * Q_COLS + HEADS * D_NOPE
NEG = -1e30
SEQ = ("x", "zh", "zl", "c")


def place_of(block, shift=0):
    group, i = divmod(block, 4)
    group = (group + shift) % 16
    xo, zh = divmod(group, 4)
    x, z, c = (i + xo) % 4, zh * 2 + (xo & 1), xo >> 1
    return (x * 8 + z) * 2 + c


OWN_ROUTE = [(b, place_of(b)) for b in range(64)]
HALO_ROUTE = [(b, place_of(b, 1)) for b in range(60) if b % 4]
Z_ROUTE = [(z * 2 + c, (z + (-1 if c else 1)) % 8 * 2 + c) for z in range(8) for c in range(2)]


def ring(value, axis, distance):
    n = lax.axis_size(axis)
    return lax.ppermute(value, axis, [(i, (i + distance) % n) for i in range(n)])


def pack_weights_kernel(x_ref, wn_ref, wr_ref, wk_ref, *out_refs):
    for d in range(4):
        to = lax.rem(x_ref[0] + d, 4)
        out = out_refs[d]
        for t in range(3):
            rows = pl.ds(t * 8, 8)
            at = t * Q_COLS
            out[:, at : at + 1024] = wn_ref[rows, pl.ds(pl.multiple_of(to * 1024, 1024), 1024)]
            out[:, at + 1024 : at + 1536] = wr_ref[rows, pl.ds(pl.multiple_of(to * 512, 512), 512)]
        out[:, 3 * Q_COLS :] = wk_ref[:, pl.ds(pl.multiple_of(to * 1024, 1024), 1024)]


def pack_weights(x, wn, wr, wk):
    vmem = pl.BlockSpec(memory_space=pltpu.VMEM)
    return pl.pallas_call(
        pack_weights_kernel,
        out_shape=[jax.ShapeDtypeStruct((8, W_COLS), jnp.bfloat16)] * 4,
        in_specs=[pl.BlockSpec(memory_space=pltpu.SMEM), vmem, vmem, vmem],
        out_specs=[vmem] * 4,
        name="pack_weights",
    )(x, wn, wr, wk)


def pack_latents_kernel(q_ref, kv_ref, rope_ref, seg_ref, own_ref, halo_ref):
    old = lax.broadcasted_iota(jnp.int32, (384, 384), 0)
    new = lax.broadcasted_iota(jnp.int32, (384, 384), 1)
    t, rest = new // 128, new % 128
    pick = old == (rest // 8) * 24 + t * 8 + rest % 8
    chosen = jnp.where(pick, 1.0, 0.0).astype(jnp.bfloat16)
    own_ref[:, :384] = jnp.dot(q_ref[...], chosen, preferred_element_type=jnp.float32).astype(
        jnp.bfloat16
    )
    kv = kv_ref[...]
    own_ref[:, 384:512] = kv
    halo_ref[:, :128] = kv
    seg = jnp.broadcast_to((seg_ref[...] + 1).astype(jnp.float32), (128, BLK))
    column = jnp.transpose(seg).astype(jnp.bfloat16)
    rope = jnp.transpose(rope_ref[...].astype(jnp.float32)).astype(jnp.bfloat16)
    for ref, at in ((own_ref, 512), (halo_ref, 128)):
        ref[:, at : at + 128] = column
        ref[:, at : at + 64] = rope


def pack_latents(q, kv, rope, seg):
    vmem = pl.BlockSpec(memory_space=pltpu.VMEM)
    return pl.pallas_call(
        pack_latents_kernel,
        out_shape=[
            jax.ShapeDtypeStruct((BLK, 640), jnp.bfloat16),
            jax.ShapeDtypeStruct((BLK, 256), jnp.bfloat16),
        ],
        in_specs=[vmem] * 4,
        out_specs=[vmem] * 2,
        name="pack_latents",
    )(q, kv, rope.T, seg.reshape(1, BLK))


def join_kernel(c_ref, mine_ref, theirs_ref, out_ref):
    for core in range(2):

        @pl.when(c_ref[0] == core)
        def _():
            out_ref[:, core * 8 : core * 8 + 8, :] = mine_ref[...]
            out_ref[:, 8 - core * 8 : 16 - core * 8, :] = theirs_ref[...]


def join(c, mine, theirs):
    vmem = pl.BlockSpec(memory_space=pltpu.VMEM)
    return pl.pallas_call(
        join_kernel,
        out_shape=jax.ShapeDtypeStruct((4, 16, W_COLS), jnp.bfloat16),
        in_specs=[pl.BlockSpec(memory_space=pltpu.SMEM), vmem, vmem],
        out_specs=vmem,
        name="join_cores",
    )(c.reshape(1), mine, theirs)


N_W, N_L, N_R = 9, 5, 4


def main_kernel(place_ref, *refs):
    w_refs, refs = refs[:N_W], refs[N_W:]
    a_refs, b_refs, r_refs = refs[:N_L], refs[N_L : 2 * N_L], refs[2 * N_L : 2 * N_L + N_R]
    ex_ref, w, lat, rs, kn, kr, qn, qr, bias, sems = refs[2 * N_L + N_R :]
    i_own, delta, xo, z, c = (place_ref[n] for n in range(5))
    count = [0]

    def fetch(src, dst):
        copy = pltpu.make_async_copy(src, dst, sems.at[count[0]])
        count[0] += 1
        copy.start()
        return copy

    sign = 2 * c - 1
    early = [fetch(r_refs[d], rs.at[d]) for d in range(4)]
    late = []
    for n in range(N_W):
        step = (n + 1) // 2
        towards = sign if n % 2 else -sign
        rows = pl.ds(pl.multiple_of(lax.rem(z + towards * step + 8, 8) * 16, 16), 16)
        if step < 4:
            late.append(fetch(w_refs[n], w.at[:, rows, :]))
        else:
            half = pl.ds(2 * c, 2) if n % 2 else pl.ds(2 - 2 * c, 2)
            late.append(fetch(w_refs[n], w.at[half, rows, :]))
    low, high = pl.ds(0, 128), pl.ds(128, 128)
    for n, d in enumerate((0, 1, 3)):
        late.append(fetch(a_refs[n], lat.at[d, :, low, :]))
        late.append(fetch(b_refs[n], lat.at[:, d, high, :]))
    for n in range(2):
        late.append(fetch(a_refs[3 + n], lat.at[2, pl.ds(2 * n, 2), low, :]))
        late.append(fetch(b_refs[3 + n], lat.at[pl.ds(2 * n, 2), 2, high, :]))

    for copy in early:
        copy.wait()
    lane = lax.broadcasted_iota(jnp.int32, (128, 128), 1)
    seg_rows = []
    for d in range(4):
        seg_row = []
        for n in range(4):
            at = d + 4 * (n % 2)
            rows = pl.ds((n // 2) * 128, 128)
            part = rs[d, :, n * 128 : n * 128 + 128].astype(jnp.float32)
            kr[0, at, rows, :] = jnp.where(lane < 64, part, 0.0).astype(jnp.bfloat16)
            turned = pltpu.roll(part, 64, 1)
            kr[1, at, rows, :] = jnp.where(lane >= 64, turned, 0.0).astype(jnp.bfloat16)
            kr[2, at, rows, :] = turned.astype(jnp.bfloat16)
            if n % 2 == 0:
                seg_row.append(jnp.transpose(part)[64:65, :])
        seg_rows.append(jnp.concatenate(seg_row, axis=1))
    k_iota = lax.broadcasted_iota(jnp.int32, (BLK, BLK), 0)
    q_iota = lax.broadcasted_iota(jnp.int32, (BLK, BLK), 1)
    which = []
    for d in range(4):
        i_q = lax.rem(i_own - d + 4, 4)
        for f in range(4):
            i_k = lax.rem(i_own - f + 4, 4)
            at = jnp.where(i_k > i_q, f + 4, f)
            which.append(at)
            seg_k = kr[2, at, :, 0:1].astype(jnp.float32)
            allowed = seg_k == seg_rows[d]
            if d == f:
                allowed = allowed & (k_iota <= q_iota)
            bias[d, f] = jnp.where(allowed, 0.0, NEG)

    for copy in late:
        copy.wait()
    slots = [lax.rem(delta + e, 4) for e in range(4)]
    k_scale = 1.0 / math.sqrt(KVLORA)
    wk = jnp.concatenate([w[slot, :, 3 * Q_COLS :] for slot in slots], axis=0)
    for b in range(8):
        at = 384 + 128 * (b // 4)
        kv = jnp.concatenate([lat[b % 4, e, :, at : at + 128] for e in range(4)], axis=1)
        kn[b] = (jnp.dot(kv, wk, preferred_element_type=jnp.float32) * k_scale).astype(jnp.bfloat16)
    q_scale = 1.0 / math.sqrt(QLORA)
    for out, at, columns in ((qn, 0, 512), (qn, 512, 512), (qr, 1024, 512)):
        wq = [
            w[slot, :, t * Q_COLS + at : t * Q_COLS + at + columns]
            for slot in slots
            for t in range(3)
        ]
        wq = jnp.concatenate(wq, axis=0)
        for d in range(4):
            ql = jnp.concatenate([lat[d, e, :, :384] for e in range(4)], axis=1)
            to = at % 1024
            out[d, :, to : to + columns] = (
                jnp.dot(ql, wq, preferred_element_type=jnp.float32) * q_scale
            ).astype(jnp.bfloat16)

    score_scale = 1.0 / math.sqrt(D_NOPE + D_ROPE)
    for h in range(HEADS):
        best_h = None
        for d in range(4):
            pair = (h // 2) * 128
            query = jnp.concatenate(
                [qn[d, :, h * 128 : h * 128 + 128], qr[d, :, pair : pair + 128]], axis=1
            )
            best = None
            for f in range(4):
                at = which[d * 4 + f]
                keys = jnp.concatenate([kn[at, :, h * 128 : h * 128 + 128], kr[h % 2, at]], axis=1)
                s = lax.dot_general(
                    keys, query, (((1,), (1,)), ((), ())), preferred_element_type=jnp.float32
                )
                s = jnp.max((s + bias[d, f]).reshape(BLK // 8, 8, BLK), axis=0)
                best = s if best is None else jnp.maximum(best, s)
            row = jnp.max(best, axis=0, keepdims=True) * score_scale
            home = 4 * xo + lax.rem(i_own - d + 4, 4)
            ex_ref[home, h : h + 1, 0:BLK] = row
            best_h = row if best_h is None else jnp.maximum(best_h, row)
        top = jnp.max(best_h, axis=1, keepdims=True)
        ex_ref[0, h : h + 1, BLK:] = jnp.broadcast_to(top, (1, 128))
    tops = ex_ref[0, :, BLK:]
    for n in range(1, 16):
        ex_ref[n, :, BLK:] = tops


def main(place, w, a, b, r):
    vmem = pl.BlockSpec(memory_space=pltpu.VMEM)
    bf16, f32 = jnp.bfloat16, jnp.float32
    return pl.pallas_call(
        main_kernel,
        out_shape=jax.ShapeDtypeStruct((16, HEADS, BLK + 128), f32),
        in_specs=[pl.BlockSpec(memory_space=pltpu.SMEM)]
        + [pl.BlockSpec(memory_space=pl.ANY)] * (N_W + 2 * N_L + N_R),
        out_specs=vmem,
        scratch_shapes=[
            pltpu.VMEM((4, 128, W_COLS), bf16),
            pltpu.VMEM((4, 4, BLK, 640), bf16),
            pltpu.VMEM((4, 128, 512), bf16),
            pltpu.VMEM((8, BLK, 1024), bf16),
            pltpu.VMEM((3, 8, BLK, 128), bf16),
            pltpu.VMEM((4, BLK, 1024), bf16),
            pltpu.VMEM((4, BLK, 512), bf16),
            pltpu.VMEM((4, 4, BLK, BLK), f32),
            pltpu.SemaphoreType.DMA((N_W + 2 * N_L + N_R,)),
        ],
        compiler_params=pltpu.CompilerParams(vmem_limit_bytes=48 * 2**20),
        cost_estimate=pl.CostEstimate(
            flops=2 * 2048 * 512 * 1024 + 2 * 1024 * 1536 * 1536 + 2 * 128 * 256**3,
            bytes_accessed=12 * 2**20,
            transcendentals=0,
        ),
        name="row_maxima",
    )(place, *w, *a, *b, *r)


def exchanged_weights(x, c, wn, wr, wk):
    parts = pack_weights(x.reshape(1), wn, wr, wk)
    moved = [parts[0], ring(parts[1], "x", 1), ring(parts[2], "x", 2), ring(parts[3], "x", -1)]
    mine = jnp.stack(moved)
    return join(c, mine, ring(mine, "c", 1))


def gathered_weights(c, own):
    pieces = [own]
    held = own
    for step in range(1, 5):
        if step == 4:
            held = lax.dynamic_slice_in_dim(held, 2 * c, 2, axis=0)
        held = lax.ppermute(held, ("zh", "zl", "c"), Z_ROUTE)
        pieces += [held, ring(held, "c", 1)]
    return pieces


def gathered_latents(q_latent, kv_latent, k_rope, segment_ids):
    own, halo = pack_latents(q_latent, kv_latent, k_rope, segment_ids)
    own = lax.ppermute(own, SEQ, OWN_ROUTE)
    halo = lax.ppermute(halo, SEQ, HALO_ROUTE)
    first = jnp.concatenate([own[:128, :512], halo[:128, :128]], axis=1)
    second = jnp.concatenate([own[128:, :512], halo[128:, :128]], axis=1)
    ropes = [own[:128, 512:], halo[:128, 128:], own[128:, 512:], halo[128:, 128:]]
    ropes = jnp.concatenate(ropes, axis=1)

    def around(value, axis):
        return [value, ring(value, axis, 1), ring(value, axis, 2), ring(value, axis, -1)]

    def both_ways(value, axis):
        up, down = ring(value, axis, 1), ring(value, axis, -1)
        return [value, up, down, ring(up[:2], axis, 1), ring(down[2:], axis, -1)]

    by_y, by_x, r = around(first, "y"), around(second, "x"), around(ropes, "x")
    return both_ways(jnp.stack(by_y), "x"), both_ways(jnp.stack(by_x), "y"), r


def local(q_latent, kv_latent, k_rope, segment_ids, w_q_nope, w_q_rope, w_kv_nope, threshold):
    x, zh, zl, c, y = (lax.axis_index(a).astype(jnp.int32) for a in ("x", "zh", "zl", "c", "y"))
    own = exchanged_weights(x, c, w_q_nope, w_q_rope, w_kv_nope)
    w = gathered_weights(c, own)
    a, b, r = gathered_latents(q_latent, kv_latent, k_rope, segment_ids)
    xo = zl + 2 * c
    place = jnp.stack([lax.rem(x - xo + 4, 4), lax.rem(x - y + 4, 4), xo, 2 * zh + zl, c])
    out = main(place, w, a, b, r)

    got = lax.all_to_all(out, ("x", "zl", "c"), 0, 0, tiled=True)
    got = got.reshape(4, 4, HEADS, BLK + 128)
    top = jnp.max(got[..., BLK:], axis=1).reshape(4 * HEADS, 128)
    top = jnp.maximum(
        jnp.maximum(top, ring(top, "zh", 2)), jnp.maximum(ring(top, "zh", 1), ring(top, "zh", -1))
    )
    head_max = top[:, 0]
    sent_from = 2 * lax.rem(x, 2) + x // 2
    rows = lax.dynamic_slice_in_dim(got[..., :BLK], sent_from, 1, axis=1)
    row_max = rows.reshape(4 * HEADS, BLK).T

    clip = threshold[0] / jnp.maximum(head_max, threshold[0])
    root = jnp.sqrt(clip)
    new_q_nope = (w_q_nope.astype(jnp.float32) * jnp.repeat(root, D_NOPE)[None, :]).astype(
        jnp.bfloat16
    )
    new_q_rope = (w_q_rope.astype(jnp.float32) * jnp.repeat(clip, D_ROPE)[None, :]).astype(
        jnp.bfloat16
    )
    new_kv_nope = (w_kv_nope.astype(jnp.float32) * jnp.repeat(root, D_NOPE)[None, :]).astype(
        jnp.bfloat16
    )
    return (new_q_nope, new_q_rope, new_kv_nope, head_max, row_max)


def solution(mesh):
    fine = Mesh(mesh.devices.reshape(4, 4, 2, 2, 4), ("x", "zh", "zl", "c", "y"))
    in_specs = (
        P(SEQ, "y"),
        P(SEQ, "y"),
        P(SEQ, None),
        P(SEQ),
        P(SEQ, "y"),
        P(SEQ, "y"),
        P(SEQ, "y"),
        P(),
    )
    out_specs = (P(SEQ, "y"), P(SEQ, "y"), P(SEQ, "y"), P("y"), P(SEQ, "y"))
    return jax.shard_map(local, mesh=fine, in_specs=in_specs, out_specs=out_specs, check_vma=False)
```

time: 143 us -> 173 us (1.21)
  starting transfers between devices: 62.4 us -> 84.2 us
  waiting for transfers between devices: 32.6 us -> 50.3 us
  between operations: 15.8 us -> 1.52 us
  Pallas kernels: 19 us -> 22.5 us
    ppermute x17 -> x28, starting transfers between devices: 27 us -> 55.8 us  [ring(): lax.ppermute(value, axis, [(i, (i + distance) % n) for i in range(n)])]
    ppermute x17 -> x28, waiting for transfers between devices: 24.1 us -> 36.7 us  [ring(): lax.ppermute(value, axis, [(i, (i + distance) % n) for i in range(n)])]
    ppermute x1, starting transfers between devices: 6.53 us -> 2 us  [gathered_latents(): halo = lax.ppermute(halo, SEQ, HALO_ROUTE)]
    pallas_call x1 -> x2, Pallas kernels: 15.2 us -> 18.8 us  [the longest x1 16.8 us: main(): pl.pallas_call(main_kernel, out_shape=jax.ShapeDtypeStruct((16, HEADS, BL...]
    ppermute x1, waiting for transfers between devices: 0.01 us -> 3.43 us  [gathered_latents(): own = lax.ppermute(own, SEQ, OWN_ROUTE)]
    ppermute x4, waiting for transfers between devices: 0.01 us -> 2.62 us  [gathered_weights(): held = lax.ppermute(held, ('zh', 'zl', 'c'), Z_ROUTE)]
    ppermute x1, starting transfers between devices: 4.5 us -> 1.92 us  [gathered_latents(): own = lax.ppermute(own, SEQ, OWN_ROUTE)]
    all_to_all x1, waiting for transfers between devices: 8.47 us -> 6.03 us  [local(): got = lax.all_to_all(out, ('x', 'zl', 'c'), 0, 0, tiled=True)]
  transfers between devices with their start and end apart: 25 -> 35, of which waited for: 12 -> 15; matrix products, arithmetic and copies ran while one was open for 3% -> 2% of each run, Pallas kernels for 1% -> 1%
where the time goes in v2:
time: 173 us; the launch traced here: 171 us
  starting transfers between devices  84.2 us (49%)
  waiting for transfers between devices  50.3 us (29%)
  Pallas kernels  22.5 us (13%)
  local copies, waits for them, and re-layouts  9.32 us (5%)
  other arithmetic  3.36 us (2%)
    ppermute x28, starting transfers between devices, ring(): lax.ppermute(value, axis, [(i, (i + distance) % n) for i in range(n)])  55.8 us
    ppermute x28, waiting for transfers between devices, ring(): lax.ppermute(value, axis, [(i, (i + distance) % n) for i in range(n)])  36.7 us
    ppermute x4, starting transfers between devices, gathered_weights(): held = lax.ppermute(held, ('zh', 'zl', 'c'), Z_ROUTE)  17.4 us
    pallas_call x1, Pallas kernels, main(): pl.pallas_call(main_kernel, out_shape=jax.ShapeDtypeStruct((16, HEADS, BL...  16.8 us
    all_to_all x1, starting transfers between devices, local(): got = lax.all_to_all(out, ('x', 'zl', 'c'), 0, 0, tiled=True)  7.03 us
    unnamed x30, local copies, waits for them, and re-layouts  6.48 us
    all_to_all x1, waiting for transfers between devices, local(): got = lax.all_to_all(out, ('x', 'zl', 'c'), 0, 0, tiled=True)  6.03 us
  transfers between devices with their start and end apart: 35, of which 15 were waited for; matrix products, arithmetic and copies ran while one was open for 2% of the time, Pallas kernels for 1%

profile of v2, /device:TPU:1, one launch (start us, length us, event | category | flops | bytes accessed | tf_op | source)
XLA Modules:
  0.0 171.1 jit_solution(8469065845044612050)
XLA Ops:
  2.4 2.0 %collective-permute-start = (bf16[8,5632]{1,0:T(8,128)(2,1)}, bf16[8,5632]{1,0:T(8,128)(2,1)S(1)}, u32[]{:S(2)}, u32[]{:S(2)}) collective-permute-start(bf16[8,5632]{1,0:T(8,128)(2,1)} %get-tuple-element.12), channel_id=1, source_target_pairs={{0,64},{64,128},{128,192},{192,0},{1,65},{65,129},{129,193},{193,1... | collective-permute-start | bytes 270344 | tf_op jit(solution)/shard_map/ppermute | solution.py:39
  4.4 2.5 %collective-permute-start.1 = (bf16[8,5632]{1,0:T(8,128)(2,1)}, bf16[8,5632]{1,0:T(8,128)(2,1)S(1)}, u32[]{:S(2)}, u32[]{:S(2)}) collective-permute-start(bf16[8,5632]{1,0:T(8,128)(2,1)} %get-tuple-element.13), channel_id=1, source_target_pairs={{0,128},{64,192},{128,0},{192,64},{1,129},{65,193},{129,1},{193,65... | collective-permute-start | bytes 270344 | tf_op jit(solution)/shard_map/ppermute | solution.py:39
  8.0 2.7 %collective-permute-done.1 = bf16[8,5632]{1,0:T(8,128)(2,1)S(1)} collective-permute-done((bf16[8,5632]{1,0:T(8,128)(2,1)}, bf16[8,5632]{1,0:T(8,128)(2,1)S(1)}, u32[]{:S(2)}, u32[]{:S(2)}) %collective-permute-start.1) | collective-permute-done | bytes 90144 | tf_op jit(solution)/shard_map/ppermute | solution.py:39
  11.7 2.7 %collective-permute-start.3 = (bf16[4,8,5632]{2,1,0:T(8,128)(2,1)S(1)}, bf16[4,8,5632]{2,1,0:T(8,128)(2,1)S(1)}, u32[]{:S(2)}, u32[]{:S(2)}) collective-permute-start(bf16[4,8,5632]{2,1,0:T(8,128)(2,1)S(1)} %pad_maximum_fusion.2.mine_ref), channel_id=1, source_target_pairs={{0,4},{4,0},{1,5},{5,1},{2,6},{6,2},{3,7},{7,3},{8,12},{12,8},{9,1... | collective-permute-start | bytes 1081352 | tf_op jit(solution)/shard_map/ppermute | solution.py:39
  16.5 2.0 %join_cores.1.refs_0_ = bf16[4,16,5632]{2,1,0:T(8,128)(2,1)} custom-call(s32[1]{0:T(128)} %bitcast.5.c_ref, bf16[4,8,5632]{2,1,0:T(8,128)(2,1)} %copy-done.8, bf16[4,8,5632]{2,1,0:T(8,128)(2,1)} %copy-done.11), custom_call_target="tpu_custom_call" | custom-call | tf_op jit(solution)/shard_map/join_cores/pallas_call | solution.py:110
  18.5 5.0 %collective-permute-start.4 = (bf16[4,16,5632]{2,1,0:T(8,128)(2,1)}, bf16[4,16,5632]{2,1,0:T(8,128)(2,1)}, u32[]{:S(2)}, u32[]{:S(2)}) collective-permute-start(bf16[4,16,5632]{2,1,0:T(8,128)(2,1)} %join_cores.1.refs_0_), channel_id=1, source_target_pairs={{0,8},{4,60},{8,16},{12,4},{16,24},{20,12},{24,32},{28,20},{32,40}... | collective-permute-start | bytes 2162696 | tf_op jit(solution)/shard_map/ppermute | solution.py:282
  23.5 2.0 %pack_latents.1 = (bf16[256,640]{1,0:T(8,128)(2,1)}, bf16[256,256]{1,0:T(8,128)(2,1)}) custom-call(bf16[256,384]{1,0:T(8,128)(2,1)} %q_ref.1, bf16[256,128]{1,0:T(8,128)(2,1)} %kv_ref.1, bf16[64,256]{1,0:T(8,128)(2,1)} %bitcast.48, s32[1,256]{1,0:T(1,128)} %bitcast.49), custom_call_target="tpu_custom_call" | custom-call | tf_op jit(solution)/shard_map/pack_latents/pallas_call | solution.py:87
  25.5 2.0 %collective-permute-start.13 = (bf16[256,256]{1,0:T(8,128)(2,1)}, bf16[256,256]{1,0:T(8,128)(2,1)S(1)}, u32[]{:S(2)}, u32[]{:S(2)}) collective-permute-start(bf16[256,256]{1,0:T(8,128)(2,1)} %get-tuple-element.16), channel_id=1, source_target_pairs={{4,80},{8,144},{12,208},{20,96},{24,160},{28,224},{36,112},{40,176... | collective-permute-start | bytes 393224 | tf_op jit(solution)/shard_map/ppermute | solution.py:290
  29.4 2.6 %collective-permute-done.4.refs_1_ = bf16[4,16,5632]{2,1,0:T(8,128)(2,1)} collective-permute-done((bf16[4,16,5632]{2,1,0:T(8,128)(2,1)}, bf16[4,16,5632]{2,1,0:T(8,128)(2,1)}, u32[]{:S(2)}, u32[]{:S(2)}) %collective-permute-start.4) | collective-permute-done | bytes 720928 | tf_op jit(solution)/shard_map/ppermute | solution.py:282
  32.1 3.3 %collective-permute-start.6 = (bf16[4,16,5632]{2,1,0:T(8,128)(2,1)}, bf16[4,16,5632]{2,1,0:T(8,128)(2,1)}, u32[]{:S(2)}, u32[]{:S(2)}) collective-permute-start(bf16[4,16,5632]{2,1,0:T(8,128)(2,1)} %collective-permute-done.4.refs_1_), channel_id=1, source_target_pairs={{0,8},{4,60},{8,16},{12,4},{16,24},{20,12},{24,32},{28,20},{32,40}... | collective-permute-start | bytes 2162696 | tf_op jit(solution)/shard_map/ppermute | solution.py:282
  36.9 3.4 %collective-permute-done.12 = bf16[256,640]{1,0:T(8,128)(2,1)S(1)} collective-permute-done((bf16[256,640]{1,0:T(8,128)(2,1)}, bf16[256,640]{1,0:T(8,128)(2,1)S(1)}, u32[]{:S(2)}, u32[]{:S(2)}) %collective-permute-start.12) | collective-permute-done | bytes 327712 | tf_op jit(solution)/shard_map/ppermute | solution.py:289
  40.4 3.0 %collective-permute-start.15 = (bf16[128,640]{1,0:T(8,128)(2,1)S(1)}, bf16[128,640]{1,0:T(8,128)(2,1)S(1)}, u32[]{:S(2)}, u32[]{:S(2)}) collective-permute-start(bf16[128,640]{1,0:T(8,128)(2,1)S(1)} %get-tuple-element.26), channel_id=1, source_target_pairs={{0,2},{1,3},{2,0},{3,1},{4,6},{5,7},{6,4},{7,5},{8,10},{9,11},{10,... | collective-permute-start | bytes 491528 | tf_op jit(solution)/shard_map/ppermute | solution.py:39
  43.8 2.3 %collective-permute-start.16 = (bf16[128,640]{1,0:T(8,128)(2,1)S(1)}, bf16[128,640]{1,0:T(8,128)(2,1)S(1)}, u32[]{:S(2)}, u32[]{:S(2)}) collective-permute-start(bf16[128,640]{1,0:T(8,128)(2,1)S(1)} %get-tuple-element.26), channel_id=1, source_target_pairs={{0,3},{1,0},{2,1},{3,2},{4,7},{5,4},{6,5},{7,6},{8,11},{9,8},{10,9... | collective-permute-start | bytes 491528 | tf_op jit(solution)/shard_map/ppermute | solution.py:39
  46.9 2.4 %collective-permute-done.14 = bf16[128,640]{1,0:T(8,128)(2,1)S(1)} collective-permute-done((bf16[128,640]{1,0:T(8,128)(2,1)S(1)}, bf16[128,640]{1,0:T(8,128)(2,1)S(1)}, u32[]{:S(2)}, u32[]{:S(2)}) %collective-permute-start.14) | collective-permute-done | bytes 163872 | tf_op jit(solution)/shard_map/ppermute | solution.py:39
  49.4 4.6 %collective-permute-start.18 = (bf16[4,128,640]{2,1,0:T(8,128)(2,1)S(1)}, bf16[4,128,640]{2,1,0:T(8,128)(2,1)S(1)}, u32[]{:S(2)}, u32[]{:S(2)}) collective-permute-start(bf16[4,128,640]{2,1,0:T(8,128)(2,1)S(1)} %pad_maximum_fusion.refs_9_), channel_id=1, source_target_pairs={{0,192},{64,0},{128,64},{192,128},{1,193},{65,1},{129,65},{193,129... | collective-permute-start | bytes 1966088 | tf_op jit(solution)/shard_map/ppermute | solution.py:39
  54.1 4.8 %collective-permute-start.8 = (bf16[4,16,5632]{2,1,0:T(8,128)(2,1)}, bf16[4,16,5632]{2,1,0:T(8,128)(2,1)}, u32[]{:S(2)}, u32[]{:S(2)}) collective-permute-start(bf16[4,16,5632]{2,1,0:T(8,128)(2,1)} %collective-permute-done.6.refs_3_), channel_id=1, source_target_pairs={{0,8},{4,60},{8,16},{12,4},{16,24},{20,12},{24,32},{28,20},{32,40}... | collective-permute-start | bytes 2162696 | tf_op jit(solution)/shard_map/ppermute | solution.py:282
  60.3 2.0 %collective-permute-start.21 = (bf16[128,640]{1,0:T(8,128)(2,1)S(1)}, bf16[128,640]{1,0:T(8,128)(2,1)S(1)}, u32[]{:S(2)}, u32[]{:S(2)}) collective-permute-start(bf16[128,640]{1,0:T(8,128)(2,1)S(1)} %get-tuple-element.24), channel_id=1, source_target_pairs={{0,64},{64,128},{128,192},{192,0},{1,65},{65,129},{129,193},{193,1... | collective-permute-start | bytes 491528 | tf_op jit(solution)/shard_map/ppermute | solution.py:39
  62.3 10.9 %collective-permute-done.22 = bf16[128,640]{1,0:T(8,128)(2,1)S(1)} collective-permute-done((bf16[128,640]{1,0:T(8,128)(2,1)S(1)}, bf16[128,640]{1,0:T(8,128)(2,1)S(1)}, u32[]{:S(2)}, u32[]{:S(2)}) %collective-permute-start.22) | collective-permute-done | bytes 163872 | tf_op jit(solution)/shard_map/ppermute | solution.py:39
  73.7 4.0 %collective-permute-done.21 = bf16[128,640]{1,0:T(8,128)(2,1)S(1)} collective-permute-done((bf16[128,640]{1,0:T(8,128)(2,1)S(1)}, bf16[128,640]{1,0:T(8,128)(2,1)S(1)}, u32[]{:S(2)}, u32[]{:S(2)}) %collective-permute-start.21) | collective-permute-done | bytes 163872 | tf_op jit(solution)/shard_map/ppermute | solution.py:39
  79.9 2.9 %collective-permute-start.25 = (bf16[4,128,640]{2,1,0:T(8,128)(2,1)S(1)}, bf16[4,128,640]{2,1,0:T(8,128)(2,1)S(1)}, u32[]{:S(2)}, u32[]{:S(2)}) collective-permute-start(bf16[4,128,640]{2,1,0:T(8,128)(2,1)S(1)} %pad_maximum_fusion.1.refs_14_), channel_id=1, source_target_pairs={{0,3},{1,0},{2,1},{3,2},{4,7},{5,4},{6,5},{7,6},{8,11},{9,8},{10,9... | collective-permute-start | bytes 1966088 | tf_op jit(solution)/shard_map/ppermute | solution.py:39
  83.1 3.1 %collective-permute-start.20 = (bf16[2,128,640]{2,1,0:T(8,128)(2,1)S(1)}, bf16[2,128,640]{2,1,0:T(8,128)(2,1)S(1)}, u32[]{:S(2)}, u32[]{:S(2)}) collective-permute-start(bf16[2,128,640]{2,1,0:T(8,128)(2,1)S(1)} %slice.63), channel_id=1, source_target_pairs={{0,192},{64,0},{128,64},{192,128},{1,193},{65,1},{129,65},{193,129... | collective-permute-start | bytes 983048 | tf_op jit(solution)/shard_map/ppermute | solution.py:39
  87.3 4.6 %collective-permute-start.5 = (bf16[4,16,5632]{2,1,0:T(8,128)(2,1)}, bf16[4,16,5632]{2,1,0:T(8,128)(2,1)}, u32[]{:S(2)}, u32[]{:S(2)}) collective-permute-start(bf16[4,16,5632]{2,1,0:T(8,128)(2,1)} %collective-permute-done.4.refs_1_), channel_id=1, source_target_pairs={{0,4},{4,0},{1,5},{5,1},{2,6},{6,2},{3,7},{7,3},{8,12},{12,8},{9,1... | collective-permute-start | bytes 2162696 | tf_op jit(solution)/shard_map/ppermute | solution.py:39
  92.5 4.3 %collective-permute-start.10 = (bf16[2,16,5632]{2,1,0:T(8,128)(2,1)S(1)}, bf16[2,16,5632]{2,1,0:T(8,128)(2,1)}, u32[]{:S(2)}, u32[]{:S(2)}) collective-permute-start(bf16[2,16,5632]{2,1,0:T(8,128)(2,1)S(1)} %constant_dynamic-slice_fusion), channel_id=1, source_target_pairs={{0,8},{4,60},{8,16},{12,4},{16,24},{20,12},{24,32},{28,20},{32,40}... | collective-permute-start | bytes 1081352 | tf_op jit(solution)/shard_map/ppermute | solution.py:282
  96.8 4.5 %collective-permute-start.7 = (bf16[4,16,5632]{2,1,0:T(8,128)(2,1)}, bf16[4,16,5632]{2,1,0:T(8,128)(2,1)}, u32[]{:S(2)}, u32[]{:S(2)}) collective-permute-start(bf16[4,16,5632]{2,1,0:T(8,128)(2,1)} %collective-permute-done.6.refs_3_), channel_id=1, source_target_pairs={{0,4},{4,0},{1,5},{5,1},{2,6},{6,2},{3,7},{7,3},{8,12},{12,8},{9,1... | collective-permute-start | bytes 2162696 | tf_op jit(solution)/shard_map/ppermute | solution.py:39
  102.9 5.1 %collective-permute-start.11 = (bf16[2,16,5632]{2,1,0:T(8,128)(2,1)}, bf16[2,16,5632]{2,1,0:T(8,128)(2,1)}, u32[]{:S(2)}, u32[]{:S(2)}) collective-permute-start(bf16[2,16,5632]{2,1,0:T(8,128)(2,1)} %collective-permute-done.10.refs_7_), channel_id=1, source_target_pairs={{0,4},{4,0},{1,5},{5,1},{2,6},{6,2},{3,7},{7,3},{8,12},{12,8},{9,1... | collective-permute-start | bytes 1081352 | tf_op jit(solution)/shard_map/ppermute | solution.py:39
  108.8 2.5 %collective-permute-done.27.refs_18_ = bf16[2,128,640]{2,1,0:T(8,128)(2,1)S(1)} collective-permute-done((bf16[2,128,640]{2,1,0:T(8,128)(2,1)S(1)}, bf16[2,128,640]{2,1,0:T(8,128)(2,1)S(1)}, u32[]{:S(2)}, u32[]{:S(2)}) %collective-permute-start.27) | collective-permute-done | bytes 327712 | tf_op jit(solution)/shard_map/ppermute | solution.py:39
  112.1 9.9 %collective-permute-done.26.refs_17_ = bf16[2,128,640]{2,1,0:T(8,128)(2,1)} collective-permute-done((bf16[2,128,640]{2,1,0:T(8,128)(2,1)}, bf16[2,128,640]{2,1,0:T(8,128)(2,1)}, u32[]{:S(2)}, u32[]{:S(2)}) %collective-permute-start.26) | collective-permute-done | bytes 327712 | tf_op jit(solution)/shard_map/ppermute | solution.py:39
  125.9 16.8 %row_maxima.1 = f32[16,8,384]{2,1,0:T(8,128)} custom-call(s32[5]{0:T(128)S(1)} %stack.68.place_ref, bf16[4,16,5632]{2,1,0:T(8,128)(2,1)} %join_cores.1.refs_0_, bf16[4,16,5632]{2,1,0:T(8,128)(2,1)} %collective-permute-done.4.refs_1_, bf16[4,16,5632]{2,1,0:T(8,128)(2,1)} %collective-permute-done.5.refs_2_, ...), custom_call_target="tpu_custom_call" | custom-call | flops 11274289152 | bytes 12582912 | tf_op jit(solution)/shard_map/row_maxima/pallas_call | solution.py:242
  142.6 7.0 %all-to-all-start = ((f32[16,8,384]{2,1,0:T(8,128)}), f32[16,8,384]{2,1,0:T(8,128)S(1)}, u32[]{:S(2)}, u32[]{:S(2)}) async-start(f32[16,8,384]{2,1,0:T(8,128)} %row_maxima.1), calls=%async_computation | async-start | bytes 393216 | tf_op jit(solution)/shard_map/all_to_all | solution.py:316
  150.3 6.0 %all-to-all-done = f32[16,8,384]{2,1,0:T(8,128)S(1)} async-done(((f32[16,8,384]{2,1,0:T(8,128)}), f32[16,8,384]{2,1,0:T(8,128)S(1)}, u32[]{:S(2)}, u32[]{:S(2)}) %all-to-all-start) | async-done | bytes 196640 | tf_op jit(solution)/shard_map/all_to_all | solution.py:316
  156.4 5.3 %collective-permute-start.33 = (f32[32,128]{1,0:T(8,128)S(1)}, f32[32,128]{1,0:T(8,128)S(1)}, u32[]{:S(2)}, u32[]{:S(2)}) collective-permute-start(f32[32,128]{1,0:T(8,128)S(1)} %bitcast.44), channel_id=1, source_target_pairs={{0,48},{16,0},{32,16},{48,32},{1,49},{17,1},{33,17},{49,33},{2,50}... | collective-permute-start | bytes 49160 | tf_op jit(solution)/shard_map/ppermute | solution.py:39
  161.7 4.6 %collective-permute-start.31 = (f32[32,128]{1,0:T(8,128)S(1)}, f32[32,128]{1,0:T(8,128)S(1)}, u32[]{:S(2)}, u32[]{:S(2)}) collective-permute-start(f32[32,128]{1,0:T(8,128)S(1)} %bitcast.46), channel_id=1, source_target_pairs={{0,32},{16,48},{32,0},{48,16},{1,33},{17,49},{33,1},{49,17},{2,34}... | collective-permute-start | bytes 49160 | tf_op jit(solution)/shard_map/ppermute | solution.py:39
  (98 shorter events, 28.9 us)
Async XLA Ops:
  2.4 5.6 %collective-permute-start = (bf16[8,5632]{1,0:T(8,128)(2,1)}, bf16[8,5632]{1,0:T(8,128)(2,1)S(1)}, u32[]{:S(2)}, u32[]{:S(2)}) collective-permute-start(bf16[8,5632]{1,0:T(8,128)(2,1)} %get-tuple-element.12), channel_id=1, source_target_pairs={{0,64},{64,128},{128,192},{192,0},{1,65},{65,129},{129,193},{193,1... | collective-permute-start | bytes 270344 | tf_op jit(solution)/shard_map/ppermute | solution.py:39
  4.4 6.3 %collective-permute-start.1 = (bf16[8,5632]{1,0:T(8,128)(2,1)}, bf16[8,5632]{1,0:T(8,128)(2,1)S(1)}, u32[]{:S(2)}, u32[]{:S(2)}) collective-permute-start(bf16[8,5632]{1,0:T(8,128)(2,1)} %get-tuple-element.13), channel_id=1, source_target_pairs={{0,128},{64,192},{128,0},{192,64},{1,129},{65,193},{129,1},{193,65... | collective-permute-start | bytes 270344 | tf_op jit(solution)/shard_map/ppermute | solution.py:39
  18.5 13.6 %collective-permute-start.4 = (bf16[4,16,5632]{2,1,0:T(8,128)(2,1)}, bf16[4,16,5632]{2,1,0:T(8,128)(2,1)}, u32[]{:S(2)}, u32[]{:S(2)}) collective-permute-start(bf16[4,16,5632]{2,1,0:T(8,128)(2,1)} %join_cores.1.refs_0_), channel_id=1, source_target_pairs={{0,8},{4,60},{8,16},{12,4},{16,24},{20,12},{24,32},{28,20},{32,40}... | collective-permute-start | bytes 2162696 | tf_op jit(solution)/shard_map/ppermute | solution.py:282
  25.5 11.3 %collective-permute-start.13 = (bf16[256,256]{1,0:T(8,128)(2,1)}, bf16[256,256]{1,0:T(8,128)(2,1)S(1)}, u32[]{:S(2)}, u32[]{:S(2)}) collective-permute-start(bf16[256,256]{1,0:T(8,128)(2,1)} %get-tuple-element.16), channel_id=1, source_target_pairs={{4,80},{8,144},{12,208},{20,96},{24,160},{28,224},{36,112},{40,176... | collective-permute-start | bytes 393224 | tf_op jit(solution)/shard_map/ppermute | solution.py:290
  27.5 12.8 %collective-permute-start.12 = (bf16[256,640]{1,0:T(8,128)(2,1)}, bf16[256,640]{1,0:T(8,128)(2,1)S(1)}, u32[]{:S(2)}, u32[]{:S(2)}) collective-permute-start(bf16[256,640]{1,0:T(8,128)(2,1)} %get-tuple-element.15), channel_id=1, source_target_pairs={{0,0},{4,64},{8,128},{12,192},{16,16},{20,80},{24,144},{28,208},{3... | collective-permute-start | bytes 983048 | tf_op jit(solution)/shard_map/ppermute | solution.py:289
  32.1 22.0 %collective-permute-start.6 = (bf16[4,16,5632]{2,1,0:T(8,128)(2,1)}, bf16[4,16,5632]{2,1,0:T(8,128)(2,1)}, u32[]{:S(2)}, u32[]{:S(2)}) collective-permute-start(bf16[4,16,5632]{2,1,0:T(8,128)(2,1)} %collective-permute-done.4.refs_1_), channel_id=1, source_target_pairs={{0,8},{4,60},{8,16},{12,4},{16,24},{20,12},{24,32},{28,20},{32,40}... | collective-permute-start | bytes 2162696 | tf_op jit(solution)/shard_map/ppermute | solution.py:282
  40.4 6.6 %collective-permute-start.15 = (bf16[128,640]{1,0:T(8,128)(2,1)S(1)}, bf16[128,640]{1,0:T(8,128)(2,1)S(1)}, u32[]{:S(2)}, u32[]{:S(2)}) collective-permute-start(bf16[128,640]{1,0:T(8,128)(2,1)S(1)} %get-tuple-element.26), channel_id=1, source_target_pairs={{0,2},{1,3},{2,0},{3,1},{4,6},{5,7},{6,4},{7,5},{8,10},{9,11},{10,... | collective-permute-start | bytes 491528 | tf_op jit(solution)/shard_map/ppermute | solution.py:39
  43.4 5.9 %collective-permute-start.14 = (bf16[128,640]{1,0:T(8,128)(2,1)S(1)}, bf16[128,640]{1,0:T(8,128)(2,1)S(1)}, u32[]{:S(2)}, u32[]{:S(2)}) collective-permute-start(bf16[128,640]{1,0:T(8,128)(2,1)S(1)} %get-tuple-element.26), channel_id=1, source_target_pairs={{0,1},{1,2},{2,3},{3,0},{4,5},{5,6},{6,7},{7,4},{8,9},{9,10},{10,1... | collective-permute-start | bytes 491528 | tf_op jit(solution)/shard_map/ppermute | solution.py:39
  43.8 5.5 %collective-permute-start.16 = (bf16[128,640]{1,0:T(8,128)(2,1)S(1)}, bf16[128,640]{1,0:T(8,128)(2,1)S(1)}, u32[]{:S(2)}, u32[]{:S(2)}) collective-permute-start(bf16[128,640]{1,0:T(8,128)(2,1)S(1)} %get-tuple-element.26), channel_id=1, source_target_pairs={{0,3},{1,0},{2,1},{3,2},{4,7},{5,4},{6,5},{7,6},{8,11},{9,8},{10,9... | collective-permute-start | bytes 491528 | tf_op jit(solution)/shard_map/ppermute | solution.py:39
  49.4 29.7 %collective-permute-start.18 = (bf16[4,128,640]{2,1,0:T(8,128)(2,1)S(1)}, bf16[4,128,640]{2,1,0:T(8,128)(2,1)S(1)}, u32[]{:S(2)}, u32[]{:S(2)}) collective-permute-start(bf16[4,128,640]{2,1,0:T(8,128)(2,1)S(1)} %pad_maximum_fusion.refs_9_), channel_id=1, source_target_pairs={{0,192},{64,0},{128,64},{192,128},{1,193},{65,1},{129,65},{193,129... | collective-permute-start | bytes 1966088 | tf_op jit(solution)/shard_map/ppermute | solution.py:39
  54.1 25.8 %collective-permute-start.17 = (bf16[4,128,640]{2,1,0:T(8,128)(2,1)S(1)}, bf16[4,128,640]{2,1,0:T(8,128)(2,1)S(1)}, u32[]{:S(2)}, u32[]{:S(2)}) collective-permute-start(bf16[4,128,640]{2,1,0:T(8,128)(2,1)S(1)} %pad_maximum_fusion.refs_9_), channel_id=1, source_target_pairs={{0,64},{64,128},{128,192},{192,0},{1,65},{65,129},{129,193},{193,1... | collective-permute-start | bytes 1966088 | tf_op jit(solution)/shard_map/ppermute | solution.py:39
  54.1 32.2 %collective-permute-start.8 = (bf16[4,16,5632]{2,1,0:T(8,128)(2,1)}, bf16[4,16,5632]{2,1,0:T(8,128)(2,1)}, u32[]{:S(2)}, u32[]{:S(2)}) collective-permute-start(bf16[4,16,5632]{2,1,0:T(8,128)(2,1)} %collective-permute-done.6.refs_3_), channel_id=1, source_target_pairs={{0,8},{4,60},{8,16},{12,4},{16,24},{20,12},{24,32},{28,20},{32,40}... | collective-permute-start | bytes 2162696 | tf_op jit(solution)/shard_map/ppermute | solution.py:282
  58.9 14.2 %collective-permute-start.22 = (bf16[128,640]{1,0:T(8,128)(2,1)S(1)}, bf16[128,640]{1,0:T(8,128)(2,1)S(1)}, u32[]{:S(2)}, u32[]{:S(2)}) collective-permute-start(bf16[128,640]{1,0:T(8,128)(2,1)S(1)} %get-tuple-element.24), channel_id=1, source_target_pairs={{0,128},{64,192},{128,0},{192,64},{1,129},{65,193},{129,1},{193,65... | collective-permute-start | bytes 491528 | tf_op jit(solution)/shard_map/ppermute | solution.py:39
  60.3 17.4 %collective-permute-start.21 = (bf16[128,640]{1,0:T(8,128)(2,1)S(1)}, bf16[128,640]{1,0:T(8,128)(2,1)S(1)}, u32[]{:S(2)}, u32[]{:S(2)}) collective-permute-start(bf16[128,640]{1,0:T(8,128)(2,1)S(1)} %get-tuple-element.24), channel_id=1, source_target_pairs={{0,64},{64,128},{128,192},{192,0},{1,65},{65,129},{129,193},{193,1... | collective-permute-start | bytes 491528 | tf_op jit(solution)/shard_map/ppermute | solution.py:39
  77.7 5.1 %collective-permute-start.30 = (bf16[128,512]{1,0:T(8,128)(2,1)S(1)}, bf16[128,512]{1,0:T(8,128)(2,1)S(1)}, u32[]{:S(2)}, u32[]{:S(2)}) collective-permute-start(bf16[128,512]{1,0:T(8,128)(2,1)S(1)} %pad_maximum_fusion.5.refs_19_), channel_id=1, source_target_pairs={{0,192},{64,0},{128,64},{192,128},{1,193},{65,1},{129,65},{193,129... | collective-permute-start | bytes 393224 | tf_op jit(solution)/shard_map/ppermute | solution.py:39
  77.7 5.4 %collective-permute-start.29 = (bf16[128,512]{1,0:T(8,128)(2,1)S(1)}, bf16[128,512]{1,0:T(8,128)(2,1)}, u32[]{:S(2)}, u32[]{:S(2)}) collective-permute-start(bf16[128,512]{1,0:T(8,128)(2,1)S(1)} %pad_maximum_fusion.5.refs_19_), channel_id=1, source_target_pairs={{0,128},{64,192},{128,0},{192,64},{1,129},{65,193},{129,1},{193,65... | collective-permute-start | bytes 393224 | tf_op jit(solution)/shard_map/ppermute | solution.py:39
  79.1 8.1 %collective-permute-start.28 = (bf16[128,512]{1,0:T(8,128)(2,1)S(1)}, bf16[128,512]{1,0:T(8,128)(2,1)S(1)}, u32[]{:S(2)}, u32[]{:S(2)}) collective-permute-start(bf16[128,512]{1,0:T(8,128)(2,1)S(1)} %pad_maximum_fusion.5.refs_19_), channel_id=1, source_target_pairs={{0,64},{64,128},{128,192},{192,0},{1,65},{65,129},{129,193},{193,1... | collective-permute-start | bytes 393224 | tf_op jit(solution)/shard_map/ppermute | solution.py:39
  79.9 12.6 %collective-permute-start.25 = (bf16[4,128,640]{2,1,0:T(8,128)(2,1)S(1)}, bf16[4,128,640]{2,1,0:T(8,128)(2,1)S(1)}, u32[]{:S(2)}, u32[]{:S(2)}) collective-permute-start(bf16[4,128,640]{2,1,0:T(8,128)(2,1)S(1)} %pad_maximum_fusion.1.refs_14_), channel_id=1, source_target_pairs={{0,3},{1,0},{2,1},{3,2},{4,7},{5,4},{6,5},{7,6},{8,11},{9,8},{10,9... | collective-permute-start | bytes 1966088 | tf_op jit(solution)/shard_map/ppermute | solution.py:39
  82.8 14.0 %collective-permute-start.24 = (bf16[4,128,640]{2,1,0:T(8,128)(2,1)S(1)}, bf16[4,128,640]{2,1,0:T(8,128)(2,1)S(1)}, u32[]{:S(2)}, u32[]{:S(2)}) collective-permute-start(bf16[4,128,640]{2,1,0:T(8,128)(2,1)S(1)} %pad_maximum_fusion.1.refs_14_), channel_id=1, source_target_pairs={{0,1},{1,2},{2,3},{3,0},{4,5},{5,6},{6,7},{7,4},{8,9},{9,10},{10,1... | collective-permute-start | bytes 1966088 | tf_op jit(solution)/shard_map/ppermute | solution.py:39
  83.1 18.1 %collective-permute-start.20 = (bf16[2,128,640]{2,1,0:T(8,128)(2,1)S(1)}, bf16[2,128,640]{2,1,0:T(8,128)(2,1)S(1)}, u32[]{:S(2)}, u32[]{:S(2)}) collective-permute-start(bf16[2,128,640]{2,1,0:T(8,128)(2,1)S(1)} %slice.63), channel_id=1, source_target_pairs={{0,192},{64,0},{128,64},{192,128},{1,193},{65,1},{129,65},{193,129... | collective-permute-start | bytes 983048 | tf_op jit(solution)/shard_map/ppermute | solution.py:39
  86.2 15.7 %collective-permute-start.19 = (bf16[2,128,640]{2,1,0:T(8,128)(2,1)S(1)}, bf16[2,128,640]{2,1,0:T(8,128)(2,1)S(1)}, u32[]{:S(2)}, u32[]{:S(2)}) collective-permute-start(bf16[2,128,640]{2,1,0:T(8,128)(2,1)S(1)} %slice.62), channel_id=1, source_target_pairs={{0,64},{64,128},{128,192},{192,0},{1,65},{65,129},{129,193},{193,1... | collective-permute-start | bytes 983048 | tf_op jit(solution)/shard_map/ppermute | solution.py:39
  87.3 34.8 %collective-permute-start.5 = (bf16[4,16,5632]{2,1,0:T(8,128)(2,1)}, bf16[4,16,5632]{2,1,0:T(8,128)(2,1)}, u32[]{:S(2)}, u32[]{:S(2)}) collective-permute-start(bf16[4,16,5632]{2,1,0:T(8,128)(2,1)} %collective-permute-done.4.refs_1_), channel_id=1, source_target_pairs={{0,4},{4,0},{1,5},{5,1},{2,6},{6,2},{3,7},{7,3},{8,12},{12,8},{9,1... | collective-permute-start | bytes 2162696 | tf_op jit(solution)/shard_map/ppermute | solution.py:39
  92.5 10.4 %collective-permute-start.10 = (bf16[2,16,5632]{2,1,0:T(8,128)(2,1)S(1)}, bf16[2,16,5632]{2,1,0:T(8,128)(2,1)}, u32[]{:S(2)}, u32[]{:S(2)}) collective-permute-start(bf16[2,16,5632]{2,1,0:T(8,128)(2,1)S(1)} %constant_dynamic-slice_fusion), channel_id=1, source_target_pairs={{0,8},{4,60},{8,16},{12,4},{16,24},{20,12},{24,32},{28,20},{32,40}... | collective-permute-start | bytes 1081352 | tf_op jit(solution)/shard_map/ppermute | solution.py:282
  96.8 25.3 %collective-permute-start.7 = (bf16[4,16,5632]{2,1,0:T(8,128)(2,1)}, bf16[4,16,5632]{2,1,0:T(8,128)(2,1)}, u32[]{:S(2)}, u32[]{:S(2)}) collective-permute-start(bf16[4,16,5632]{2,1,0:T(8,128)(2,1)} %collective-permute-done.6.refs_3_), channel_id=1, source_target_pairs={{0,4},{4,0},{1,5},{5,1},{2,6},{6,2},{3,7},{7,3},{8,12},{12,8},{9,1... | collective-permute-start | bytes 2162696 | tf_op jit(solution)/shard_map/ppermute | solution.py:39
  101.2 20.8 %collective-permute-start.9 = (bf16[4,16,5632]{2,1,0:T(8,128)(2,1)}, bf16[4,16,5632]{2,1,0:T(8,128)(2,1)}, u32[]{:S(2)}, u32[]{:S(2)}) collective-permute-start(bf16[4,16,5632]{2,1,0:T(8,128)(2,1)} %collective-permute-done.8.refs_5_), channel_id=1, source_target_pairs={{0,4},{4,0},{1,5},{5,1},{2,6},{6,2},{3,7},{7,3},{8,12},{12,8},{9,1... | collective-permute-start | bytes 2162696 | tf_op jit(solution)/shard_map/ppermute | solution.py:39
  101.9 9.3 %collective-permute-start.27 = (bf16[2,128,640]{2,1,0:T(8,128)(2,1)S(1)}, bf16[2,128,640]{2,1,0:T(8,128)(2,1)S(1)}, u32[]{:S(2)}, u32[]{:S(2)}) collective-permute-start(bf16[2,128,640]{2,1,0:T(8,128)(2,1)S(1)} %slice.67), channel_id=1, source_target_pairs={{0,3},{1,0},{2,1},{3,2},{4,7},{5,4},{6,5},{7,6},{8,11},{9,8},{10,9... | collective-permute-start | bytes 983048 | tf_op jit(solution)/shard_map/ppermute | solution.py:39
  102.9 19.1 %collective-permute-start.11 = (bf16[2,16,5632]{2,1,0:T(8,128)(2,1)}, bf16[2,16,5632]{2,1,0:T(8,128)(2,1)}, u32[]{:S(2)}, u32[]{:S(2)}) collective-permute-start(bf16[2,16,5632]{2,1,0:T(8,128)(2,1)} %collective-permute-done.10.refs_7_), channel_id=1, source_target_pairs={{0,4},{4,0},{1,5},{5,1},{2,6},{6,2},{3,7},{7,3},{8,12},{12,8},{9,1... | collective-permute-start | bytes 1081352 | tf_op jit(solution)/shard_map/ppermute | solution.py:39
  112.0 10.0 %collective-permute-start.26 = (bf16[2,128,640]{2,1,0:T(8,128)(2,1)}, bf16[2,128,640]{2,1,0:T(8,128)(2,1)}, u32[]{:S(2)}, u32[]{:S(2)}) collective-permute-start(bf16[2,128,640]{2,1,0:T(8,128)(2,1)} %slice.66), channel_id=1, source_target_pairs={{0,1},{1,2},{2,3},{3,0},{4,5},{5,6},{6,7},{7,4},{8,9},{9,10},{10,1... | collective-permute-start | bytes 983048 | tf_op jit(solution)/shard_map/ppermute | solution.py:39
  142.6 13.7 %all-to-all-start = ((f32[16,8,384]{2,1,0:T(8,128)}), f32[16,8,384]{2,1,0:T(8,128)S(1)}, u32[]{:S(2)}, u32[]{:S(2)}) async-start(f32[16,8,384]{2,1,0:T(8,128)} %row_maxima.1), calls=%async_computation | async-start | bytes 393216 | tf_op jit(solution)/shard_map/all_to_all | solution.py:316
  156.4 10.5 %collective-permute-start.33 = (f32[32,128]{1,0:T(8,128)S(1)}, f32[32,128]{1,0:T(8,128)S(1)}, u32[]{:S(2)}, u32[]{:S(2)}) collective-permute-start(f32[32,128]{1,0:T(8,128)S(1)} %bitcast.44), channel_id=1, source_target_pairs={{0,48},{16,0},{32,16},{48,32},{1,49},{17,1},{33,17},{49,33},{2,50}... | collective-permute-start | bytes 49160 | tf_op jit(solution)/shard_map/ppermute | solution.py:39
  161.7 5.2 %collective-permute-start.32 = (f32[32,128]{1,0:T(8,128)S(1)}, f32[32,128]{1,0:T(8,128)S(1)}, u32[]{:S(2)}, u32[]{:S(2)}) collective-permute-start(f32[32,128]{1,0:T(8,128)S(1)} %bitcast.45), channel_id=1, source_target_pairs={{0,16},{16,32},{32,48},{48,0},{1,17},{17,33},{33,49},{49,1},{2,18}... | collective-permute-start | bytes 49160 | tf_op jit(solution)/shard_map/ppermute | solution.py:39
  161.7 6.5 %collective-permute-start.31 = (f32[32,128]{1,0:T(8,128)S(1)}, f32[32,128]{1,0:T(8,128)S(1)}, u32[]{:S(2)}, u32[]{:S(2)}) collective-permute-start(f32[32,128]{1,0:T(8,128)S(1)} %bitcast.46), channel_id=1, source_target_pairs={{0,32},{16,48},{32,0},{48,16},{1,33},{17,49},{33,1},{49,17},{2,34}... | collective-permute-start | bytes 49160 | tf_op jit(solution)/shard_map/ppermute | solution.py:39
  (18 other events, 89.5 us)

commit v3 on v2

--- a/solution.py
+++ b/solution.py
@@ -32,6 +32,10 @@
 OWN_ROUTE = [(b, place_of(b)) for b in range(64)]
 HALO_ROUTE = [(b, place_of(b, 1)) for b in range(60) if b % 4]
 Z_ROUTE = [(z * 2 + c, (z + (-1 if c else 1)) % 8 * 2 + c) for z in range(8) for c in range(2)]
+
+TURNS = ((1, 3), (3, 1))
+X_ROUTES = [[(x * 2 + c, (x ^ TURNS[c][n]) * 2 + c) for x in range(4) for c in range(2)] for n in range(2)]
+Y_ROUTES = [[(c * 4 + y, c * 4 + (y ^ TURNS[c][n])) for y in range(4) for c in range(2)] for n in range(2)]
 
 
 def ring(value, axis, distance):
@@ -116,14 +120,18 @@
     )(c.reshape(1), mine, theirs)
 
 
-N_W, N_L, N_R = 9, 5, 4
+N_W, N_L, N_R = 9, 4, 4
 
 
 def main_kernel(place_ref, *refs):
     w_refs, refs = refs[:N_W], refs[N_W:]
     a_refs, b_refs, r_refs = refs[:N_L], refs[N_L : 2 * N_L], refs[2 * N_L : 2 * N_L + N_R]
     ex_ref, w, lat, rs, kn, kr, qn, qr, bias, sems = refs[2 * N_L + N_R :]
-    i_own, delta, xo, z, c = (place_ref[n] for n in range(5))
+    x, z, c, y = (place_ref[n] for n in range(4))
+    xo = lax.rem(z, 2) + 2 * c
+    met = (0, 1 + 2 * c, 3 - 2 * c, 2)
+    index = [lax.rem((x ^ m) - xo + 4, 4) for m in met]
+    slots = [lax.rem(x - (y ^ m) + 4, 4) for m in met]
     count = [0]
 
     def fetch(src, dst):
@@ -133,7 +141,7 @@
         return copy
 
     sign = 2 * c - 1
-    early = [fetch(r_refs[d], rs.at[d]) for d in range(4)]
+    early = [fetch(r_refs[d].at[:, pl.ds(640, 512)], rs.at[d]) for d in range(4)]
     late = []
     for n in range(N_W):
         step = (n + 1) // 2
@@ -145,12 +153,9 @@
             half = pl.ds(2 * c, 2) if n % 2 else pl.ds(2 - 2 * c, 2)
             late.append(fetch(w_refs[n], w.at[half, rows, :]))
     low, high = pl.ds(0, 128), pl.ds(128, 128)
-    for n, d in enumerate((0, 1, 3)):
-        late.append(fetch(a_refs[n], lat.at[d, :, low, :]))
-        late.append(fetch(b_refs[n], lat.at[:, d, high, :]))
-    for n in range(2):
-        late.append(fetch(a_refs[3 + n], lat.at[2, pl.ds(2 * n, 2), low, :]))
-        late.append(fetch(b_refs[3 + n], lat.at[pl.ds(2 * n, 2), 2, high, :]))
+    for d in range(4):
+        late.append(fetch(a_refs[d], lat.at[d, :, low, :]))
+        late.append(fetch(b_refs[d], lat.at[:, d, high, :]))
 
     for copy in early:
         copy.wait()
@@ -173,10 +178,8 @@
     q_iota = lax.broadcasted_iota(jnp.int32, (BLK, BLK), 1)
     which = []
     for d in range(4):
-        i_q = lax.rem(i_own - d + 4, 4)
         for f in range(4):
-            i_k = lax.rem(i_own - f + 4, 4)
-            at = jnp.where(i_k > i_q, f + 4, f)
+            at = jnp.where(index[f] > index[d], f + 4, f)
             which.append(at)
             seg_k = kr[2, at, :, 0:1].astype(jnp.float32)
             allowed = seg_k == seg_rows[d]
@@ -186,7 +189,6 @@
 
     for copy in late:
         copy.wait()
-    slots = [lax.rem(delta + e, 4) for e in range(4)]
     k_scale = 1.0 / math.sqrt(KVLORA)
     wk = jnp.concatenate([w[slot, :, 3 * Q_COLS :] for slot in slots], axis=0)
     for b in range(8):
@@ -226,8 +228,7 @@
                 s = jnp.max((s + bias[d, f]).reshape(BLK // 8, 8, BLK), axis=0)
                 best = s if best is None else jnp.maximum(best, s)
             row = jnp.max(best, axis=0, keepdims=True) * score_scale
-            home = 4 * xo + lax.rem(i_own - d + 4, 4)
-            ex_ref[home, h : h + 1, 0:BLK] = row
+            ex_ref[4 * xo + index[d], h : h + 1, 0:BLK] = row
             best_h = row if best_h is None else jnp.maximum(best_h, row)
         top = jnp.max(best_h, axis=1, keepdims=True)
         ex_ref[0, h : h + 1, BLK:] = jnp.broadcast_to(top, (1, 128))
@@ -266,60 +267,68 @@
     )(place, *w, *a, *b, *r)
 
 
-def exchanged_weights(x, c, wn, wr, wk):
-    parts = pack_weights(x.reshape(1), wn, wr, wk)
+def after(values, *others):
+    return lax.optimization_barrier((values, others))[0]
+
+
+def gathered(x, c, weights, latents):
+    def along_z(value):
+        return lax.ppermute(value, ("zh", "zl", "c"), Z_ROUTE)
+
+    def along(value, axis, turn):
+        if axis == "x":
+            return lax.ppermute(value, ("x", "c"), X_ROUTES[turn])
+        return lax.ppermute(value, ("c", "y"), Y_ROUTES[turn])
+
+    own, halo = pack_latents(*latents)
+    weights = after(weights, own)
+    own = lax.ppermute(own, SEQ, OWN_ROUTE)
+    halo = lax.ppermute(halo, SEQ, HALO_ROUTE)
+    parts = pack_weights(x.reshape(1), *weights)
     moved = [parts[0], ring(parts[1], "x", 1), ring(parts[2], "x", 2), ring(parts[3], "x", -1)]
     mine = jnp.stack(moved)
-    return join(c, mine, ring(mine, "c", 1))
-
-
-def gathered_weights(c, own):
-    pieces = [own]
-    held = own
-    for step in range(1, 5):
-        if step == 4:
-            held = lax.dynamic_slice_in_dim(held, 2 * c, 2, axis=0)
-        held = lax.ppermute(held, ("zh", "zl", "c"), Z_ROUTE)
-        pieces += [held, ring(held, "c", 1)]
-    return pieces
-
-
-def gathered_latents(q_latent, kv_latent, k_rope, segment_ids):
-    own, halo = pack_latents(q_latent, kv_latent, k_rope, segment_ids)
-    own = lax.ppermute(own, SEQ, OWN_ROUTE)
-    halo = lax.ppermute(halo, SEQ, HALO_ROUTE)
+    w0 = join(c, mine, ring(mine, "c", 1))
+    w1 = along_z(w0)
+
     first = jnp.concatenate([own[:128, :512], halo[:128, :128]], axis=1)
-    second = jnp.concatenate([own[128:, :512], halo[128:, :128]], axis=1)
-    ropes = [own[:128, 512:], halo[:128, 128:], own[128:, 512:], halo[128:, 128:]]
-    ropes = jnp.concatenate(ropes, axis=1)
-
-    def around(value, axis):
-        return [value, ring(value, axis, 1), ring(value, axis, 2), ring(value, axis, -1)]
-
-    def both_ways(value, axis):
-        up, down = ring(value, axis, 1), ring(value, axis, -1)
-        return [value, up, down, ring(up[:2], axis, 1), ring(down[2:], axis, -1)]
-
-    by_y, by_x, r = around(first, "y"), around(second, "x"), around(ropes, "x")
-    return both_ways(jnp.stack(by_y), "x"), both_ways(jnp.stack(by_x), "y"), r
+    second = [
+        own[128:, :512], halo[128:, :128],
+        own[:128, 512:], halo[:128, 128:], own[128:, 512:], halo[128:, 128:],
+    ]
+    second = jnp.concatenate(second, axis=1)
+    first, second = after((first, second), w0)
+    y1, y2 = along(first, "y", 0), along(first, "y", 1)
+    x1, x2 = along(second, "x", 0), along(second, "x", 1)
+    y1, y2, x1, x2, w1 = after((y1, y2, x1, x2, w1))
+    y3, x3 = along(y1, "y", 1), along(x1, "x", 1)
+    w2, w1p = along_z(w1), ring(w1, "c", 1)
+    y3, x3, w2 = after((y3, x3, w2), w1p)
+    r = [second, x1, x2, x3]
+    a = jnp.stack([first, y1, y2, y3])
+    b = jnp.stack([v[:, :640] for v in r])
+    a1, a2 = along(a, "x", 0), along(a, "x", 1)
+    b1, b2 = along(b, "y", 0), along(b, "y", 1)
+    w3 = along_z(w2)
+    a1, a2, b1, b2, w2, w3 = after((a1, a2, b1, b2, w2, w3))
+    a3, b3 = along(a1, "x", 1), along(b1, "y", 1)
+    w4 = along_z(lax.dynamic_slice_in_dim(w3, 2 * c, 2, axis=0))
+    w2p, w3p = ring(w2, "c", 1), ring(w3, "c", 1)
+    w4p = ring(w4, "c", 1)
+    return [w0, w1, w1p, w2, w2p, w3, w3p, w4, w4p], [a, a1, a2, a3], [b, b1, b2, b3], r
 
 
 def local(q_latent, kv_latent, k_rope, segment_ids, w_q_nope, w_q_rope, w_kv_nope, threshold):
     x, zh, zl, c, y = (lax.axis_index(a).astype(jnp.int32) for a in ("x", "zh", "zl", "c", "y"))
-    own = exchanged_weights(x, c, w_q_nope, w_q_rope, w_kv_nope)
-    w = gathered_weights(c, own)
-    a, b, r = gathered_latents(q_latent, kv_latent, k_rope, segment_ids)
-    xo = zl + 2 * c
-    place = jnp.stack([lax.rem(x - xo + 4, 4), lax.rem(x - y + 4, 4), xo, 2 * zh + zl, c])
-    out = main(place, w, a, b, r)
+    weights = (w_q_nope, w_q_rope, w_kv_nope)
+    latents = (q_latent, kv_latent, k_rope, segment_ids)
+    w, a, b, r = gathered(x, c, weights, latents)
+    out = main(jnp.stack([x, 2 * zh + zl, c, y]), w, a, b, r)
 
     got = lax.all_to_all(out, ("x", "zl", "c"), 0, 0, tiled=True)
     got = got.reshape(4, 4, HEADS, BLK + 128)
     top = jnp.max(got[..., BLK:], axis=1).reshape(4 * HEADS, 128)
-    top = jnp.maximum(
-        jnp.maximum(top, ring(top, "zh", 2)), jnp.maximum(ring(top, "zh", 1), ring(top, "zh", -1))
-    )
-    head_max = top[:, 0]
+    tops = lax.all_to_all(jnp.broadcast_to(top[None], (4, 32, 128)), "zh", 0, 0, tiled=True)
+    head_max = jnp.max(tops, axis=0)[:, 0]
     sent_from = 2 * lax.rem(x, 2) + x // 2
     rows = lax.dynamic_slice_in_dim(got[..., :BLK], sent_from, 1, axis=1)
     row_max = rows.reshape(4 * HEADS, BLK).T

time: 173 us -> 140 us (0.81)
  starting transfers between devices: 84.2 us -> 57.3 us
  local copies, waits for them, and re-layouts: 9.32 us -> 4.25 us
    ppermute x28 -> x8, starting transfers between devices: 55.8 us -> 10.2 us  [ring(): lax.ppermute(value, axis, [(i, (i + distance) % n) for i in range(n)])]
    ppermute x28 -> x8, waiting for transfers between devices: 36.7 us -> 0.02 us  [ring(): lax.ppermute(value, axis, [(i, (i + distance) % n) for i in range(n)])]
    ppermute x6 -> x18, waiting for transfers between devices: 7.53 us -> 37.9 us  [the longest x6 18.9 us: along(): return lax.ppermute(value, ('c', 'y'), Y_ROUTES[turn])]
    ppermute x6 -> x18, starting transfers between devices: 21.4 us -> 35.4 us  [the longest x4 13.5 us: along_z(): return lax.ppermute(value, ('zh', 'zl', 'c'), Z_ROUTE)]
    all_to_all x0 -> x1, waiting for transfers between devices: none -> 6.26 us  [local(): lax.all_to_all(jnp.broadcast_to(top[None], (4, 32, 128)), 'zh', 0, 0, til...]
    all_to_all x0 -> x1, starting transfers between devices: none -> 5.02 us  [local(): lax.all_to_all(jnp.broadcast_to(top[None], (4, 32, 128)), 'zh', 0, 0, til...]
    unnamed x30 -> x23, local copies, waits for them, and re-layouts: 6.48 us -> 1.58 us
  transfers between devices with their start and end apart: 35 -> 28, of which waited for: 15 -> 15; matrix products, arithmetic and copies ran while one was open for 2% -> 1% of each run, Pallas kernels for 1% -> 0%
where the time goes in v3:
time: 140 us; the launch traced here: 139 us
  starting transfers between devices  57.3 us (41%)
  waiting for transfers between devices  50.2 us (36%)
  Pallas kernels  22.6 us (16%)
  local copies, waits for them, and re-layouts  4.25 us (3%)
  other arithmetic  3.29 us (2%)
  between operations  1.54 us (1%)
    ppermute x6, waiting for transfers between devices, along(): return lax.ppermute(value, ('c', 'y'), Y_ROUTES[turn])  18.9 us
    pallas_call x1, Pallas kernels, main(): pl.pallas_call(main_kernel, out_shape=jax.ShapeDtypeStruct((16, HEADS, BL...  16.9 us
    ppermute x4, starting transfers between devices, along_z(): return lax.ppermute(value, ('zh', 'zl', 'c'), Z_ROUTE)  13.5 us
    ppermute x8, starting transfers between devices, ring(): lax.ppermute(value, axis, [(i, (i + distance) % n) for i in range(n)])  10.2 us
    ppermute x6, starting transfers between devices, along(): return lax.ppermute(value, ('c', 'y'), Y_ROUTES[turn])  8.28 us
    ppermute x4, waiting for transfers between devices, along_z(): return lax.ppermute(value, ('zh', 'zl', 'c'), Z_ROUTE)  6.93 us
    ppermute x6, waiting for transfers between devices, along(): return lax.ppermute(value, ('x', 'c'), X_ROUTES[turn])  6.81 us
    all_to_all x1, starting transfers between devices, local(): got = lax.all_to_all(out, ('x', 'zl', 'c'), 0, 0, tiled=True)  6.79 us
  transfers between devices with their start and end apart: 28, of which 15 were waited for; matrix products, arithmetic and copies ran while one was open for 1% of the time, Pallas kernels for 0%

profile of v3, /device:TPU:1, one launch (start us, length us, event | category | flops | bytes accessed | tf_op | source)
XLA Modules:
  0.0 139.3 jit_solution(8595669524812493866)
XLA Ops:
  0.6 2.0 %pack_latents.1 = (bf16[256,640]{1,0:T(8,128)(2,1)}, bf16[256,256]{1,0:T(8,128)(2,1)}) custom-call(bf16[256,384]{1,0:T(8,128)(2,1)} %q_ref.1, bf16[256,128]{1,0:T(8,128)(2,1)} %kv_ref.1, bf16[64,256]{1,0:T(8,128)(2,1)} %bitcast.43, s32[1,256]{1,0:T(1,128)} %bitcast.44), custom_call_target="tpu_custom_call" | custom-call | tf_op jit(solution)/shard_map/pack_latents/pallas_call | solution.py:91
  2.6 1.8 %pack_weights.1 = (bf16[8,5632]{1,0:T(8,128)(2,1)}, bf16[8,5632]{1,0:T(8,128)(2,1)}, bf16[8,5632]{1,0:T(8,128)(2,1)}, bf16[8,5632]{1,0:T(8,128)(2,1)}) custom-call(s32[1]{0:T(128)} %bitcast.1.x_ref, bf16[24,4096]{1,0:T(8,128)(2,1)} %wn_ref, bf16[24,2048]{1,0:T(8,128)(2,1)} %wr_ref, bf16[8,4096]{1,0:T(8,128)(2,1)} %wk_ref), custom_call_target="tpu_custom_call" | custom-call | tf_op jit(solution)/shard_map/pack_weights/pallas_call | solution.py:60
  4.4 3.3 %collective-permute-start.2 = (bf16[8,5632]{1,0:T(8,128)(2,1)}, bf16[8,5632]{1,0:T(8,128)(2,1)S(1)}, u32[]{:S(2)}, u32[]{:S(2)}) collective-permute-start(bf16[8,5632]{1,0:T(8,128)(2,1)} %get-tuple-element.37), channel_id=1, source_target_pairs={{0,192},{64,0},{128,64},{192,128},{1,193},{65,1},{129,65},{193,129... | collective-permute-start | bytes 270344 | tf_op jit(solution)/shard_map/ppermute | solution.py:43
  7.7 1.7 %collective-permute-start.1 = (bf16[8,5632]{1,0:T(8,128)(2,1)}, bf16[8,5632]{1,0:T(8,128)(2,1)S(1)}, u32[]{:S(2)}, u32[]{:S(2)}) collective-permute-start(bf16[8,5632]{1,0:T(8,128)(2,1)} %get-tuple-element.36), channel_id=1, source_target_pairs={{0,128},{64,192},{128,0},{192,64},{1,129},{65,193},{129,1},{193,65... | collective-permute-start | bytes 270344 | tf_op jit(solution)/shard_map/ppermute | solution.py:43
  9.4 4.8 %collective-permute-start.4 = (bf16[256,640]{1,0:T(8,128)(2,1)S(1)}, bf16[256,640]{1,0:T(8,128)(2,1)S(1)}, u32[]{:S(2)}, u32[]{:S(2)}) collective-permute-start(bf16[256,640]{1,0:T(8,128)(2,1)S(1)} %copy-done.8), channel_id=1, source_target_pairs={{0,0},{4,64},{8,128},{12,192},{16,16},{20,80},{24,144},{28,208},{3... | collective-permute-start | bytes 983048 | tf_op jit(solution)/shard_map/ppermute | solution.py:285
  14.2 6.5 %collective-permute-start.5 = (bf16[256,256]{1,0:T(8,128)(2,1)}, bf16[256,256]{1,0:T(8,128)(2,1)S(1)}, u32[]{:S(2)}, u32[]{:S(2)}) collective-permute-start(bf16[256,256]{1,0:T(8,128)(2,1)} %get-tuple-element.38), channel_id=1, source_target_pairs={{4,80},{8,144},{12,208},{20,96},{24,160},{28,224},{36,112},{40,176... | collective-permute-start | bytes 393224 | tf_op jit(solution)/shard_map/ppermute | solution.py:286
  21.9 1.6 %collective-permute-done.4 = bf16[256,640]{1,0:T(8,128)(2,1)S(1)} collective-permute-done((bf16[256,640]{1,0:T(8,128)(2,1)S(1)}, bf16[256,640]{1,0:T(8,128)(2,1)S(1)}, u32[]{:S(2)}, u32[]{:S(2)}) %collective-permute-start.4) | collective-permute-done | bytes 327712 | tf_op jit(solution)/shard_map/ppermute | solution.py:285
  23.5 3.7 %collective-permute-done.5 = bf16[256,256]{1,0:T(8,128)(2,1)S(1)} collective-permute-done((bf16[256,256]{1,0:T(8,128)(2,1)}, bf16[256,256]{1,0:T(8,128)(2,1)S(1)}, u32[]{:S(2)}, u32[]{:S(2)}) %collective-permute-start.5) | collective-permute-done | bytes 131104 | tf_op jit(solution)/shard_map/ppermute | solution.py:286
  28.0 2.0 %join_cores.1.refs_0_ = bf16[4,16,5632]{2,1,0:T(8,128)(2,1)} custom-call(s32[1]{0:T(128)} %bitcast.3.c_ref, bf16[4,8,5632]{2,1,0:T(8,128)(2,1)} %copy-done, bf16[4,8,5632]{2,1,0:T(8,128)(2,1)} %copy-done.3), custom_call_target="tpu_custom_call" | custom-call | tf_op jit(solution)/shard_map/join_cores/pallas_call | solution.py:114
  30.0 7.2 %collective-permute-start.10 = (bf16[4,16,5632]{2,1,0:T(8,128)(2,1)}, bf16[4,16,5632]{2,1,0:T(8,128)(2,1)S(1)}, u32[]{:S(2)}, u32[]{:S(2)}) collective-permute-start(bf16[4,16,5632]{2,1,0:T(8,128)(2,1)} %join_cores.1.refs_0_), channel_id=1, source_target_pairs={{0,8},{4,60},{8,16},{12,4},{16,24},{20,12},{24,32},{28,20},{32,40}... | collective-permute-start | bytes 2162696 | tf_op jit(solution)/shard_map/ppermute | solution.py:276
  37.8 2.7 %collective-permute-start.6 = (bf16[128,640]{1,0:T(8,128)(2,1)S(1)}, bf16[128,640]{1,0:T(8,128)(2,1)S(1)}, u32[]{:S(2)}, u32[]{:S(2)}) collective-permute-start(bf16[128,640]{1,0:T(8,128)(2,1)S(1)} %pad_maximum_fusion.3), channel_id=1, source_target_pairs={{0,1},{4,7},{1,0},{5,6},{2,3},{6,5},{3,2},{7,4},{8,9},{12,15},{9,8... | collective-permute-start | bytes 491528 | tf_op jit(solution)/shard_map/ppermute | solution.py:281
  40.5 3.5 %collective-permute-done.6 = bf16[128,640]{1,0:T(8,128)(2,1)S(1)} collective-permute-done((bf16[128,640]{1,0:T(8,128)(2,1)S(1)}, bf16[128,640]{1,0:T(8,128)(2,1)S(1)}, u32[]{:S(2)}, u32[]{:S(2)}) %collective-permute-start.6) | collective-permute-done | bytes 163872 | tf_op jit(solution)/shard_map/ppermute | solution.py:281
  45.7 3.0 %collective-permute-start.14 = (bf16[4,16,5632]{2,1,0:T(8,128)(2,1)S(1)}, bf16[4,16,5632]{2,1,0:T(8,128)(2,1)}, u32[]{:S(2)}, u32[]{:S(2)}) collective-permute-start(bf16[4,16,5632]{2,1,0:T(8,128)(2,1)S(1)} %collective-permute-done.10.refs_1_), channel_id=1, source_target_pairs={{0,8},{4,60},{8,16},{12,4},{16,24},{20,12},{24,32},{28,20},{32,40}... | collective-permute-start | bytes 2162696 | tf_op jit(solution)/shard_map/ppermute | solution.py:276
  48.8 1.4 collective-permute-start.12
  50.2 3.2 %collective-permute-done.12 = bf16[128,640]{1,0:T(8,128)(2,1)S(1)} collective-permute-done((bf16[128,640]{1,0:T(8,128)(2,1)S(1)}, bf16[128,640]{1,0:T(8,128)(2,1)S(1)}, u32[]{:S(2)}, u32[]{:S(2)}) %collective-permute-start.12) | collective-permute-done | bytes 163872 | tf_op jit(solution)/shard_map/ppermute | solution.py:281
  53.4 1.3 collective-permute-done.13.refs_20_
  54.7 2.3 %collective-permute-done.14.refs_3_ = bf16[4,16,5632]{2,1,0:T(8,128)(2,1)} collective-permute-done((bf16[4,16,5632]{2,1,0:T(8,128)(2,1)S(1)}, bf16[4,16,5632]{2,1,0:T(8,128)(2,1)}, u32[]{:S(2)}, u32[]{:S(2)}) %collective-permute-start.14) | collective-permute-done | bytes 720928 | tf_op jit(solution)/shard_map/ppermute | solution.py:276
  57.1 2.8 %collective-permute-start.17 = (bf16[4,128,640]{2,1,0:T(8,128)(2,1)S(1)}, bf16[4,128,640]{2,1,0:T(8,128)(2,1)S(1)}, u32[]{:S(2)}, u32[]{:S(2)}) collective-permute-start(bf16[4,128,640]{2,1,0:T(8,128)(2,1)S(1)} %pad_maximum_fusion.1.refs_13_), channel_id=1, source_target_pairs={{0,1},{4,7},{1,0},{5,6},{2,3},{6,5},{3,2},{7,4},{8,9},{12,15},{9,8... | collective-permute-start | bytes 1966088 | tf_op jit(solution)/shard_map/ppermute | solution.py:281
  60.0 3.2 %collective-permute-start.19 = (bf16[4,16,5632]{2,1,0:T(8,128)(2,1)}, bf16[4,16,5632]{2,1,0:T(8,128)(2,1)}, u32[]{:S(2)}, u32[]{:S(2)}) collective-permute-start(bf16[4,16,5632]{2,1,0:T(8,128)(2,1)} %collective-permute-done.14.refs_3_), channel_id=1, source_target_pairs={{0,8},{4,60},{8,16},{12,4},{16,24},{20,12},{24,32},{28,20},{32,40}... | collective-permute-start | bytes 2162696 | tf_op jit(solution)/shard_map/ppermute | solution.py:276
  65.0 6.4 %collective-permute-done.17.refs_14_ = bf16[4,128,640]{2,1,0:T(8,128)(2,1)S(1)} collective-permute-done((bf16[4,128,640]{2,1,0:T(8,128)(2,1)S(1)}, bf16[4,128,640]{2,1,0:T(8,128)(2,1)S(1)}, u32[]{:S(2)}, u32[]{:S(2)}) %collective-permute-start.17) | collective-permute-done | bytes 655392 | tf_op jit(solution)/shard_map/ppermute | solution.py:281
  71.4 5.1 %collective-permute-done.18.refs_15_ = bf16[4,128,640]{2,1,0:T(8,128)(2,1)} collective-permute-done((bf16[4,128,640]{2,1,0:T(8,128)(2,1)S(1)}, bf16[4,128,640]{2,1,0:T(8,128)(2,1)}, u32[]{:S(2)}, u32[]{:S(2)}) %collective-permute-start.18) | collective-permute-done | bytes 655392 | tf_op jit(solution)/shard_map/ppermute | solution.py:281
  76.5 4.0 %collective-permute-done.15.refs_10_ = bf16[4,128,640]{2,1,0:T(8,128)(2,1)} collective-permute-done((bf16[4,128,640]{2,1,0:T(8,128)(2,1)S(1)}, bf16[4,128,640]{2,1,0:T(8,128)(2,1)}, u32[]{:S(2)}, u32[]{:S(2)}) %collective-permute-start.15) | collective-permute-done | bytes 655392 | tf_op jit(solution)/shard_map/ppermute | solution.py:280
  81.5 1.5 %collective-permute-start.20 = (bf16[4,16,5632]{2,1,0:T(8,128)(2,1)}, bf16[4,16,5632]{2,1,0:T(8,128)(2,1)}, u32[]{:S(2)}, u32[]{:S(2)}) collective-permute-start(bf16[4,16,5632]{2,1,0:T(8,128)(2,1)} %collective-permute-done.14.refs_3_), channel_id=1, source_target_pairs={{0,4},{4,0},{1,5},{5,1},{2,6},{6,2},{3,7},{7,3},{8,12},{12,8},{9,1... | collective-permute-start | bytes 2162696 | tf_op jit(solution)/shard_map/ppermute | solution.py:43
  83.1 1.3 collective-permute-start.25
  84.5 3.6 %collective-permute-done.22.refs_7_ = bf16[2,16,5632]{2,1,0:T(8,128)(2,1)S(1)} collective-permute-done((bf16[2,16,5632]{2,1,0:T(8,128)(2,1)S(1)}, bf16[2,16,5632]{2,1,0:T(8,128)(2,1)S(1)}, u32[]{:S(2)}, u32[]{:S(2)}) %collective-permute-start.22) | collective-permute-done | bytes 360480 | tf_op jit(solution)/shard_map/ppermute | solution.py:276
  88.1 3.5 %collective-permute-start.23 = (bf16[2,16,5632]{2,1,0:T(8,128)(2,1)S(1)}, bf16[2,16,5632]{2,1,0:T(8,128)(2,1)}, u32[]{:S(2)}, u32[]{:S(2)}) collective-permute-start(bf16[2,16,5632]{2,1,0:T(8,128)(2,1)S(1)} %collective-permute-done.22.refs_7_), channel_id=1, source_target_pairs={{0,4},{4,0},{1,5},{5,1},{2,6},{6,2},{3,7},{7,3},{8,12},{12,8},{9,1... | collective-permute-start | bytes 1081352 | tf_op jit(solution)/shard_map/ppermute | solution.py:43
  91.6 1.5 %collective-permute-done.24.refs_12_ = bf16[4,128,640]{2,1,0:T(8,128)(2,1)} collective-permute-done((bf16[4,128,640]{2,1,0:T(8,128)(2,1)}, bf16[4,128,640]{2,1,0:T(8,128)(2,1)}, u32[]{:S(2)}, u32[]{:S(2)}) %collective-permute-start.24) | collective-permute-done | bytes 655392 | tf_op jit(solution)/shard_map/ppermute | solution.py:280
  93.2 16.9 %row_maxima.1 = f32[16,8,384]{2,1,0:T(8,128)} custom-call(s32[4]{0:T(128)S(1)} %pad_add_fusion.place_ref, bf16[4,16,5632]{2,1,0:T(8,128)(2,1)} %join_cores.1.refs_0_, bf16[4,16,5632]{2,1,0:T(8,128)(2,1)} %copy-done.6, bf16[4,16,5632]{2,1,0:T(8,128)(2,1)} %copy-done.7, bf16[4,16,5632]{2,1,0:T(8,128)(2,1)} %collective-permute-done.14.refs_3_, ...), custom_call_target="tpu_custom_call" | custom-call | flops 11274289152 | bytes 12582912 | tf_op jit(solution)/shard_map/row_maxima/pallas_call | solution.py:243
  110.1 6.8 %all-to-all-start = ((f32[16,8,384]{2,1,0:T(8,128)}), f32[16,8,384]{2,1,0:T(8,128)S(1)}, u32[]{:S(2)}, u32[]{:S(2)}) async-start(f32[16,8,384]{2,1,0:T(8,128)} %row_maxima.1), calls=%async_computation | async-start | bytes 393216 | tf_op jit(solution)/shard_map/all_to_all | solution.py:327
  117.5 6.0 %all-to-all-done = f32[16,8,384]{2,1,0:T(8,128)S(1)} async-done(((f32[16,8,384]{2,1,0:T(8,128)}), f32[16,8,384]{2,1,0:T(8,128)S(1)}, u32[]{:S(2)}, u32[]{:S(2)}) %all-to-all-start) | async-done | bytes 196640 | tf_op jit(solution)/shard_map/all_to_all | solution.py:327
  124.2 5.0 %all-to-all-start.1 = ((f32[4,32,128]{2,1,0:T(8,128)}), f32[4,32,128]{2,1,0:T(8,128)S(1)}, u32[]{:S(2)}, u32[]{:S(2)}) async-start(f32[4,32,128]{2,1,0:T(8,128)} %broadcast_in_dim.15), calls=%async_computation.1 | async-start | bytes 131072 | tf_op jit(solution)/shard_map/all_to_all | solution.py:330
  129.9 6.3 %all-to-all-done.1 = f32[4,32,128]{2,1,0:T(8,128)S(1)} async-done(((f32[4,32,128]{2,1,0:T(8,128)}), f32[4,32,128]{2,1,0:T(8,128)S(1)}, u32[]{:S(2)}, u32[]{:S(2)}) %all-to-all-start.1) | async-done | bytes 65568 | tf_op jit(solution)/shard_map/all_to_all | solution.py:330
  (74 shorter events, 11.8 us)
Async XLA Ops:
  2.6 6.8 %copy-start.8 = (bf16[256,640]{1,0:T(8,128)(2,1)S(1)}, bf16[256,640]{1,0:T(8,128)(2,1)}, u32[]{:S(2)}) copy-start(bf16[256,640]{1,0:T(8,128)(2,1)} %get-tuple-element.30) | copy-start | bytes 983044
  4.4 16.4 %collective-permute-start.2 = (bf16[8,5632]{1,0:T(8,128)(2,1)}, bf16[8,5632]{1,0:T(8,128)(2,1)S(1)}, u32[]{:S(2)}, u32[]{:S(2)}) collective-permute-start(bf16[8,5632]{1,0:T(8,128)(2,1)} %get-tuple-element.37), channel_id=1, source_target_pairs={{0,192},{64,0},{128,64},{192,128},{1,193},{65,1},{129,65},{193,129... | collective-permute-start | bytes 270344 | tf_op jit(solution)/shard_map/ppermute | solution.py:43
  7.7 13.1 %collective-permute-start = (bf16[8,5632]{1,0:T(8,128)(2,1)}, bf16[8,5632]{1,0:T(8,128)(2,1)S(1)}, u32[]{:S(2)}, u32[]{:S(2)}) collective-permute-start(bf16[8,5632]{1,0:T(8,128)(2,1)} %get-tuple-element.35), channel_id=1, source_target_pairs={{0,64},{64,128},{128,192},{192,0},{1,65},{65,129},{129,193},{193,1... | collective-permute-start | bytes 270344 | tf_op jit(solution)/shard_map/ppermute | solution.py:43
  7.7 13.1 %collective-permute-start.1 = (bf16[8,5632]{1,0:T(8,128)(2,1)}, bf16[8,5632]{1,0:T(8,128)(2,1)S(1)}, u32[]{:S(2)}, u32[]{:S(2)}) collective-permute-start(bf16[8,5632]{1,0:T(8,128)(2,1)} %get-tuple-element.36), channel_id=1, source_target_pairs={{0,128},{64,192},{128,0},{192,64},{1,129},{65,193},{129,1},{193,65... | collective-permute-start | bytes 270344 | tf_op jit(solution)/shard_map/ppermute | solution.py:43
  9.4 14.1 %collective-permute-start.4 = (bf16[256,640]{1,0:T(8,128)(2,1)S(1)}, bf16[256,640]{1,0:T(8,128)(2,1)S(1)}, u32[]{:S(2)}, u32[]{:S(2)}) collective-permute-start(bf16[256,640]{1,0:T(8,128)(2,1)S(1)} %copy-done.8), channel_id=1, source_target_pairs={{0,0},{4,64},{8,128},{12,192},{16,16},{20,80},{24,144},{28,208},{3... | collective-permute-start | bytes 983048 | tf_op jit(solution)/shard_map/ppermute | solution.py:285
  14.2 13.0 %collective-permute-start.5 = (bf16[256,256]{1,0:T(8,128)(2,1)}, bf16[256,256]{1,0:T(8,128)(2,1)S(1)}, u32[]{:S(2)}, u32[]{:S(2)}) collective-permute-start(bf16[256,256]{1,0:T(8,128)(2,1)} %get-tuple-element.38), channel_id=1, source_target_pairs={{4,80},{8,144},{12,208},{20,96},{24,160},{28,224},{36,112},{40,176... | collective-permute-start | bytes 393224 | tf_op jit(solution)/shard_map/ppermute | solution.py:286
  21.8 5.5 %copy-start = (bf16[4,8,5632]{2,1,0:T(8,128)(2,1)}, bf16[4,8,5632]{2,1,0:T(8,128)(2,1)S(1)}, u32[]{:S(2)}) copy-start(bf16[4,8,5632]{2,1,0:T(8,128)(2,1)S(1)} %pad_maximum_fusion.2.mine_ref) | copy-start | bytes 1081348
  21.8 5.5 %collective-permute-start.3 = (bf16[4,8,5632]{2,1,0:T(8,128)(2,1)S(1)}, bf16[4,8,5632]{2,1,0:T(8,128)(2,1)S(1)}, u32[]{:S(2)}, u32[]{:S(2)}) collective-permute-start(bf16[4,8,5632]{2,1,0:T(8,128)(2,1)S(1)} %pad_maximum_fusion.2.mine_ref), channel_id=1, source_target_pairs={{0,4},{4,0},{1,5},{5,1},{2,6},{6,2},{3,7},{7,3},{8,12},{12,8},{9,1... | collective-permute-start | bytes 1081352 | tf_op jit(solution)/shard_map/ppermute | solution.py:43
  30.0 15.7 %collective-permute-start.10 = (bf16[4,16,5632]{2,1,0:T(8,128)(2,1)}, bf16[4,16,5632]{2,1,0:T(8,128)(2,1)S(1)}, u32[]{:S(2)}, u32[]{:S(2)}) collective-permute-start(bf16[4,16,5632]{2,1,0:T(8,128)(2,1)} %join_cores.1.refs_0_), channel_id=1, source_target_pairs={{0,8},{4,60},{8,16},{12,4},{16,24},{20,12},{24,32},{28,20},{32,40}... | collective-permute-start | bytes 2162696 | tf_op jit(solution)/shard_map/ppermute | solution.py:276
  37.2 7.4 %collective-permute-start.8 = (bf16[128,1152]{1,0:T(8,128)(2,1)S(1)}, bf16[128,1152]{1,0:T(8,128)(2,1)S(1)}, u32[]{:S(2)}, u32[]{:S(2)}) collective-permute-start(bf16[128,1152]{1,0:T(8,128)(2,1)S(1)} %get-tuple-element.40.refs_17_), channel_id=1, source_target_pairs={{0,64},{4,196},{64,0},{68,132},{128,192},{132,68},{192,128},{196,4... | collective-permute-start | bytes 884744 | tf_op jit(solution)/shard_map/ppermute | solution.py:280
  37.8 6.9 %collective-permute-start.9 = (bf16[128,1152]{1,0:T(8,128)(2,1)S(1)}, bf16[128,1152]{1,0:T(8,128)(2,1)S(1)}, u32[]{:S(2)}, u32[]{:S(2)}) collective-permute-start(bf16[128,1152]{1,0:T(8,128)(2,1)S(1)} %get-tuple-element.40.refs_17_), channel_id=1, source_target_pairs={{0,192},{4,68},{64,128},{68,4},{128,64},{132,196},{192,0},{196,132... | collective-permute-start | bytes 884744 | tf_op jit(solution)/shard_map/ppermute | solution.py:280
  37.8 6.3 %collective-permute-start.6 = (bf16[128,640]{1,0:T(8,128)(2,1)S(1)}, bf16[128,640]{1,0:T(8,128)(2,1)S(1)}, u32[]{:S(2)}, u32[]{:S(2)}) collective-permute-start(bf16[128,640]{1,0:T(8,128)(2,1)S(1)} %pad_maximum_fusion.3), channel_id=1, source_target_pairs={{0,1},{4,7},{1,0},{5,6},{2,3},{6,5},{3,2},{7,4},{8,9},{12,15},{9,8... | collective-permute-start | bytes 491528 | tf_op jit(solution)/shard_map/ppermute | solution.py:281
  40.5 4.2 %collective-permute-start.7 = (bf16[128,640]{1,0:T(8,128)(2,1)S(1)}, bf16[128,640]{1,0:T(8,128)(2,1)S(1)}, u32[]{:S(2)}, u32[]{:S(2)}) collective-permute-start(bf16[128,640]{1,0:T(8,128)(2,1)S(1)} %pad_maximum_fusion.3), channel_id=1, source_target_pairs={{0,3},{4,5},{1,2},{5,4},{2,1},{6,7},{3,0},{7,6},{8,11},{12,13},{9,... | collective-permute-start | bytes 491528 | tf_op jit(solution)/shard_map/ppermute | solution.py:281
  45.7 11.3 %copy-start.6 = (bf16[4,16,5632]{2,1,0:T(8,128)(2,1)}, bf16[4,16,5632]{2,1,0:T(8,128)(2,1)S(1)}, u32[]{:S(2)}) copy-start(bf16[4,16,5632]{2,1,0:T(8,128)(2,1)S(1)} %collective-permute-done.10.refs_1_) | copy-start | bytes 2162692
  45.7 9.0 %collective-permute-start.11 = (bf16[4,16,5632]{2,1,0:T(8,128)(2,1)S(1)}, bf16[4,16,5632]{2,1,0:T(8,128)(2,1)S(1)}, u32[]{:S(2)}, u32[]{:S(2)}) collective-permute-start(bf16[4,16,5632]{2,1,0:T(8,128)(2,1)S(1)} %collective-permute-done.10.refs_1_), channel_id=1, source_target_pairs={{0,4},{4,0},{1,5},{5,1},{2,6},{6,2},{3,7},{7,3},{8,12},{12,8},{9,1... | collective-permute-start | bytes 2162696 | tf_op jit(solution)/shard_map/ppermute | solution.py:43
  45.7 11.2 %collective-permute-start.14 = (bf16[4,16,5632]{2,1,0:T(8,128)(2,1)S(1)}, bf16[4,16,5632]{2,1,0:T(8,128)(2,1)}, u32[]{:S(2)}, u32[]{:S(2)}) collective-permute-start(bf16[4,16,5632]{2,1,0:T(8,128)(2,1)S(1)} %collective-permute-done.10.refs_1_), channel_id=1, source_target_pairs={{0,8},{4,60},{8,16},{12,4},{16,24},{20,12},{24,32},{28,20},{32,40}... | collective-permute-start | bytes 2162696 | tf_op jit(solution)/shard_map/ppermute | solution.py:276
  48.8 6.0 %collective-permute-start.13 = (bf16[128,1152]{1,0:T(8,128)(2,1)S(1)}, bf16[128,1152]{1,0:T(8,128)(2,1)S(1)}, u32[]{:S(2)}, u32[]{:S(2)}) collective-permute-start(bf16[128,1152]{1,0:T(8,128)(2,1)S(1)} %collective-permute-done.8.refs_18_), channel_id=1, source_target_pairs={{0,192},{4,68},{64,128},{68,4},{128,64},{132,196},{192,0},{196,132... | collective-permute-start | bytes 884744 | tf_op jit(solution)/shard_map/ppermute | solution.py:280
  48.8 4.7 %collective-permute-start.12 = (bf16[128,640]{1,0:T(8,128)(2,1)S(1)}, bf16[128,640]{1,0:T(8,128)(2,1)S(1)}, u32[]{:S(2)}, u32[]{:S(2)}) collective-permute-start(bf16[128,640]{1,0:T(8,128)(2,1)S(1)} %collective-permute-done.6), channel_id=1, source_target_pairs={{0,3},{4,5},{1,2},{5,4},{2,1},{6,7},{3,0},{7,6},{8,11},{12,13},{9,... | collective-permute-start | bytes 491528 | tf_op jit(solution)/shard_map/ppermute | solution.py:281
  57.1 14.3 %collective-permute-start.17 = (bf16[4,128,640]{2,1,0:T(8,128)(2,1)S(1)}, bf16[4,128,640]{2,1,0:T(8,128)(2,1)S(1)}, u32[]{:S(2)}, u32[]{:S(2)}) collective-permute-start(bf16[4,128,640]{2,1,0:T(8,128)(2,1)S(1)} %pad_maximum_fusion.1.refs_13_), channel_id=1, source_target_pairs={{0,1},{4,7},{1,0},{5,6},{2,3},{6,5},{3,2},{7,4},{8,9},{12,15},{9,8... | collective-permute-start | bytes 1966088 | tf_op jit(solution)/shard_map/ppermute | solution.py:281
  60.0 16.5 %collective-permute-start.18 = (bf16[4,128,640]{2,1,0:T(8,128)(2,1)S(1)}, bf16[4,128,640]{2,1,0:T(8,128)(2,1)}, u32[]{:S(2)}, u32[]{:S(2)}) collective-permute-start(bf16[4,128,640]{2,1,0:T(8,128)(2,1)S(1)} %pad_maximum_fusion.1.refs_13_), channel_id=1, source_target_pairs={{0,3},{4,5},{1,2},{5,4},{2,1},{6,7},{3,0},{7,6},{8,11},{12,13},{9,... | collective-permute-start | bytes 1966088 | tf_op jit(solution)/shard_map/ppermute | solution.py:281
  60.0 20.5 %collective-permute-start.19 = (bf16[4,16,5632]{2,1,0:T(8,128)(2,1)}, bf16[4,16,5632]{2,1,0:T(8,128)(2,1)}, u32[]{:S(2)}, u32[]{:S(2)}) collective-permute-start(bf16[4,16,5632]{2,1,0:T(8,128)(2,1)} %collective-permute-done.14.refs_3_), channel_id=1, source_target_pairs={{0,8},{4,60},{8,16},{12,4},{16,24},{20,12},{24,32},{28,20},{32,40}... | collective-permute-start | bytes 2162696 | tf_op jit(solution)/shard_map/ppermute | solution.py:276
  63.3 17.2 %collective-permute-start.15 = (bf16[4,128,640]{2,1,0:T(8,128)(2,1)S(1)}, bf16[4,128,640]{2,1,0:T(8,128)(2,1)}, u32[]{:S(2)}, u32[]{:S(2)}) collective-permute-start(bf16[4,128,640]{2,1,0:T(8,128)(2,1)S(1)} %pad_maximum_fusion.refs_9_), channel_id=1, source_target_pairs={{0,64},{4,196},{64,0},{68,132},{128,192},{132,68},{192,128},{196,4... | collective-permute-start | bytes 1966088 | tf_op jit(solution)/shard_map/ppermute | solution.py:280
  63.8 16.6 %collective-permute-start.16 = (bf16[4,128,640]{2,1,0:T(8,128)(2,1)S(1)}, bf16[4,128,640]{2,1,0:T(8,128)(2,1)}, u32[]{:S(2)}, u32[]{:S(2)}) collective-permute-start(bf16[4,128,640]{2,1,0:T(8,128)(2,1)S(1)} %pad_maximum_fusion.refs_9_), channel_id=1, source_target_pairs={{0,192},{4,68},{64,128},{68,4},{128,64},{132,196},{192,0},{196,132... | collective-permute-start | bytes 1966088 | tf_op jit(solution)/shard_map/ppermute | solution.py:280
  81.5 6.6 %collective-permute-start.22 = (bf16[2,16,5632]{2,1,0:T(8,128)(2,1)S(1)}, bf16[2,16,5632]{2,1,0:T(8,128)(2,1)S(1)}, u32[]{:S(2)}, u32[]{:S(2)}) collective-permute-start(bf16[2,16,5632]{2,1,0:T(8,128)(2,1)S(1)} %constant_dynamic-slice_fusion), channel_id=1, source_target_pairs={{0,8},{4,60},{8,16},{12,4},{16,24},{20,12},{24,32},{28,20},{32,40}... | collective-permute-start | bytes 1081352 | tf_op jit(solution)/shard_map/ppermute | solution.py:276
  81.5 11.6 %collective-permute-start.20 = (bf16[4,16,5632]{2,1,0:T(8,128)(2,1)}, bf16[4,16,5632]{2,1,0:T(8,128)(2,1)}, u32[]{:S(2)}, u32[]{:S(2)}) collective-permute-start(bf16[4,16,5632]{2,1,0:T(8,128)(2,1)} %collective-permute-done.14.refs_3_), channel_id=1, source_target_pairs={{0,4},{4,0},{1,5},{5,1},{2,6},{6,2},{3,7},{7,3},{8,12},{12,8},{9,1... | collective-permute-start | bytes 2162696 | tf_op jit(solution)/shard_map/ppermute | solution.py:43
  83.0 10.2 %collective-permute-start.21 = (bf16[4,16,5632]{2,1,0:T(8,128)(2,1)}, bf16[4,16,5632]{2,1,0:T(8,128)(2,1)}, u32[]{:S(2)}, u32[]{:S(2)}) collective-permute-start(bf16[4,16,5632]{2,1,0:T(8,128)(2,1)} %collective-permute-done.19.refs_5_), channel_id=1, source_target_pairs={{0,4},{4,0},{1,5},{5,1},{2,6},{6,2},{3,7},{7,3},{8,12},{12,8},{9,1... | collective-permute-start | bytes 2162696 | tf_op jit(solution)/shard_map/ppermute | solution.py:43
  83.1 10.0 %collective-permute-start.24 = (bf16[4,128,640]{2,1,0:T(8,128)(2,1)}, bf16[4,128,640]{2,1,0:T(8,128)(2,1)}, u32[]{:S(2)}, u32[]{:S(2)}) collective-permute-start(bf16[4,128,640]{2,1,0:T(8,128)(2,1)} %collective-permute-done.15.refs_10_), channel_id=1, source_target_pairs={{0,192},{4,68},{64,128},{68,4},{128,64},{132,196},{192,0},{196,132... | collective-permute-start | bytes 1966088 | tf_op jit(solution)/shard_map/ppermute | solution.py:280
  83.1 10.0 %collective-permute-start.25 = (bf16[4,128,640]{2,1,0:T(8,128)(2,1)S(1)}, bf16[4,128,640]{2,1,0:T(8,128)(2,1)}, u32[]{:S(2)}, u32[]{:S(2)}) collective-permute-start(bf16[4,128,640]{2,1,0:T(8,128)(2,1)S(1)} %collective-permute-done.17.refs_14_), channel_id=1, source_target_pairs={{0,3},{4,5},{1,2},{5,4},{2,1},{6,7},{3,0},{7,6},{8,11},{12,13},{9,... | collective-permute-start | bytes 1966088 | tf_op jit(solution)/shard_map/ppermute | solution.py:281
  88.1 5.1 %collective-permute-start.23 = (bf16[2,16,5632]{2,1,0:T(8,128)(2,1)S(1)}, bf16[2,16,5632]{2,1,0:T(8,128)(2,1)}, u32[]{:S(2)}, u32[]{:S(2)}) collective-permute-start(bf16[2,16,5632]{2,1,0:T(8,128)(2,1)S(1)} %collective-permute-done.22.refs_7_), channel_id=1, source_target_pairs={{0,4},{4,0},{1,5},{5,1},{2,6},{6,2},{3,7},{7,3},{8,12},{12,8},{9,1... | collective-permute-start | bytes 1081352 | tf_op jit(solution)/shard_map/ppermute | solution.py:43
  110.1 13.5 %all-to-all-start = ((f32[16,8,384]{2,1,0:T(8,128)}), f32[16,8,384]{2,1,0:T(8,128)S(1)}, u32[]{:S(2)}, u32[]{:S(2)}) async-start(f32[16,8,384]{2,1,0:T(8,128)} %row_maxima.1), calls=%async_computation | async-start | bytes 393216 | tf_op jit(solution)/shard_map/all_to_all | solution.py:327
  123.6 13.3 %copy-start.1 = (bf16[24,4096]{1,0:T(8,128)(2,1)S(1)}, bf16[24,4096]{1,0:T(8,128)(2,1)}, u32[]{:S(2)}) copy-start(bf16[24,4096]{1,0:T(8,128)(2,1)} %wn_ref) | copy-start | bytes 589828
  124.2 11.9 %all-to-all-start.1 = ((f32[4,32,128]{2,1,0:T(8,128)}), f32[4,32,128]{2,1,0:T(8,128)S(1)}, u32[]{:S(2)}, u32[]{:S(2)}) async-start(f32[4,32,128]{2,1,0:T(8,128)} %broadcast_in_dim.15), calls=%async_computation.1 | async-start | bytes 131072 | tf_op jit(solution)/shard_map/all_to_all | solution.py:330
  (5 other events, 5.3 us)

commit v4 on v3

--- a/solution.py
+++ b/solution.py
@@ -14,7 +14,6 @@
 KVLORA = 512
 BLK = 256
 HEADS = 8
-NX = 4
 Q_COLS = HEADS * (D_NOPE + D_ROPE)
 W_COLS = 3 * Q_COLS + HEADS * D_NOPE
 NEG = -1e30
@@ -120,7 +119,7 @@
     )(c.reshape(1), mine, theirs)
 
 
-N_W, N_L, N_R = 9, 4, 4
+N_W, N_L, N_R = 8, 4, 4
 
 
 def main_kernel(place_ref, *refs):
@@ -140,22 +139,31 @@
         copy.start()
         return copy
 
+    low, high = pl.ds(0, 128), pl.ds(128, 128)
+    key_lanes, query_lanes = pl.ds(384, 256), pl.ds(0, 384)
+    key_columns, query_columns = pl.ds(3 * Q_COLS, 1024), pl.ds(0, 3 * Q_COLS)
+
+    def fetch_latents(lanes):
+        copies = []
+        for n in range(4):
+            copies.append(fetch(a_refs[n].at[:, :, lanes], lat.at[n, :, low, lanes]))
+            copies.append(fetch(b_refs[n].at[:, :, lanes], lat.at[:, n, high, lanes]))
+        return copies
+
     sign = 2 * c - 1
+
+    def fetch_weights(columns):
+        copies = []
+        for n in range(N_W):
+            step = (n + 1) // 2
+            towards = sign if n % 2 else -sign
+            rows = pl.ds(pl.multiple_of(lax.rem(z + towards * step + 8, 8) * 16, 16), 16)
+            copies.append(fetch(w_refs[n].at[:, :, columns], w.at[:, rows, columns]))
+        return copies
+
     early = [fetch(r_refs[d].at[:, pl.ds(640, 512)], rs.at[d]) for d in range(4)]
-    late = []
-    for n in range(N_W):
-        step = (n + 1) // 2
-        towards = sign if n % 2 else -sign
-        rows = pl.ds(pl.multiple_of(lax.rem(z + towards * step + 8, 8) * 16, 16), 16)
-        if step < 4:
-            late.append(fetch(w_refs[n], w.at[:, rows, :]))
-        else:
-            half = pl.ds(2 * c, 2) if n % 2 else pl.ds(2 - 2 * c, 2)
-            late.append(fetch(w_refs[n], w.at[half, rows, :]))
-    low, high = pl.ds(0, 128), pl.ds(128, 128)
-    for d in range(4):
-        late.append(fetch(a_refs[d], lat.at[d, :, low, :]))
-        late.append(fetch(b_refs[d], lat.at[:, d, high, :]))
+    middle = fetch_weights(key_columns) + fetch_latents(key_lanes)
+    late = fetch_weights(query_columns) + fetch_latents(query_lanes)
 
     for copy in early:
         copy.wait()
@@ -187,7 +195,7 @@
                 allowed = allowed & (k_iota <= q_iota)
             bias[d, f] = jnp.where(allowed, 0.0, NEG)
 
-    for copy in late:
+    for copy in middle:
         copy.wait()
     k_scale = 1.0 / math.sqrt(KVLORA)
     wk = jnp.concatenate([w[slot, :, 3 * Q_COLS :] for slot in slots], axis=0)
@@ -195,6 +203,8 @@
         at = 384 + 128 * (b // 4)
         kv = jnp.concatenate([lat[b % 4, e, :, at : at + 128] for e in range(4)], axis=1)
         kn[b] = (jnp.dot(kv, wk, preferred_element_type=jnp.float32) * k_scale).astype(jnp.bfloat16)
+    for copy in late:
+        copy.wait()
     q_scale = 1.0 / math.sqrt(QLORA)
     for out, at, columns in ((qn, 0, 512), (qn, 512, 512), (qr, 1024, 512)):
         wq = [
@@ -255,7 +265,7 @@
             pltpu.VMEM((4, BLK, 1024), bf16),
             pltpu.VMEM((4, BLK, 512), bf16),
             pltpu.VMEM((4, 4, BLK, BLK), f32),
-            pltpu.SemaphoreType.DMA((N_W + 2 * N_L + N_R,)),
+            pltpu.SemaphoreType.DMA((2 * N_W + 4 * N_L + N_R,)),
         ],
         compiler_params=pltpu.CompilerParams(vmem_limit_bytes=48 * 2**20),
         cost_estimate=pl.CostEstimate(
@@ -264,7 +274,7 @@
             transcendentals=0,
         ),
         name="row_maxima",
-    )(place, *w, *a, *b, *r)
+    )(place, *(pltpu.with_memory_space_constraint(v, pltpu.HBM) for v in (*w, *a, *b, *r)))
 
 
 def after(values, *others):
@@ -282,14 +292,13 @@
 
     own, halo = pack_latents(*latents)
     weights = after(weights, own)
+    halo = lax.ppermute(halo, SEQ, HALO_ROUTE)
     own = lax.ppermute(own, SEQ, OWN_ROUTE)
-    halo = lax.ppermute(halo, SEQ, HALO_ROUTE)
     parts = pack_weights(x.reshape(1), *weights)
     moved = [parts[0], ring(parts[1], "x", 1), ring(parts[2], "x", 2), ring(parts[3], "x", -1)]
     mine = jnp.stack(moved)
     w0 = join(c, mine, ring(mine, "c", 1))
     w1 = along_z(w0)
-
     first = jnp.concatenate([own[:128, :512], halo[:128, :128]], axis=1)
     second = [
         own[128:, :512], halo[128:, :128],
@@ -311,10 +320,43 @@
     w3 = along_z(w2)
     a1, a2, b1, b2, w2, w3 = after((a1, a2, b1, b2, w2, w3))
     a3, b3 = along(a1, "x", 1), along(b1, "y", 1)
-    w4 = along_z(lax.dynamic_slice_in_dim(w3, 2 * c, 2, axis=0))
-    w2p, w3p = ring(w2, "c", 1), ring(w3, "c", 1)
-    w4p = ring(w4, "c", 1)
-    return [w0, w1, w1p, w2, w2p, w3, w3p, w4, w4p], [a, a1, a2, a3], [b, b1, b2, b3], r
+    w4, w2p, w3p = along_z(w3), ring(w2, "c", 1), ring(w3, "c", 1)
+    return [w0, w1, w1p, w2, w2p, w3, w3p, w4], [a, a1, a2, a3], [b, b1, b2, b3], r
+
+
+def scale_kernel(threshold_ref, tops_ref, wn_ref, wr_ref, wk_ref, nn_ref, nr_ref, nk_ref, hm_ref):
+    top = tops_ref[0]
+    for n in range(1, 4):
+        top = jnp.maximum(top, tops_ref[n])
+    threshold = jnp.full(top.shape, threshold_ref[0], jnp.float32)
+    clip = threshold / jnp.maximum(top, threshold)
+    root = jnp.sqrt(clip)
+    for h in range(32):
+        at = slice(h * 128, h * 128 + 128)
+        by = root[h : h + 1, :]
+        nn_ref[:, at] = (wn_ref[:, at].astype(jnp.float32) * by).astype(jnp.bfloat16)
+        nk_ref[:, at] = (wk_ref[:, at].astype(jnp.float32) * by).astype(jnp.bfloat16)
+    lane = lax.broadcasted_iota(jnp.int32, (1, 128), 1)
+    for p in range(16):
+        at = slice(p * 128, p * 128 + 128)
+        by = jnp.where(lane < 64, clip[2 * p : 2 * p + 1, :], clip[2 * p + 1 : 2 * p + 2, :])
+        nr_ref[:, at] = (wr_ref[:, at].astype(jnp.float32) * by).astype(jnp.bfloat16)
+    row = lax.broadcasted_iota(jnp.int32, (32, 128), 0)
+    column = lax.broadcasted_iota(jnp.int32, (32, 128), 1)
+    line = jnp.sum(jnp.where(row == column, top, 0.0), axis=0, keepdims=True)
+    hm_ref[...] = line[:, :32]
+
+
+def scaled(threshold, tops, wn, wr, wk):
+    vmem = pl.BlockSpec(memory_space=pltpu.VMEM)
+    return pl.pallas_call(
+        scale_kernel,
+        out_shape=[jax.ShapeDtypeStruct(v.shape, v.dtype) for v in (wn, wr, wk)]
+        + [jax.ShapeDtypeStruct((1, 32), jnp.float32)],
+        in_specs=[pl.BlockSpec(memory_space=pltpu.SMEM)] + [vmem] * 4,
+        out_specs=[vmem] * 4,
+        name="scaled_weights",
+    )(threshold, tops, wn, wr, wk)
 
 
 def local(q_latent, kv_latent, k_rope, segment_ids, w_q_nope, w_q_rope, w_kv_nope, threshold):
@@ -328,23 +370,12 @@
     got = got.reshape(4, 4, HEADS, BLK + 128)
     top = jnp.max(got[..., BLK:], axis=1).reshape(4 * HEADS, 128)
     tops = lax.all_to_all(jnp.broadcast_to(top[None], (4, 32, 128)), "zh", 0, 0, tiled=True)
-    head_max = jnp.max(tops, axis=0)[:, 0]
+    new_q_nope, new_q_rope, new_kv_nope, head_max = scaled(threshold, tops, *weights)
     sent_from = 2 * lax.rem(x, 2) + x // 2
     rows = lax.dynamic_slice_in_dim(got[..., :BLK], sent_from, 1, axis=1)
     row_max = rows.reshape(4 * HEADS, BLK).T
 
-    clip = threshold[0] / jnp.maximum(head_max, threshold[0])
-    root = jnp.sqrt(clip)
-    new_q_nope = (w_q_nope.astype(jnp.float32) * jnp.repeat(root, D_NOPE)[None, :]).astype(
-        jnp.bfloat16
-    )
-    new_q_rope = (w_q_rope.astype(jnp.float32) * jnp.repeat(clip, D_ROPE)[None, :]).astype(
-        jnp.bfloat16
-    )
-    new_kv_nope = (w_kv_nope.astype(jnp.float32) * jnp.repeat(root, D_NOPE)[None, :]).astype(
-        jnp.bfloat16
-    )
-    return (new_q_nope, new_q_rope, new_kv_nope, head_max, row_max)
+    return (new_q_nope, new_q_rope, new_kv_nope, head_max.reshape(32), row_max)
 
 
 def solution(mesh):

time: 140 us -> 138 us (0.986)
  starting transfers between devices: 57.3 us -> 55.1 us
  waiting for transfers between devices: 50.2 us -> 52.3 us
  other arithmetic: 3.29 us -> 1.24 us
    ppermute x6, waiting for transfers between devices: 6.81 us -> 12.7 us  [along(): return lax.ppermute(value, ('x', 'c'), X_ROUTES[turn])]
    ppermute x4, waiting for transfers between devices: 6.93 us -> 2.51 us  [along_z(): return lax.ppermute(value, ('zh', 'zl', 'c'), Z_ROUTE)]
    ppermute x8 -> x7, starting transfers between devices: 10.2 us -> 7.35 us  [ring(): lax.ppermute(value, axis, [(i, (i + distance) % n) for i in range(n)])]
    ppermute x6, starting transfers between devices: 2.24 us -> 4.7 us  [along(): return lax.ppermute(value, ('x', 'c'), X_ROUTES[turn])]
    convert_element_type x3 -> x0, other arithmetic: 2.03 us -> none  [the longest x1 0.73 us: local(): (w_q_nope.astype(jnp.float32) * jnp.repeat(root, D_NOPE)[None, :]).astype...]
    pallas_call x0 -> x1, Pallas kernels: none -> 1.82 us  [scaled(): pl.pallas_call(scale_kernel, out_shape=[jax.ShapeDtypeStruct(v.shape, v.d...]
  transfers between devices with their start and end apart: 28 -> 27, of which waited for: 15 -> 16; matrix products, arithmetic and copies ran while one was open for 1% -> 1% of each run, Pallas kernels for 0% -> 0%
where the time goes in v4:
time: 138 us; the launch traced here: 137 us
  starting transfers between devices  55.1 us (40%)
  waiting for transfers between devices  52.3 us (38%)
  Pallas kernels  23.3 us (17%)
  local copies, waits for them, and re-layouts  3.88 us (3%)
  between operations  1.62 us (1%)
    ppermute x6, waiting for transfers between devices, along(): return lax.ppermute(value, ('c', 'y'), Y_ROUTES[turn])  19.5 us
    pallas_call x1, Pallas kernels, main(): pl.pallas_call(main_kernel, out_shape=jax.ShapeDtypeStruct((16, HEADS, BL...  15.7 us
    ppermute x4, starting transfers between devices, along_z(): return lax.ppermute(value, ('zh', 'zl', 'c'), Z_ROUTE)  14.4 us
    ppermute x6, waiting for transfers between devices, along(): return lax.ppermute(value, ('x', 'c'), X_ROUTES[turn])  12.7 us
    ppermute x6, starting transfers between devices, along(): return lax.ppermute(value, ('c', 'y'), Y_ROUTES[turn])  7.48 us
    ppermute x7, starting transfers between devices, ring(): lax.ppermute(value, axis, [(i, (i + distance) % n) for i in range(n)])  7.35 us
    all_to_all x1, starting transfers between devices, local(): got = lax.all_to_all(out, ('x', 'zl', 'c'), 0, 0, tiled=True)  6.58 us
    ppermute x1, starting transfers between devices, gathered(): halo = lax.ppermute(halo, SEQ, HALO_ROUTE)  6.53 us
  transfers between devices with their start and end apart: 27, of which 16 were waited for; matrix products, arithmetic and copies ran while one was open for 1% of the time, Pallas kernels for 0%

profile of v4, /device:TPU:1, one launch (start us, length us, event | category | flops | bytes accessed | tf_op | source)
XLA Modules:
  0.0 137.4 jit_solution(13015016143146893231)
XLA Ops:
  0.6 2.0 %pack_latents.1 = (bf16[256,640]{1,0:T(8,128)(2,1)}, bf16[256,256]{1,0:T(8,128)(2,1)}) custom-call(bf16[256,384]{1,0:T(8,128)(2,1)} %q_ref.1, bf16[256,128]{1,0:T(8,128)(2,1)} %kv_ref.1, bf16[64,256]{1,0:T(8,128)(2,1)} %bitcast.40, s32[1,256]{1,0:T(1,128)} %bitcast.41), custom_call_target="tpu_custom_call" | custom-call | tf_op jit(solution)/shard_map/pack_latents/pallas_call | solution.py:90
  2.6 1.8 %pack_weights.1 = (bf16[8,5632]{1,0:T(8,128)(2,1)}, bf16[8,5632]{1,0:T(8,128)(2,1)}, bf16[8,5632]{1,0:T(8,128)(2,1)}, bf16[8,5632]{1,0:T(8,128)(2,1)}) custom-call(s32[1]{0:T(128)} %bitcast.x_ref, bf16[24,4096]{1,0:T(8,128)(2,1)} %wn_ref.2, bf16[24,2048]{1,0:T(8,128)(2,1)} %wr_ref.2, bf16[8,4096]{1,0:T(8,128)(2,1)} %wk_ref.2), custom_call_target="tpu_custom_call" | custom-call | tf_op jit(solution)/shard_map/pack_weights/pallas_call | solution.py:59
  4.4 2.0 %collective-permute-start = (bf16[8,5632]{1,0:T(8,128)(2,1)}, bf16[8,5632]{1,0:T(8,128)(2,1)S(1)}, u32[]{:S(2)}, u32[]{:S(2)}) collective-permute-start(bf16[8,5632]{1,0:T(8,128)(2,1)} %get-tuple-element.39), channel_id=1, source_target_pairs={{0,64},{64,128},{128,192},{192,0},{1,65},{65,129},{129,193},{193,1... | collective-permute-start | bytes 270344 | tf_op jit(solution)/shard_map/ppermute | solution.py:42
  6.4 2.5 %collective-permute-start.1 = (bf16[8,5632]{1,0:T(8,128)(2,1)}, bf16[8,5632]{1,0:T(8,128)(2,1)S(1)}, u32[]{:S(2)}, u32[]{:S(2)}) collective-permute-start(bf16[8,5632]{1,0:T(8,128)(2,1)} %get-tuple-element.40), channel_id=1, source_target_pairs={{0,128},{64,192},{128,0},{192,64},{1,129},{65,193},{129,1},{193,65... | collective-permute-start | bytes 270344 | tf_op jit(solution)/shard_map/ppermute | solution.py:42
  10.0 3.6 %collective-permute-start.4 = (bf16[256,640]{1,0:T(8,128)(2,1)S(1)}, bf16[256,640]{1,0:T(8,128)(2,1)S(1)}, u32[]{:S(2)}, u32[]{:S(2)}) collective-permute-start(bf16[256,640]{1,0:T(8,128)(2,1)S(1)} %copy-done.17), channel_id=1, source_target_pairs={{0,0},{4,64},{8,128},{12,192},{16,16},{20,80},{24,144},{28,208},{3... | collective-permute-start | bytes 983048 | tf_op jit(solution)/shard_map/ppermute | solution.py:296
  13.6 6.5 %collective-permute-start.5 = (bf16[256,256]{1,0:T(8,128)(2,1)}, bf16[256,256]{1,0:T(8,128)(2,1)S(1)}, u32[]{:S(2)}, u32[]{:S(2)}) collective-permute-start(bf16[256,256]{1,0:T(8,128)(2,1)} %get-tuple-element.42), channel_id=1, source_target_pairs={{4,80},{8,144},{12,208},{20,96},{24,160},{28,224},{36,112},{40,176... | collective-permute-start | bytes 393224 | tf_op jit(solution)/shard_map/ppermute | solution.py:295
  21.3 1.6 %collective-permute-done.4 = bf16[256,640]{1,0:T(8,128)(2,1)S(1)} collective-permute-done((bf16[256,640]{1,0:T(8,128)(2,1)S(1)}, bf16[256,640]{1,0:T(8,128)(2,1)S(1)}, u32[]{:S(2)}, u32[]{:S(2)}) %collective-permute-start.4) | collective-permute-done | bytes 327712 | tf_op jit(solution)/shard_map/ppermute | solution.py:296
  22.9 3.7 %collective-permute-done.5 = bf16[256,256]{1,0:T(8,128)(2,1)S(1)} collective-permute-done((bf16[256,256]{1,0:T(8,128)(2,1)}, bf16[256,256]{1,0:T(8,128)(2,1)S(1)}, u32[]{:S(2)}, u32[]{:S(2)}) %collective-permute-start.5) | collective-permute-done | bytes 131104 | tf_op jit(solution)/shard_map/ppermute | solution.py:295
  27.4 2.0 %join_cores.1.refs_0_ = bf16[4,16,5632]{2,1,0:T(8,128)(2,1)} custom-call(s32[1]{0:T(128)} %bitcast.2.c_ref, bf16[4,8,5632]{2,1,0:T(8,128)(2,1)} %copy-done, bf16[4,8,5632]{2,1,0:T(8,128)(2,1)} %copy-done.3), custom_call_target="tpu_custom_call" | custom-call | tf_op jit(solution)/shard_map/join_cores/pallas_call | solution.py:113
  29.4 7.2 %collective-permute-start.10 = (bf16[4,16,5632]{2,1,0:T(8,128)(2,1)}, bf16[4,16,5632]{2,1,0:T(8,128)(2,1)S(1)}, u32[]{:S(2)}, u32[]{:S(2)}) collective-permute-start(bf16[4,16,5632]{2,1,0:T(8,128)(2,1)} %join_cores.1.refs_0_), channel_id=1, source_target_pairs={{0,8},{4,60},{8,16},{12,4},{16,24},{20,12},{24,32},{28,20},{32,40}... | collective-permute-start | bytes 2162696 | tf_op jit(solution)/shard_map/ppermute | solution.py:286
  36.7 1.3 collective-permute-start.8
  38.1 2.7 %collective-permute-start.6 = (bf16[128,640]{1,0:T(8,128)(2,1)S(1)}, bf16[128,640]{1,0:T(8,128)(2,1)S(1)}, u32[]{:S(2)}, u32[]{:S(2)}) collective-permute-start(bf16[128,640]{1,0:T(8,128)(2,1)S(1)} %pad_maximum_fusion.3), channel_id=1, source_target_pairs={{0,1},{4,7},{1,0},{5,6},{2,3},{6,5},{3,2},{7,4},{8,9},{12,15},{9,8... | collective-permute-start | bytes 491528 | tf_op jit(solution)/shard_map/ppermute | solution.py:291
  40.8 2.8 %collective-permute-done.6 = bf16[128,640]{1,0:T(8,128)(2,1)S(1)} collective-permute-done((bf16[128,640]{1,0:T(8,128)(2,1)S(1)}, bf16[128,640]{1,0:T(8,128)(2,1)S(1)}, u32[]{:S(2)}, u32[]{:S(2)}) %collective-permute-start.6) | collective-permute-done | bytes 163872 | tf_op jit(solution)/shard_map/ppermute | solution.py:291
  43.6 1.4 %collective-permute-done.7 = bf16[128,640]{1,0:T(8,128)(2,1)S(1)} collective-permute-done((bf16[128,640]{1,0:T(8,128)(2,1)S(1)}, bf16[128,640]{1,0:T(8,128)(2,1)S(1)}, u32[]{:S(2)}, u32[]{:S(2)}) %collective-permute-start.7) | collective-permute-done | bytes 163872 | tf_op jit(solution)/shard_map/ppermute | solution.py:291
  45.2 3.5 %collective-permute-start.14 = (bf16[4,16,5632]{2,1,0:T(8,128)(2,1)S(1)}, bf16[4,16,5632]{2,1,0:T(8,128)(2,1)}, u32[]{:S(2)}, u32[]{:S(2)}) collective-permute-start(bf16[4,16,5632]{2,1,0:T(8,128)(2,1)S(1)} %collective-permute-done.10.refs_1_), channel_id=1, source_target_pairs={{0,8},{4,60},{8,16},{12,4},{16,24},{20,12},{24,32},{28,20},{32,40}... | collective-permute-start | bytes 2162696 | tf_op jit(solution)/shard_map/ppermute | solution.py:286
  49.7 3.7 %collective-permute-done.12 = bf16[128,640]{1,0:T(8,128)(2,1)S(1)} collective-permute-done((bf16[128,640]{1,0:T(8,128)(2,1)S(1)}, bf16[128,640]{1,0:T(8,128)(2,1)S(1)}, u32[]{:S(2)}, u32[]{:S(2)}) %collective-permute-start.12) | collective-permute-done | bytes 163872 | tf_op jit(solution)/shard_map/ppermute | solution.py:291
  54.7 2.3 %collective-permute-done.14.refs_3_ = bf16[4,16,5632]{2,1,0:T(8,128)(2,1)} collective-permute-done((bf16[4,16,5632]{2,1,0:T(8,128)(2,1)S(1)}, bf16[4,16,5632]{2,1,0:T(8,128)(2,1)}, u32[]{:S(2)}, u32[]{:S(2)}) %collective-permute-start.14) | collective-permute-done | bytes 720928 | tf_op jit(solution)/shard_map/ppermute | solution.py:286
  57.1 2.3 %collective-permute-start.17 = (bf16[4,128,640]{2,1,0:T(8,128)(2,1)S(1)}, bf16[4,128,640]{2,1,0:T(8,128)(2,1)}, u32[]{:S(2)}, u32[]{:S(2)}) collective-permute-start(bf16[4,128,640]{2,1,0:T(8,128)(2,1)S(1)} %pad_maximum_fusion.1.refs_12_), channel_id=1, source_target_pairs={{0,1},{4,7},{1,0},{5,6},{2,3},{6,5},{3,2},{7,4},{8,9},{12,15},{9,8... | collective-permute-start | bytes 1966088 | tf_op jit(solution)/shard_map/ppermute | solution.py:291
  59.5 3.2 %collective-permute-start.19 = (bf16[4,16,5632]{2,1,0:T(8,128)(2,1)}, bf16[4,16,5632]{2,1,0:T(8,128)(2,1)S(1)}, u32[]{:S(2)}, u32[]{:S(2)}) collective-permute-start(bf16[4,16,5632]{2,1,0:T(8,128)(2,1)} %collective-permute-done.14.refs_3_), channel_id=1, source_target_pairs={{0,8},{4,60},{8,16},{12,4},{16,24},{20,12},{24,32},{28,20},{32,40}... | collective-permute-start | bytes 2162696 | tf_op jit(solution)/shard_map/ppermute | solution.py:286
  62.8 1.3 collective-permute-start.15
  65.3 6.3 %collective-permute-done.17.refs_13_ = bf16[4,128,640]{2,1,0:T(8,128)(2,1)} collective-permute-done((bf16[4,128,640]{2,1,0:T(8,128)(2,1)S(1)}, bf16[4,128,640]{2,1,0:T(8,128)(2,1)}, u32[]{:S(2)}, u32[]{:S(2)}) %collective-permute-start.17) | collective-permute-done | bytes 655392 | tf_op jit(solution)/shard_map/ppermute | solution.py:291
  71.6 4.4 %collective-permute-done.18.refs_14_ = bf16[4,128,640]{2,1,0:T(8,128)(2,1)S(1)} collective-permute-done((bf16[4,128,640]{2,1,0:T(8,128)(2,1)S(1)}, bf16[4,128,640]{2,1,0:T(8,128)(2,1)S(1)}, u32[]{:S(2)}, u32[]{:S(2)}) %collective-permute-start.18) | collective-permute-done | bytes 655392 | tf_op jit(solution)/shard_map/ppermute | solution.py:291
  76.0 3.5 %collective-permute-done.15.refs_9_ = bf16[4,128,640]{2,1,0:T(8,128)(2,1)} collective-permute-done((bf16[4,128,640]{2,1,0:T(8,128)(2,1)S(1)}, bf16[4,128,640]{2,1,0:T(8,128)(2,1)}, u32[]{:S(2)}, u32[]{:S(2)}) %collective-permute-start.15) | collective-permute-done | bytes 655392 | tf_op jit(solution)/shard_map/ppermute | solution.py:290
  79.8 1.5 %collective-permute-start.20 = (bf16[4,16,5632]{2,1,0:T(8,128)(2,1)}, bf16[4,16,5632]{2,1,0:T(8,128)(2,1)S(1)}, u32[]{:S(2)}, u32[]{:S(2)}) collective-permute-start(bf16[4,16,5632]{2,1,0:T(8,128)(2,1)} %collective-permute-done.14.refs_3_), channel_id=1, source_target_pairs={{0,4},{4,0},{1,5},{5,1},{2,6},{6,2},{3,7},{7,3},{8,12},{12,8},{9,1... | collective-permute-start | bytes 2162696 | tf_op jit(solution)/shard_map/ppermute | solution.py:42
  82.8 1.5 %collective-permute-start.24 = (bf16[4,128,640]{2,1,0:T(8,128)(2,1)}, bf16[4,128,640]{2,1,0:T(8,128)(2,1)}, u32[]{:S(2)}, u32[]{:S(2)}) collective-permute-start(bf16[4,128,640]{2,1,0:T(8,128)(2,1)} %collective-permute-done.17.refs_13_), channel_id=1, source_target_pairs={{0,3},{4,5},{1,2},{5,4},{2,1},{6,7},{3,0},{7,6},{8,11},{12,13},{9,... | collective-permute-start | bytes 1966088 | tf_op jit(solution)/shard_map/ppermute | solution.py:291
  84.4 7.6 %collective-permute-done.23.refs_11_ = bf16[4,128,640]{2,1,0:T(8,128)(2,1)S(1)} collective-permute-done((bf16[4,128,640]{2,1,0:T(8,128)(2,1)}, bf16[4,128,640]{2,1,0:T(8,128)(2,1)S(1)}, u32[]{:S(2)}, u32[]{:S(2)}) %collective-permute-start.23) | collective-permute-done | bytes 655392 | tf_op jit(solution)/shard_map/ppermute | solution.py:290
  94.0 15.7 %row_maxima.1 = f32[16,8,384]{2,1,0:T(8,128)} custom-call(s32[4]{0:T(128)S(1)} %pad_add_fusion.place_ref, bf16[4,16,5632]{2,1,0:T(8,128)(2,1)} %join_cores.1.refs_0_, bf16[4,16,5632]{2,1,0:T(8,128)(2,1)} %copy-done.9, bf16[4,16,5632]{2,1,0:T(8,128)(2,1)} %copy-done.10, bf16[4,16,5632]{2,1,0:T(8,128)(2,1)} %collective-permute-done.14.refs_3_, ...), custom_call_target="tpu_custom_call" | custom-call | flops 11274289152 | bytes 12582912 | tf_op jit(solution)/shard_map/row_maxima/pallas_call | solution.py:253
  109.7 6.6 %all-to-all-start = ((f32[16,8,384]{2,1,0:T(8,128)}), f32[16,8,384]{2,1,0:T(8,128)S(1)}, u32[]{:S(2)}, u32[]{:S(2)}) async-start(f32[16,8,384]{2,1,0:T(8,128)} %row_maxima.1), calls=%async_computation | async-start | bytes 393216 | tf_op jit(solution)/shard_map/all_to_all | solution.py:369
  116.9 6.0 %all-to-all-done = f32[16,8,384]{2,1,0:T(8,128)S(1)} async-done(((f32[16,8,384]{2,1,0:T(8,128)}), f32[16,8,384]{2,1,0:T(8,128)S(1)}, u32[]{:S(2)}, u32[]{:S(2)}) %all-to-all-start) | async-done | bytes 196640 | tf_op jit(solution)/shard_map/all_to_all | solution.py:369
  123.6 4.4 %all-to-all-start.1 = ((f32[4,32,128]{2,1,0:T(8,128)}), f32[4,32,128]{2,1,0:T(8,128)S(1)}, u32[]{:S(2)}, u32[]{:S(2)}) async-start(f32[4,32,128]{2,1,0:T(8,128)} %broadcast_in_dim.8), calls=%async_computation.1 | async-start | bytes 131072 | tf_op jit(solution)/shard_map/all_to_all | solution.py:372
  128.7 6.3 %all-to-all-done.1.tops_ref = f32[4,32,128]{2,1,0:T(8,128)S(1)} async-done(((f32[4,32,128]{2,1,0:T(8,128)}), f32[4,32,128]{2,1,0:T(8,128)S(1)}, u32[]{:S(2)}, u32[]{:S(2)}) %all-to-all-start.1) | async-done | bytes 65568 | tf_op jit(solution)/shard_map/all_to_all | solution.py:372
  135.6 1.8 %scaled_weights.1 = (bf16[24,4096]{1,0:T(8,128)(2,1)}, bf16[24,2048]{1,0:T(8,128)(2,1)}, bf16[8,4096]{1,0:T(8,128)(2,1)}, f32[1,32]{1,0:T(1,128)}) custom-call(f32[1]{0:T(128)S(6)} %copy.18.threshold_ref, f32[4,32,128]{2,1,0:T(8,128)} %copy-done.5, bf16[24,4096]{1,0:T(8,128)(2,1)} %wn_ref.2, bf16[24,2048]{1,0:T(8,128)(2,1)} %wr_ref.2, bf16[8,4096]{1,0:T(8,128)(2,1)} %wk_ref.2), custom_call_target="tpu_custom_call" | custom-call | tf_op jit(solution)/shard_map/scaled_weights/pallas_call | solution.py:352
  (81 shorter events, 12.7 us)
Async XLA Ops:
  2.6 7.4 %copy-start.17 = (bf16[256,640]{1,0:T(8,128)(2,1)S(1)}, bf16[256,640]{1,0:T(8,128)(2,1)}, u32[]{:S(2)}) copy-start(bf16[256,640]{1,0:T(8,128)(2,1)} %get-tuple-element.34) | copy-start | bytes 983044
  4.4 15.8 %collective-permute-start = (bf16[8,5632]{1,0:T(8,128)(2,1)}, bf16[8,5632]{1,0:T(8,128)(2,1)S(1)}, u32[]{:S(2)}, u32[]{:S(2)}) collective-permute-start(bf16[8,5632]{1,0:T(8,128)(2,1)} %get-tuple-element.39), channel_id=1, source_target_pairs={{0,64},{64,128},{128,192},{192,0},{1,65},{65,129},{129,193},{193,1... | collective-permute-start | bytes 270344 | tf_op jit(solution)/shard_map/ppermute | solution.py:42
  6.4 13.8 %collective-permute-start.1 = (bf16[8,5632]{1,0:T(8,128)(2,1)}, bf16[8,5632]{1,0:T(8,128)(2,1)S(1)}, u32[]{:S(2)}, u32[]{:S(2)}) collective-permute-start(bf16[8,5632]{1,0:T(8,128)(2,1)} %get-tuple-element.40), channel_id=1, source_target_pairs={{0,128},{64,192},{128,0},{192,64},{1,129},{65,193},{129,1},{193,65... | collective-permute-start | bytes 270344 | tf_op jit(solution)/shard_map/ppermute | solution.py:42
  8.9 11.3 %collective-permute-start.2 = (bf16[8,5632]{1,0:T(8,128)(2,1)}, bf16[8,5632]{1,0:T(8,128)(2,1)S(1)}, u32[]{:S(2)}, u32[]{:S(2)}) collective-permute-start(bf16[8,5632]{1,0:T(8,128)(2,1)} %get-tuple-element.41), channel_id=1, source_target_pairs={{0,192},{64,0},{128,64},{192,128},{1,193},{65,1},{129,65},{193,129... | collective-permute-start | bytes 270344 | tf_op jit(solution)/shard_map/ppermute | solution.py:42
  10.0 12.9 %collective-permute-start.4 = (bf16[256,640]{1,0:T(8,128)(2,1)S(1)}, bf16[256,640]{1,0:T(8,128)(2,1)S(1)}, u32[]{:S(2)}, u32[]{:S(2)}) collective-permute-start(bf16[256,640]{1,0:T(8,128)(2,1)S(1)} %copy-done.17), channel_id=1, source_target_pairs={{0,0},{4,64},{8,128},{12,192},{16,16},{20,80},{24,144},{28,208},{3... | collective-permute-start | bytes 983048 | tf_op jit(solution)/shard_map/ppermute | solution.py:296
  13.6 13.0 %collective-permute-start.5 = (bf16[256,256]{1,0:T(8,128)(2,1)}, bf16[256,256]{1,0:T(8,128)(2,1)S(1)}, u32[]{:S(2)}, u32[]{:S(2)}) collective-permute-start(bf16[256,256]{1,0:T(8,128)(2,1)} %get-tuple-element.42), channel_id=1, source_target_pairs={{4,80},{8,144},{12,208},{20,96},{24,160},{28,224},{36,112},{40,176... | collective-permute-start | bytes 393224 | tf_op jit(solution)/shard_map/ppermute | solution.py:295
  21.2 5.5 %collective-permute-start.3 = (bf16[4,8,5632]{2,1,0:T(8,128)(2,1)S(1)}, bf16[4,8,5632]{2,1,0:T(8,128)(2,1)S(1)}, u32[]{:S(2)}, u32[]{:S(2)}) collective-permute-start(bf16[4,8,5632]{2,1,0:T(8,128)(2,1)S(1)} %pad_maximum_fusion.2.mine_ref), channel_id=1, source_target_pairs={{0,4},{4,0},{1,5},{5,1},{2,6},{6,2},{3,7},{7,3},{8,12},{12,8},{9,1... | collective-permute-start | bytes 1081352 | tf_op jit(solution)/shard_map/ppermute | solution.py:42
  29.4 15.8 %collective-permute-start.10 = (bf16[4,16,5632]{2,1,0:T(8,128)(2,1)}, bf16[4,16,5632]{2,1,0:T(8,128)(2,1)S(1)}, u32[]{:S(2)}, u32[]{:S(2)}) collective-permute-start(bf16[4,16,5632]{2,1,0:T(8,128)(2,1)} %join_cores.1.refs_0_), channel_id=1, source_target_pairs={{0,8},{4,60},{8,16},{12,4},{16,24},{20,12},{24,32},{28,20},{32,40}... | collective-permute-start | bytes 2162696 | tf_op jit(solution)/shard_map/ppermute | solution.py:286
  36.7 12.0 %copy-start.4 = (bf16[128,1152]{1,0:T(8,128)(2,1)}, bf16[128,1152]{1,0:T(8,128)(2,1)S(1)}, u32[]{:S(2)}) copy-start(bf16[128,1152]{1,0:T(8,128)(2,1)S(1)} %get-tuple-element.44.refs_16_) | copy-start | bytes 884740
  36.7 8.2 %collective-permute-start.8 = (bf16[128,1152]{1,0:T(8,128)(2,1)S(1)}, bf16[128,1152]{1,0:T(8,128)(2,1)S(1)}, u32[]{:S(2)}, u32[]{:S(2)}) collective-permute-start(bf16[128,1152]{1,0:T(8,128)(2,1)S(1)} %get-tuple-element.44.refs_16_), channel_id=1, source_target_pairs={{0,64},{4,196},{64,0},{68,132},{128,192},{132,68},{192,128},{196,4... | collective-permute-start | bytes 884744 | tf_op jit(solution)/shard_map/ppermute | solution.py:290
  38.1 6.9 %collective-permute-start.9 = (bf16[128,1152]{1,0:T(8,128)(2,1)S(1)}, bf16[128,1152]{1,0:T(8,128)(2,1)S(1)}, u32[]{:S(2)}, u32[]{:S(2)}) collective-permute-start(bf16[128,1152]{1,0:T(8,128)(2,1)S(1)} %get-tuple-element.44.refs_16_), channel_id=1, source_target_pairs={{0,192},{4,68},{64,128},{68,4},{128,64},{132,196},{192,0},{196,132... | collective-permute-start | bytes 884744 | tf_op jit(solution)/shard_map/ppermute | solution.py:290
  38.1 5.5 %collective-permute-start.6 = (bf16[128,640]{1,0:T(8,128)(2,1)S(1)}, bf16[128,640]{1,0:T(8,128)(2,1)S(1)}, u32[]{:S(2)}, u32[]{:S(2)}) collective-permute-start(bf16[128,640]{1,0:T(8,128)(2,1)S(1)} %pad_maximum_fusion.3), channel_id=1, source_target_pairs={{0,1},{4,7},{1,0},{5,6},{2,3},{6,5},{3,2},{7,4},{8,9},{12,15},{9,8... | collective-permute-start | bytes 491528 | tf_op jit(solution)/shard_map/ppermute | solution.py:291
  40.8 4.2 %collective-permute-start.7 = (bf16[128,640]{1,0:T(8,128)(2,1)S(1)}, bf16[128,640]{1,0:T(8,128)(2,1)S(1)}, u32[]{:S(2)}, u32[]{:S(2)}) collective-permute-start(bf16[128,640]{1,0:T(8,128)(2,1)S(1)} %pad_maximum_fusion.3), channel_id=1, source_target_pairs={{0,3},{4,5},{1,2},{5,4},{2,1},{6,7},{3,0},{7,6},{8,11},{12,13},{9,... | collective-permute-start | bytes 491528 | tf_op jit(solution)/shard_map/ppermute | solution.py:291
  45.2 11.9 %copy-start.9 = (bf16[4,16,5632]{2,1,0:T(8,128)(2,1)}, bf16[4,16,5632]{2,1,0:T(8,128)(2,1)S(1)}, u32[]{:S(2)}) copy-start(bf16[4,16,5632]{2,1,0:T(8,128)(2,1)S(1)} %collective-permute-done.10.refs_1_) | copy-start | bytes 2162692
  45.2 9.5 %collective-permute-start.11 = (bf16[4,16,5632]{2,1,0:T(8,128)(2,1)S(1)}, bf16[4,16,5632]{2,1,0:T(8,128)(2,1)S(1)}, u32[]{:S(2)}, u32[]{:S(2)}) collective-permute-start(bf16[4,16,5632]{2,1,0:T(8,128)(2,1)S(1)} %collective-permute-done.10.refs_1_), channel_id=1, source_target_pairs={{0,4},{4,0},{1,5},{5,1},{2,6},{6,2},{3,7},{7,3},{8,12},{12,8},{9,1... | collective-permute-start | bytes 2162696 | tf_op jit(solution)/shard_map/ppermute | solution.py:42
  45.2 11.7 %collective-permute-start.14 = (bf16[4,16,5632]{2,1,0:T(8,128)(2,1)S(1)}, bf16[4,16,5632]{2,1,0:T(8,128)(2,1)}, u32[]{:S(2)}, u32[]{:S(2)}) collective-permute-start(bf16[4,16,5632]{2,1,0:T(8,128)(2,1)S(1)} %collective-permute-done.10.refs_1_), channel_id=1, source_target_pairs={{0,8},{4,60},{8,16},{12,4},{16,24},{20,12},{24,32},{28,20},{32,40}... | collective-permute-start | bytes 2162696 | tf_op jit(solution)/shard_map/ppermute | solution.py:286
  48.7 6.0 %collective-permute-start.13 = (bf16[128,1152]{1,0:T(8,128)(2,1)S(1)}, bf16[128,1152]{1,0:T(8,128)(2,1)S(1)}, u32[]{:S(2)}, u32[]{:S(2)}) collective-permute-start(bf16[128,1152]{1,0:T(8,128)(2,1)S(1)} %collective-permute-done.8.refs_17_), channel_id=1, source_target_pairs={{0,192},{4,68},{64,128},{68,4},{128,64},{132,196},{192,0},{196,132... | collective-permute-start | bytes 884744 | tf_op jit(solution)/shard_map/ppermute | solution.py:290
  48.8 4.7 %collective-permute-start.12 = (bf16[128,640]{1,0:T(8,128)(2,1)S(1)}, bf16[128,640]{1,0:T(8,128)(2,1)S(1)}, u32[]{:S(2)}, u32[]{:S(2)}) collective-permute-start(bf16[128,640]{1,0:T(8,128)(2,1)S(1)} %collective-permute-done.6), channel_id=1, source_target_pairs={{0,3},{4,5},{1,2},{5,4},{2,1},{6,7},{3,0},{7,6},{8,11},{12,13},{9,... | collective-permute-start | bytes 491528 | tf_op jit(solution)/shard_map/ppermute | solution.py:291
  57.1 14.5 %collective-permute-start.17 = (bf16[4,128,640]{2,1,0:T(8,128)(2,1)S(1)}, bf16[4,128,640]{2,1,0:T(8,128)(2,1)}, u32[]{:S(2)}, u32[]{:S(2)}) collective-permute-start(bf16[4,128,640]{2,1,0:T(8,128)(2,1)S(1)} %pad_maximum_fusion.1.refs_12_), channel_id=1, source_target_pairs={{0,1},{4,7},{1,0},{5,6},{2,3},{6,5},{3,2},{7,4},{8,9},{12,15},{9,8... | collective-permute-start | bytes 1966088 | tf_op jit(solution)/shard_map/ppermute | solution.py:291
  59.5 16.6 %collective-permute-start.18 = (bf16[4,128,640]{2,1,0:T(8,128)(2,1)S(1)}, bf16[4,128,640]{2,1,0:T(8,128)(2,1)S(1)}, u32[]{:S(2)}, u32[]{:S(2)}) collective-permute-start(bf16[4,128,640]{2,1,0:T(8,128)(2,1)S(1)} %pad_maximum_fusion.1.refs_12_), channel_id=1, source_target_pairs={{0,3},{4,5},{1,2},{5,4},{2,1},{6,7},{3,0},{7,6},{8,11},{12,13},{9,... | collective-permute-start | bytes 1966088 | tf_op jit(solution)/shard_map/ppermute | solution.py:291
  59.5 20.4 %collective-permute-start.19 = (bf16[4,16,5632]{2,1,0:T(8,128)(2,1)}, bf16[4,16,5632]{2,1,0:T(8,128)(2,1)S(1)}, u32[]{:S(2)}, u32[]{:S(2)}) collective-permute-start(bf16[4,16,5632]{2,1,0:T(8,128)(2,1)} %collective-permute-done.14.refs_3_), channel_id=1, source_target_pairs={{0,8},{4,60},{8,16},{12,4},{16,24},{20,12},{24,32},{28,20},{32,40}... | collective-permute-start | bytes 2162696 | tf_op jit(solution)/shard_map/ppermute | solution.py:286
  62.8 30.1 %copy-start.2 = (bf16[4,128,640]{2,1,0:T(8,128)(2,1)}, bf16[4,128,640]{2,1,0:T(8,128)(2,1)S(1)}, u32[]{:S(2)}) copy-start(bf16[4,128,640]{2,1,0:T(8,128)(2,1)S(1)} %pad_maximum_fusion.refs_8_) | copy-start | bytes 1966084
  62.8 16.8 %collective-permute-start.15 = (bf16[4,128,640]{2,1,0:T(8,128)(2,1)S(1)}, bf16[4,128,640]{2,1,0:T(8,128)(2,1)}, u32[]{:S(2)}, u32[]{:S(2)}) collective-permute-start(bf16[4,128,640]{2,1,0:T(8,128)(2,1)S(1)} %pad_maximum_fusion.refs_8_), channel_id=1, source_target_pairs={{0,64},{4,196},{64,0},{68,132},{128,192},{132,68},{192,128},{196,4... | collective-permute-start | bytes 1966088 | tf_op jit(solution)/shard_map/ppermute | solution.py:290
  64.1 15.7 %collective-permute-start.16 = (bf16[4,128,640]{2,1,0:T(8,128)(2,1)S(1)}, bf16[4,128,640]{2,1,0:T(8,128)(2,1)S(1)}, u32[]{:S(2)}, u32[]{:S(2)}) collective-permute-start(bf16[4,128,640]{2,1,0:T(8,128)(2,1)S(1)} %pad_maximum_fusion.refs_8_), channel_id=1, source_target_pairs={{0,192},{4,68},{64,128},{68,4},{128,64},{132,196},{192,0},{196,132... | collective-permute-start | bytes 1966088 | tf_op jit(solution)/shard_map/ppermute | solution.py:290
  79.8 13.1 %copy-start.11 = (bf16[4,16,5632]{2,1,0:T(8,128)(2,1)}, bf16[4,16,5632]{2,1,0:T(8,128)(2,1)S(1)}, u32[]{:S(2)}) copy-start(bf16[4,16,5632]{2,1,0:T(8,128)(2,1)S(1)} %collective-permute-done.19.refs_5_) | copy-start | bytes 2162692
  79.8 13.0 %collective-permute-start.20 = (bf16[4,16,5632]{2,1,0:T(8,128)(2,1)}, bf16[4,16,5632]{2,1,0:T(8,128)(2,1)S(1)}, u32[]{:S(2)}, u32[]{:S(2)}) collective-permute-start(bf16[4,16,5632]{2,1,0:T(8,128)(2,1)} %collective-permute-done.14.refs_3_), channel_id=1, source_target_pairs={{0,4},{4,0},{1,5},{5,1},{2,6},{6,2},{3,7},{7,3},{8,12},{12,8},{9,1... | collective-permute-start | bytes 2162696 | tf_op jit(solution)/shard_map/ppermute | solution.py:42
  81.4 11.5 %collective-permute-start.21 = (bf16[4,16,5632]{2,1,0:T(8,128)(2,1)S(1)}, bf16[4,16,5632]{2,1,0:T(8,128)(2,1)S(1)}, u32[]{:S(2)}, u32[]{:S(2)}) collective-permute-start(bf16[4,16,5632]{2,1,0:T(8,128)(2,1)S(1)} %collective-permute-done.19.refs_5_), channel_id=1, source_target_pairs={{0,4},{4,0},{1,5},{5,1},{2,6},{6,2},{3,7},{7,3},{8,12},{12,8},{9,1... | collective-permute-start | bytes 2162696 | tf_op jit(solution)/shard_map/ppermute | solution.py:42
  81.5 11.4 %collective-permute-start.22 = (bf16[4,16,5632]{2,1,0:T(8,128)(2,1)S(1)}, bf16[4,16,5632]{2,1,0:T(8,128)(2,1)}, u32[]{:S(2)}, u32[]{:S(2)}) collective-permute-start(bf16[4,16,5632]{2,1,0:T(8,128)(2,1)S(1)} %collective-permute-done.19.refs_5_), channel_id=1, source_target_pairs={{0,8},{4,60},{8,16},{12,4},{16,24},{20,12},{24,32},{28,20},{32,40}... | collective-permute-start | bytes 2162696 | tf_op jit(solution)/shard_map/ppermute | solution.py:286
  81.9 10.0 %collective-permute-start.23 = (bf16[4,128,640]{2,1,0:T(8,128)(2,1)}, bf16[4,128,640]{2,1,0:T(8,128)(2,1)S(1)}, u32[]{:S(2)}, u32[]{:S(2)}) collective-permute-start(bf16[4,128,640]{2,1,0:T(8,128)(2,1)} %collective-permute-done.15.refs_9_), channel_id=1, source_target_pairs={{0,192},{4,68},{64,128},{68,4},{128,64},{132,196},{192,0},{196,132... | collective-permute-start | bytes 1966088 | tf_op jit(solution)/shard_map/ppermute | solution.py:290
  82.8 10.1 %collective-permute-start.24 = (bf16[4,128,640]{2,1,0:T(8,128)(2,1)}, bf16[4,128,640]{2,1,0:T(8,128)(2,1)}, u32[]{:S(2)}, u32[]{:S(2)}) collective-permute-start(bf16[4,128,640]{2,1,0:T(8,128)(2,1)} %collective-permute-done.17.refs_13_), channel_id=1, source_target_pairs={{0,3},{4,5},{1,2},{5,4},{2,1},{6,7},{3,0},{7,6},{8,11},{12,13},{9,... | collective-permute-start | bytes 1966088 | tf_op jit(solution)/shard_map/ppermute | solution.py:291
  109.7 13.3 %all-to-all-start = ((f32[16,8,384]{2,1,0:T(8,128)}), f32[16,8,384]{2,1,0:T(8,128)S(1)}, u32[]{:S(2)}, u32[]{:S(2)}) async-start(f32[16,8,384]{2,1,0:T(8,128)} %row_maxima.1), calls=%async_computation | async-start | bytes 393216 | tf_op jit(solution)/shard_map/all_to_all | solution.py:369
  123.6 11.3 %all-to-all-start.1 = ((f32[4,32,128]{2,1,0:T(8,128)}), f32[4,32,128]{2,1,0:T(8,128)S(1)}, u32[]{:S(2)}, u32[]{:S(2)}) async-start(f32[4,32,128]{2,1,0:T(8,128)} %broadcast_in_dim.8), calls=%async_computation.1 | async-start | bytes 131072 | tf_op jit(solution)/shard_map/all_to_all | solution.py:372
  (13 other events, 36.6 us)

commit v5 on v4

--- a/solution.py
+++ b/solution.py
@@ -119,7 +119,7 @@
     )(c.reshape(1), mine, theirs)
 
 
-N_W, N_L, N_R = 8, 4, 4
+N_W, N_L, N_R = 9, 4, 4
 
 
 def main_kernel(place_ref, *refs):
@@ -158,7 +158,8 @@
             step = (n + 1) // 2
             towards = sign if n % 2 else -sign
             rows = pl.ds(pl.multiple_of(lax.rem(z + towards * step + 8, 8) * 16, 16), 16)
-            copies.append(fetch(w_refs[n].at[:, :, columns], w.at[:, rows, columns]))
+            half = pl.ds(0, 4) if step < 4 else pl.ds(2 * c if n % 2 else 2 - 2 * c, 2)
+            copies.append(fetch(w_refs[n].at[:, :, columns], w.at[half, rows, columns]))
         return copies
 
     early = [fetch(r_refs[d].at[:, pl.ds(640, 512)], rs.at[d]) for d in range(4)]
@@ -274,7 +275,7 @@
             transcendentals=0,
         ),
         name="row_maxima",
-    )(place, *(pltpu.with_memory_space_constraint(v, pltpu.HBM) for v in (*w, *a, *b, *r)))
+    )(place, *w, *a, *b, *r)
 
 
 def after(values, *others):
@@ -320,8 +321,10 @@
     w3 = along_z(w2)
     a1, a2, b1, b2, w2, w3 = after((a1, a2, b1, b2, w2, w3))
     a3, b3 = along(a1, "x", 1), along(b1, "y", 1)
-    w4, w2p, w3p = along_z(w3), ring(w2, "c", 1), ring(w3, "c", 1)
-    return [w0, w1, w1p, w2, w2p, w3, w3p, w4], [a, a1, a2, a3], [b, b1, b2, b3], r
+    w4 = along_z(lax.dynamic_slice_in_dim(w3, 2 * c, 2, axis=0))
+    w2p, w3p = ring(w2, "c", 1), ring(w3, "c", 1)
+    w4p = ring(w4, "c", 1)
+    return [w0, w1, w1p, w2, w2p, w3, w3p, w4, w4p], [a, a1, a2, a3], [b, b1, b2, b3], r
 
 
 def scale_kernel(threshold_ref, tops_ref, wn_ref, wr_ref, wk_ref, nn_ref, nr_ref, nk_ref, hm_ref):

time: 138 us -> 137 us (level)
  waiting for transfers between devices: 52.3 us -> 48.8 us
  starting transfers between devices: 55.1 us -> 58.3 us
    ppermute x6, waiting for transfers between devices: 12.7 us -> 6.75 us  [along(): return lax.ppermute(value, ('x', 'c'), X_ROUTES[turn])]
    ppermute x7 -> x8, starting transfers between devices: 7.35 us -> 10.8 us  [ring(): lax.ppermute(value, axis, [(i, (i + distance) % n) for i in range(n)])]
    ppermute x4, waiting for transfers between devices: 2.51 us -> 5.14 us  [along_z(): return lax.ppermute(value, ('zh', 'zl', 'c'), Z_ROUTE)]
  transfers between devices with their start and end apart: 27 -> 28, of which waited for: 16 -> 17; matrix products, arithmetic and copies ran while one was open for 1% -> 1% of each run, Pallas kernels for 0% -> 0%
where the time goes in v5:
time: 137 us
  starting transfers between devices  58.3 us (43%)
  waiting for transfers between devices  48.8 us (36%)
  Pallas kernels  23 us (17%)
  local copies, waits for them, and re-layouts  3.78 us (3%)
  between operations  1.5 us (1%)
    ppermute x6, waiting for transfers between devices, along(): return lax.ppermute(value, ('c', 'y'), Y_ROUTES[turn])  19.2 us
    pallas_call x1, Pallas kernels, main(): pl.pallas_call(main_kernel, out_shape=jax.ShapeDtypeStruct((16, HEADS, BL...  15.4 us
    ppermute x4, starting transfers between devices, along_z(): return lax.ppermute(value, ('zh', 'zl', 'c'), Z_ROUTE)  14 us
    ppermute x8, starting transfers between devices, ring(): lax.ppermute(value, axis, [(i, (i + distance) % n) for i in range(n)])  10.8 us
    ppermute x6, starting transfers between devices, along(): return lax.ppermute(value, ('c', 'y'), Y_ROUTES[turn])  8.37 us
    ppermute x6, waiting for transfers between devices, along(): return lax.ppermute(value, ('x', 'c'), X_ROUTES[turn])  6.75 us
    all_to_all x1, starting transfers between devices, local(): got = lax.all_to_all(out, ('x', 'zl', 'c'), 0, 0, tiled=True)  6.67 us
    ppermute x1, starting transfers between devices, gathered(): halo = lax.ppermute(halo, SEQ, HALO_ROUTE)  6.53 us
  transfers between devices with their start and end apart: 28, of which 17 were waited for; matrix products, arithmetic and copies ran while one was open for 1% of the time, Pallas kernels for 0%

profile of v5, /device:TPU:1, one launch (start us, length us, event | category | flops | bytes accessed | tf_op | source)
XLA Modules:
  0.0 136.5 jit_solution(4691495936480128985)
XLA Ops:
  0.6 2.0 %pack_latents.1 = (bf16[256,640]{1,0:T(8,128)(2,1)}, bf16[256,256]{1,0:T(8,128)(2,1)}) custom-call(bf16[256,384]{1,0:T(8,128)(2,1)} %q_ref.1, bf16[256,128]{1,0:T(8,128)(2,1)} %kv_ref.1, bf16[64,256]{1,0:T(8,128)(2,1)} %bitcast.40, s32[1,256]{1,0:T(1,128)} %bitcast.41), custom_call_target="tpu_custom_call" | custom-call | tf_op jit(solution)/shard_map/pack_latents/pallas_call | solution.py:90
  2.6 1.8 %pack_weights.1 = (bf16[8,5632]{1,0:T(8,128)(2,1)}, bf16[8,5632]{1,0:T(8,128)(2,1)}, bf16[8,5632]{1,0:T(8,128)(2,1)}, bf16[8,5632]{1,0:T(8,128)(2,1)}) custom-call(s32[1]{0:T(128)} %bitcast.x_ref, bf16[24,4096]{1,0:T(8,128)(2,1)} %wn_ref.2, bf16[24,2048]{1,0:T(8,128)(2,1)} %wr_ref.2, bf16[8,4096]{1,0:T(8,128)(2,1)} %wk_ref.2), custom_call_target="tpu_custom_call" | custom-call | tf_op jit(solution)/shard_map/pack_weights/pallas_call | solution.py:59
  4.4 2.0 %collective-permute-start = (bf16[8,5632]{1,0:T(8,128)(2,1)}, bf16[8,5632]{1,0:T(8,128)(2,1)S(1)}, u32[]{:S(2)}, u32[]{:S(2)}) collective-permute-start(bf16[8,5632]{1,0:T(8,128)(2,1)} %get-tuple-element.39), channel_id=1, source_target_pairs={{0,64},{64,128},{128,192},{192,0},{1,65},{65,129},{129,193},{193,1... | collective-permute-start | bytes 270344 | tf_op jit(solution)/shard_map/ppermute | solution.py:42
  6.4 2.5 %collective-permute-start.1 = (bf16[8,5632]{1,0:T(8,128)(2,1)}, bf16[8,5632]{1,0:T(8,128)(2,1)S(1)}, u32[]{:S(2)}, u32[]{:S(2)}) collective-permute-start(bf16[8,5632]{1,0:T(8,128)(2,1)} %get-tuple-element.40), channel_id=1, source_target_pairs={{0,128},{64,192},{128,0},{192,64},{1,129},{65,193},{129,1},{193,65... | collective-permute-start | bytes 270344 | tf_op jit(solution)/shard_map/ppermute | solution.py:42
  10.0 3.6 %collective-permute-start.4 = (bf16[256,640]{1,0:T(8,128)(2,1)S(1)}, bf16[256,640]{1,0:T(8,128)(2,1)S(1)}, u32[]{:S(2)}, u32[]{:S(2)}) collective-permute-start(bf16[256,640]{1,0:T(8,128)(2,1)S(1)} %copy-done.5), channel_id=1, source_target_pairs={{0,0},{4,64},{8,128},{12,192},{16,16},{20,80},{24,144},{28,208},{3... | collective-permute-start | bytes 983048 | tf_op jit(solution)/shard_map/ppermute | solution.py:297
  13.6 6.5 %collective-permute-start.5 = (bf16[256,256]{1,0:T(8,128)(2,1)}, bf16[256,256]{1,0:T(8,128)(2,1)S(1)}, u32[]{:S(2)}, u32[]{:S(2)}) collective-permute-start(bf16[256,256]{1,0:T(8,128)(2,1)} %get-tuple-element.42), channel_id=1, source_target_pairs={{4,80},{8,144},{12,208},{20,96},{24,160},{28,224},{36,112},{40,176... | collective-permute-start | bytes 393224 | tf_op jit(solution)/shard_map/ppermute | solution.py:296
  21.3 1.6 %collective-permute-done.4 = bf16[256,640]{1,0:T(8,128)(2,1)S(1)} collective-permute-done((bf16[256,640]{1,0:T(8,128)(2,1)S(1)}, bf16[256,640]{1,0:T(8,128)(2,1)S(1)}, u32[]{:S(2)}, u32[]{:S(2)}) %collective-permute-start.4) | collective-permute-done | bytes 327712 | tf_op jit(solution)/shard_map/ppermute | solution.py:297
  22.9 3.7 %collective-permute-done.5 = bf16[256,256]{1,0:T(8,128)(2,1)S(1)} collective-permute-done((bf16[256,256]{1,0:T(8,128)(2,1)}, bf16[256,256]{1,0:T(8,128)(2,1)S(1)}, u32[]{:S(2)}, u32[]{:S(2)}) %collective-permute-start.5) | collective-permute-done | bytes 131104 | tf_op jit(solution)/shard_map/ppermute | solution.py:296
  27.4 2.0 %join_cores.1.refs_0_ = bf16[4,16,5632]{2,1,0:T(8,128)(2,1)} custom-call(s32[1]{0:T(128)} %bitcast.2.c_ref, bf16[4,8,5632]{2,1,0:T(8,128)(2,1)} %copy-done, bf16[4,8,5632]{2,1,0:T(8,128)(2,1)} %copy-done.1), custom_call_target="tpu_custom_call" | custom-call | tf_op jit(solution)/shard_map/join_cores/pallas_call | solution.py:113
  29.4 7.2 %collective-permute-start.10 = (bf16[4,16,5632]{2,1,0:T(8,128)(2,1)}, bf16[4,16,5632]{2,1,0:T(8,128)(2,1)S(1)}, u32[]{:S(2)}, u32[]{:S(2)}) collective-permute-start(bf16[4,16,5632]{2,1,0:T(8,128)(2,1)} %join_cores.1.refs_0_), channel_id=1, source_target_pairs={{0,8},{4,60},{8,16},{12,4},{16,24},{20,12},{24,32},{28,20},{32,40}... | collective-permute-start | bytes 2162696 | tf_op jit(solution)/shard_map/ppermute | solution.py:287
  38.0 2.7 %collective-permute-start.6 = (bf16[128,640]{1,0:T(8,128)(2,1)S(1)}, bf16[128,640]{1,0:T(8,128)(2,1)S(1)}, u32[]{:S(2)}, u32[]{:S(2)}) collective-permute-start(bf16[128,640]{1,0:T(8,128)(2,1)S(1)} %pad_maximum_fusion.3), channel_id=1, source_target_pairs={{0,1},{4,7},{1,0},{5,6},{2,3},{6,5},{3,2},{7,4},{8,9},{12,15},{9,8... | collective-permute-start | bytes 491528 | tf_op jit(solution)/shard_map/ppermute | solution.py:292
  40.8 2.8 %collective-permute-done.6 = bf16[128,640]{1,0:T(8,128)(2,1)S(1)} collective-permute-done((bf16[128,640]{1,0:T(8,128)(2,1)S(1)}, bf16[128,640]{1,0:T(8,128)(2,1)S(1)}, u32[]{:S(2)}, u32[]{:S(2)}) %collective-permute-start.6) | collective-permute-done | bytes 163872 | tf_op jit(solution)/shard_map/ppermute | solution.py:292
  43.5 1.4 %collective-permute-done.7 = bf16[128,640]{1,0:T(8,128)(2,1)S(1)} collective-permute-done((bf16[128,640]{1,0:T(8,128)(2,1)S(1)}, bf16[128,640]{1,0:T(8,128)(2,1)S(1)}, u32[]{:S(2)}, u32[]{:S(2)}) %collective-permute-start.7) | collective-permute-done | bytes 163872 | tf_op jit(solution)/shard_map/ppermute | solution.py:292
  45.2 3.5 %collective-permute-start.14 = (bf16[4,16,5632]{2,1,0:T(8,128)(2,1)S(1)}, bf16[4,16,5632]{2,1,0:T(8,128)(2,1)}, u32[]{:S(2)}, u32[]{:S(2)}) collective-permute-start(bf16[4,16,5632]{2,1,0:T(8,128)(2,1)S(1)} %collective-permute-done.10.refs_1_), channel_id=1, source_target_pairs={{0,8},{4,60},{8,16},{12,4},{16,24},{20,12},{24,32},{28,20},{32,40}... | collective-permute-start | bytes 2162696 | tf_op jit(solution)/shard_map/ppermute | solution.py:287
  49.7 3.7 %collective-permute-done.12 = bf16[128,640]{1,0:T(8,128)(2,1)S(1)} collective-permute-done((bf16[128,640]{1,0:T(8,128)(2,1)S(1)}, bf16[128,640]{1,0:T(8,128)(2,1)S(1)}, u32[]{:S(2)}, u32[]{:S(2)}) %collective-permute-start.12) | collective-permute-done | bytes 163872 | tf_op jit(solution)/shard_map/ppermute | solution.py:292
  54.7 2.3 %collective-permute-done.14.refs_3_ = bf16[4,16,5632]{2,1,0:T(8,128)(2,1)} collective-permute-done((bf16[4,16,5632]{2,1,0:T(8,128)(2,1)S(1)}, bf16[4,16,5632]{2,1,0:T(8,128)(2,1)}, u32[]{:S(2)}, u32[]{:S(2)}) %collective-permute-start.14) | collective-permute-done | bytes 720928 | tf_op jit(solution)/shard_map/ppermute | solution.py:287
  57.1 2.4 %collective-permute-start.17 = (bf16[4,128,640]{2,1,0:T(8,128)(2,1)S(1)}, bf16[4,128,640]{2,1,0:T(8,128)(2,1)S(1)}, u32[]{:S(2)}, u32[]{:S(2)}) collective-permute-start(bf16[4,128,640]{2,1,0:T(8,128)(2,1)S(1)} %pad_maximum_fusion.1.refs_13_), channel_id=1, source_target_pairs={{0,1},{4,7},{1,0},{5,6},{2,3},{6,5},{3,2},{7,4},{8,9},{12,15},{9,8... | collective-permute-start | bytes 1966088 | tf_op jit(solution)/shard_map/ppermute | solution.py:292
  59.4 3.2 %collective-permute-start.19 = (bf16[4,16,5632]{2,1,0:T(8,128)(2,1)}, bf16[4,16,5632]{2,1,0:T(8,128)(2,1)}, u32[]{:S(2)}, u32[]{:S(2)}) collective-permute-start(bf16[4,16,5632]{2,1,0:T(8,128)(2,1)} %collective-permute-done.14.refs_3_), channel_id=1, source_target_pairs={{0,8},{4,60},{8,16},{12,4},{16,24},{20,12},{24,32},{28,20},{32,40}... | collective-permute-start | bytes 2162696 | tf_op jit(solution)/shard_map/ppermute | solution.py:287
  65.3 6.4 %collective-permute-done.17.refs_14_ = bf16[4,128,640]{2,1,0:T(8,128)(2,1)S(1)} collective-permute-done((bf16[4,128,640]{2,1,0:T(8,128)(2,1)S(1)}, bf16[4,128,640]{2,1,0:T(8,128)(2,1)S(1)}, u32[]{:S(2)}, u32[]{:S(2)}) %collective-permute-start.17) | collective-permute-done | bytes 655392 | tf_op jit(solution)/shard_map/ppermute | solution.py:292
  71.6 4.3 %collective-permute-done.18.refs_15_ = bf16[4,128,640]{2,1,0:T(8,128)(2,1)} collective-permute-done((bf16[4,128,640]{2,1,0:T(8,128)(2,1)S(1)}, bf16[4,128,640]{2,1,0:T(8,128)(2,1)}, u32[]{:S(2)}, u32[]{:S(2)}) %collective-permute-start.18) | collective-permute-done | bytes 655392 | tf_op jit(solution)/shard_map/ppermute | solution.py:292
  76.0 3.6 %collective-permute-done.15.refs_10_ = bf16[4,128,640]{2,1,0:T(8,128)(2,1)} collective-permute-done((bf16[4,128,640]{2,1,0:T(8,128)(2,1)S(1)}, bf16[4,128,640]{2,1,0:T(8,128)(2,1)}, u32[]{:S(2)}, u32[]{:S(2)}) %collective-permute-start.15) | collective-permute-done | bytes 655392 | tf_op jit(solution)/shard_map/ppermute | solution.py:291
  81.0 1.5 %collective-permute-start.20 = (bf16[4,16,5632]{2,1,0:T(8,128)(2,1)}, bf16[4,16,5632]{2,1,0:T(8,128)(2,1)}, u32[]{:S(2)}, u32[]{:S(2)}) collective-permute-start(bf16[4,16,5632]{2,1,0:T(8,128)(2,1)} %collective-permute-done.14.refs_3_), channel_id=1, source_target_pairs={{0,4},{4,0},{1,5},{5,1},{2,6},{6,2},{3,7},{7,3},{8,12},{12,8},{9,1... | collective-permute-start | bytes 2162696 | tf_op jit(solution)/shard_map/ppermute | solution.py:42
  82.6 2.3 %collective-permute-start.25 = (bf16[4,128,640]{2,1,0:T(8,128)(2,1)S(1)}, bf16[4,128,640]{2,1,0:T(8,128)(2,1)}, u32[]{:S(2)}, u32[]{:S(2)}) collective-permute-start(bf16[4,128,640]{2,1,0:T(8,128)(2,1)S(1)} %collective-permute-done.17.refs_14_), channel_id=1, source_target_pairs={{0,3},{4,5},{1,2},{5,4},{2,1},{6,7},{3,0},{7,6},{8,11},{12,13},{9,... | collective-permute-start | bytes 1966088 | tf_op jit(solution)/shard_map/ppermute | solution.py:292
  85.0 2.6 %collective-permute-done.22.refs_7_ = bf16[2,16,5632]{2,1,0:T(8,128)(2,1)S(1)} collective-permute-done((bf16[2,16,5632]{2,1,0:T(8,128)(2,1)S(1)}, bf16[2,16,5632]{2,1,0:T(8,128)(2,1)S(1)}, u32[]{:S(2)}, u32[]{:S(2)}) %collective-permute-start.22) | collective-permute-done | bytes 360480 | tf_op jit(solution)/shard_map/ppermute | solution.py:287
  87.6 3.5 %collective-permute-start.23 = (bf16[2,16,5632]{2,1,0:T(8,128)(2,1)S(1)}, bf16[2,16,5632]{2,1,0:T(8,128)(2,1)}, u32[]{:S(2)}, u32[]{:S(2)}) collective-permute-start(bf16[2,16,5632]{2,1,0:T(8,128)(2,1)S(1)} %collective-permute-done.22.refs_7_), channel_id=1, source_target_pairs={{0,4},{4,0},{1,5},{5,1},{2,6},{6,2},{3,7},{7,3},{8,12},{12,8},{9,1... | collective-permute-start | bytes 1081352 | tf_op jit(solution)/shard_map/ppermute | solution.py:42
  91.1 1.5 %collective-permute-done.24.refs_12_ = bf16[4,128,640]{2,1,0:T(8,128)(2,1)} collective-permute-done((bf16[4,128,640]{2,1,0:T(8,128)(2,1)}, bf16[4,128,640]{2,1,0:T(8,128)(2,1)}, u32[]{:S(2)}, u32[]{:S(2)}) %collective-permute-start.24) | collective-permute-done | bytes 655392 | tf_op jit(solution)/shard_map/ppermute | solution.py:291
  93.3 15.4 %row_maxima.1 = f32[16,8,384]{2,1,0:T(8,128)} custom-call(s32[4]{0:T(128)S(1)} %pad_add_fusion.place_ref, bf16[4,16,5632]{2,1,0:T(8,128)(2,1)} %join_cores.1.refs_0_, bf16[4,16,5632]{2,1,0:T(8,128)(2,1)} %copy-done.3, bf16[4,16,5632]{2,1,0:T(8,128)(2,1)} %copy-done.4, bf16[4,16,5632]{2,1,0:T(8,128)(2,1)} %collective-permute-done.14.refs_3_, ...), custom_call_target="tpu_custom_call" | custom-call | flops 11274289152 | bytes 12582912 | tf_op jit(solution)/shard_map/row_maxima/pallas_call | solution.py:254
  108.7 6.7 %all-to-all-start = ((f32[16,8,384]{2,1,0:T(8,128)}), f32[16,8,384]{2,1,0:T(8,128)S(1)}, u32[]{:S(2)}, u32[]{:S(2)}) async-start(f32[16,8,384]{2,1,0:T(8,128)} %row_maxima.1), calls=%async_computation | async-start | bytes 393216 | tf_op jit(solution)/shard_map/all_to_all | solution.py:372
  116.1 6.1 %all-to-all-done = f32[16,8,384]{2,1,0:T(8,128)S(1)} async-done(((f32[16,8,384]{2,1,0:T(8,128)}), f32[16,8,384]{2,1,0:T(8,128)S(1)}, u32[]{:S(2)}, u32[]{:S(2)}) %all-to-all-start) | async-done | bytes 196640 | tf_op jit(solution)/shard_map/all_to_all | solution.py:372
  122.8 4.5 %all-to-all-start.1 = ((f32[4,32,128]{2,1,0:T(8,128)}), f32[4,32,128]{2,1,0:T(8,128)S(1)}, u32[]{:S(2)}, u32[]{:S(2)}) async-start(f32[4,32,128]{2,1,0:T(8,128)} %broadcast_in_dim.8), calls=%async_computation.1 | async-start | bytes 131072 | tf_op jit(solution)/shard_map/all_to_all | solution.py:375
  127.8 6.3 %all-to-all-done.1.tops_ref = f32[4,32,128]{2,1,0:T(8,128)S(1)} async-done(((f32[4,32,128]{2,1,0:T(8,128)}), f32[4,32,128]{2,1,0:T(8,128)S(1)}, u32[]{:S(2)}, u32[]{:S(2)}) %all-to-all-start.1) | async-done | bytes 65568 | tf_op jit(solution)/shard_map/all_to_all | solution.py:375
  134.7 1.8 %scaled_weights.1 = (bf16[24,4096]{1,0:T(8,128)(2,1)}, bf16[24,2048]{1,0:T(8,128)(2,1)}, bf16[8,4096]{1,0:T(8,128)(2,1)}, f32[1,32]{1,0:T(1,128)}) custom-call(f32[1]{0:T(128)S(6)} %copy.18.threshold_ref, f32[4,32,128]{2,1,0:T(8,128)} %copy-done.2, bf16[24,4096]{1,0:T(8,128)(2,1)} %wn_ref.2, bf16[24,2048]{1,0:T(8,128)(2,1)} %wr_ref.2, bf16[8,4096]{1,0:T(8,128)(2,1)} %wk_ref.2), custom_call_target="tpu_custom_call" | custom-call | tf_op jit(solution)/shard_map/scaled_weights/pallas_call | solution.py:355
  (60 shorter events, 13.8 us)
Async XLA Ops:
  2.6 7.4 %copy-start.5 = (bf16[256,640]{1,0:T(8,128)(2,1)S(1)}, bf16[256,640]{1,0:T(8,128)(2,1)}, u32[]{:S(2)}) copy-start(bf16[256,640]{1,0:T(8,128)(2,1)} %get-tuple-element.34) | copy-start | bytes 983044
  4.4 15.8 %collective-permute-start = (bf16[8,5632]{1,0:T(8,128)(2,1)}, bf16[8,5632]{1,0:T(8,128)(2,1)S(1)}, u32[]{:S(2)}, u32[]{:S(2)}) collective-permute-start(bf16[8,5632]{1,0:T(8,128)(2,1)} %get-tuple-element.39), channel_id=1, source_target_pairs={{0,64},{64,128},{128,192},{192,0},{1,65},{65,129},{129,193},{193,1... | collective-permute-start | bytes 270344 | tf_op jit(solution)/shard_map/ppermute | solution.py:42
  6.4 13.8 %collective-permute-start.1 = (bf16[8,5632]{1,0:T(8,128)(2,1)}, bf16[8,5632]{1,0:T(8,128)(2,1)S(1)}, u32[]{:S(2)}, u32[]{:S(2)}) collective-permute-start(bf16[8,5632]{1,0:T(8,128)(2,1)} %get-tuple-element.40), channel_id=1, source_target_pairs={{0,128},{64,192},{128,0},{192,64},{1,129},{65,193},{129,1},{193,65... | collective-permute-start | bytes 270344 | tf_op jit(solution)/shard_map/ppermute | solution.py:42
  8.9 11.3 %collective-permute-start.2 = (bf16[8,5632]{1,0:T(8,128)(2,1)}, bf16[8,5632]{1,0:T(8,128)(2,1)S(1)}, u32[]{:S(2)}, u32[]{:S(2)}) collective-permute-start(bf16[8,5632]{1,0:T(8,128)(2,1)} %get-tuple-element.41), channel_id=1, source_target_pairs={{0,192},{64,0},{128,64},{192,128},{1,193},{65,1},{129,65},{193,129... | collective-permute-start | bytes 270344 | tf_op jit(solution)/shard_map/ppermute | solution.py:42
  10.0 12.9 %collective-permute-start.4 = (bf16[256,640]{1,0:T(8,128)(2,1)S(1)}, bf16[256,640]{1,0:T(8,128)(2,1)S(1)}, u32[]{:S(2)}, u32[]{:S(2)}) collective-permute-start(bf16[256,640]{1,0:T(8,128)(2,1)S(1)} %copy-done.5), channel_id=1, source_target_pairs={{0,0},{4,64},{8,128},{12,192},{16,16},{20,80},{24,144},{28,208},{3... | collective-permute-start | bytes 983048 | tf_op jit(solution)/shard_map/ppermute | solution.py:297
  13.6 13.0 %collective-permute-start.5 = (bf16[256,256]{1,0:T(8,128)(2,1)}, bf16[256,256]{1,0:T(8,128)(2,1)S(1)}, u32[]{:S(2)}, u32[]{:S(2)}) collective-permute-start(bf16[256,256]{1,0:T(8,128)(2,1)} %get-tuple-element.42), channel_id=1, source_target_pairs={{4,80},{8,144},{12,208},{20,96},{24,160},{28,224},{36,112},{40,176... | collective-permute-start | bytes 393224 | tf_op jit(solution)/shard_map/ppermute | solution.py:296
  21.2 5.5 %copy-start = (bf16[4,8,5632]{2,1,0:T(8,128)(2,1)}, bf16[4,8,5632]{2,1,0:T(8,128)(2,1)S(1)}, u32[]{:S(2)}) copy-start(bf16[4,8,5632]{2,1,0:T(8,128)(2,1)S(1)} %pad_maximum_fusion.2.mine_ref) | copy-start | bytes 1081348
  21.2 5.5 %collective-permute-start.3 = (bf16[4,8,5632]{2,1,0:T(8,128)(2,1)S(1)}, bf16[4,8,5632]{2,1,0:T(8,128)(2,1)S(1)}, u32[]{:S(2)}, u32[]{:S(2)}) collective-permute-start(bf16[4,8,5632]{2,1,0:T(8,128)(2,1)S(1)} %pad_maximum_fusion.2.mine_ref), channel_id=1, source_target_pairs={{0,4},{4,0},{1,5},{5,1},{2,6},{6,2},{3,7},{7,3},{8,12},{12,8},{9,1... | collective-permute-start | bytes 1081352 | tf_op jit(solution)/shard_map/ppermute | solution.py:42
  29.4 15.8 %collective-permute-start.10 = (bf16[4,16,5632]{2,1,0:T(8,128)(2,1)}, bf16[4,16,5632]{2,1,0:T(8,128)(2,1)S(1)}, u32[]{:S(2)}, u32[]{:S(2)}) collective-permute-start(bf16[4,16,5632]{2,1,0:T(8,128)(2,1)} %join_cores.1.refs_0_), channel_id=1, source_target_pairs={{0,8},{4,60},{8,16},{12,4},{16,24},{20,12},{24,32},{28,20},{32,40}... | collective-permute-start | bytes 2162696 | tf_op jit(solution)/shard_map/ppermute | solution.py:287
  36.7 8.2 %collective-permute-start.8 = (bf16[128,1152]{1,0:T(8,128)(2,1)S(1)}, bf16[128,1152]{1,0:T(8,128)(2,1)S(1)}, u32[]{:S(2)}, u32[]{:S(2)}) collective-permute-start(bf16[128,1152]{1,0:T(8,128)(2,1)S(1)} %get-tuple-element.44.refs_17_), channel_id=1, source_target_pairs={{0,64},{4,196},{64,0},{68,132},{128,192},{132,68},{192,128},{196,4... | collective-permute-start | bytes 884744 | tf_op jit(solution)/shard_map/ppermute | solution.py:291
  38.0 6.9 %collective-permute-start.9 = (bf16[128,1152]{1,0:T(8,128)(2,1)S(1)}, bf16[128,1152]{1,0:T(8,128)(2,1)S(1)}, u32[]{:S(2)}, u32[]{:S(2)}) collective-permute-start(bf16[128,1152]{1,0:T(8,128)(2,1)S(1)} %get-tuple-element.44.refs_17_), channel_id=1, source_target_pairs={{0,192},{4,68},{64,128},{68,4},{128,64},{132,196},{192,0},{196,132... | collective-permute-start | bytes 884744 | tf_op jit(solution)/shard_map/ppermute | solution.py:291
  38.0 5.5 %collective-permute-start.6 = (bf16[128,640]{1,0:T(8,128)(2,1)S(1)}, bf16[128,640]{1,0:T(8,128)(2,1)S(1)}, u32[]{:S(2)}, u32[]{:S(2)}) collective-permute-start(bf16[128,640]{1,0:T(8,128)(2,1)S(1)} %pad_maximum_fusion.3), channel_id=1, source_target_pairs={{0,1},{4,7},{1,0},{5,6},{2,3},{6,5},{3,2},{7,4},{8,9},{12,15},{9,8... | collective-permute-start | bytes 491528 | tf_op jit(solution)/shard_map/ppermute | solution.py:292
  40.8 4.2 %collective-permute-start.7 = (bf16[128,640]{1,0:T(8,128)(2,1)S(1)}, bf16[128,640]{1,0:T(8,128)(2,1)S(1)}, u32[]{:S(2)}, u32[]{:S(2)}) collective-permute-start(bf16[128,640]{1,0:T(8,128)(2,1)S(1)} %pad_maximum_fusion.3), channel_id=1, source_target_pairs={{0,3},{4,5},{1,2},{5,4},{2,1},{6,7},{3,0},{7,6},{8,11},{12,13},{9,... | collective-permute-start | bytes 491528 | tf_op jit(solution)/shard_map/ppermute | solution.py:292
  45.2 11.7 %copy-start.3 = (bf16[4,16,5632]{2,1,0:T(8,128)(2,1)}, bf16[4,16,5632]{2,1,0:T(8,128)(2,1)S(1)}, u32[]{:S(2)}) copy-start(bf16[4,16,5632]{2,1,0:T(8,128)(2,1)S(1)} %collective-permute-done.10.refs_1_) | copy-start | bytes 2162692
  45.2 9.4 %collective-permute-start.11 = (bf16[4,16,5632]{2,1,0:T(8,128)(2,1)S(1)}, bf16[4,16,5632]{2,1,0:T(8,128)(2,1)S(1)}, u32[]{:S(2)}, u32[]{:S(2)}) collective-permute-start(bf16[4,16,5632]{2,1,0:T(8,128)(2,1)S(1)} %collective-permute-done.10.refs_1_), channel_id=1, source_target_pairs={{0,4},{4,0},{1,5},{5,1},{2,6},{6,2},{3,7},{7,3},{8,12},{12,8},{9,1... | collective-permute-start | bytes 2162696 | tf_op jit(solution)/shard_map/ppermute | solution.py:42
  45.2 11.7 %collective-permute-start.14 = (bf16[4,16,5632]{2,1,0:T(8,128)(2,1)S(1)}, bf16[4,16,5632]{2,1,0:T(8,128)(2,1)}, u32[]{:S(2)}, u32[]{:S(2)}) collective-permute-start(bf16[4,16,5632]{2,1,0:T(8,128)(2,1)S(1)} %collective-permute-done.10.refs_1_), channel_id=1, source_target_pairs={{0,8},{4,60},{8,16},{12,4},{16,24},{20,12},{24,32},{28,20},{32,40}... | collective-permute-start | bytes 2162696 | tf_op jit(solution)/shard_map/ppermute | solution.py:287
  48.7 6.0 %collective-permute-start.13 = (bf16[128,1152]{1,0:T(8,128)(2,1)S(1)}, bf16[128,1152]{1,0:T(8,128)(2,1)S(1)}, u32[]{:S(2)}, u32[]{:S(2)}) collective-permute-start(bf16[128,1152]{1,0:T(8,128)(2,1)S(1)} %collective-permute-done.8.refs_18_), channel_id=1, source_target_pairs={{0,192},{4,68},{64,128},{68,4},{128,64},{132,196},{192,0},{196,132... | collective-permute-start | bytes 884744 | tf_op jit(solution)/shard_map/ppermute | solution.py:291
  48.7 4.7 %collective-permute-start.12 = (bf16[128,640]{1,0:T(8,128)(2,1)S(1)}, bf16[128,640]{1,0:T(8,128)(2,1)S(1)}, u32[]{:S(2)}, u32[]{:S(2)}) collective-permute-start(bf16[128,640]{1,0:T(8,128)(2,1)S(1)} %collective-permute-done.6), channel_id=1, source_target_pairs={{0,3},{4,5},{1,2},{5,4},{2,1},{6,7},{3,0},{7,6},{8,11},{12,13},{9,... | collective-permute-start | bytes 491528 | tf_op jit(solution)/shard_map/ppermute | solution.py:292
  54.7 2.3 %copy-start.4 = (bf16[4,16,5632]{2,1,0:T(8,128)(2,1)}, bf16[4,16,5632]{2,1,0:T(8,128)(2,1)S(1)}, u32[]{:S(2)}) copy-start(bf16[4,16,5632]{2,1,0:T(8,128)(2,1)S(1)} %collective-permute-done.11.refs_2_) | copy-start | bytes 2162692
  57.1 14.6 %collective-permute-start.17 = (bf16[4,128,640]{2,1,0:T(8,128)(2,1)S(1)}, bf16[4,128,640]{2,1,0:T(8,128)(2,1)S(1)}, u32[]{:S(2)}, u32[]{:S(2)}) collective-permute-start(bf16[4,128,640]{2,1,0:T(8,128)(2,1)S(1)} %pad_maximum_fusion.1.refs_13_), channel_id=1, source_target_pairs={{0,1},{4,7},{1,0},{5,6},{2,3},{6,5},{3,2},{7,4},{8,9},{12,15},{9,8... | collective-permute-start | bytes 1966088 | tf_op jit(solution)/shard_map/ppermute | solution.py:292
  59.4 16.5 %collective-permute-start.18 = (bf16[4,128,640]{2,1,0:T(8,128)(2,1)S(1)}, bf16[4,128,640]{2,1,0:T(8,128)(2,1)}, u32[]{:S(2)}, u32[]{:S(2)}) collective-permute-start(bf16[4,128,640]{2,1,0:T(8,128)(2,1)S(1)} %pad_maximum_fusion.1.refs_13_), channel_id=1, source_target_pairs={{0,3},{4,5},{1,2},{5,4},{2,1},{6,7},{3,0},{7,6},{8,11},{12,13},{9,... | collective-permute-start | bytes 1966088 | tf_op jit(solution)/shard_map/ppermute | solution.py:292
  59.4 20.5 %collective-permute-start.19 = (bf16[4,16,5632]{2,1,0:T(8,128)(2,1)}, bf16[4,16,5632]{2,1,0:T(8,128)(2,1)}, u32[]{:S(2)}, u32[]{:S(2)}) collective-permute-start(bf16[4,16,5632]{2,1,0:T(8,128)(2,1)} %collective-permute-done.14.refs_3_), channel_id=1, source_target_pairs={{0,8},{4,60},{8,16},{12,4},{16,24},{20,12},{24,32},{28,20},{32,40}... | collective-permute-start | bytes 2162696 | tf_op jit(solution)/shard_map/ppermute | solution.py:287
  62.8 16.9 %collective-permute-start.15 = (bf16[4,128,640]{2,1,0:T(8,128)(2,1)S(1)}, bf16[4,128,640]{2,1,0:T(8,128)(2,1)}, u32[]{:S(2)}, u32[]{:S(2)}) collective-permute-start(bf16[4,128,640]{2,1,0:T(8,128)(2,1)S(1)} %pad_maximum_fusion.refs_9_), channel_id=1, source_target_pairs={{0,64},{4,196},{64,0},{68,132},{128,192},{132,68},{192,128},{196,4... | collective-permute-start | bytes 1966088 | tf_op jit(solution)/shard_map/ppermute | solution.py:291
  64.1 15.8 %collective-permute-start.16 = (bf16[4,128,640]{2,1,0:T(8,128)(2,1)S(1)}, bf16[4,128,640]{2,1,0:T(8,128)(2,1)}, u32[]{:S(2)}, u32[]{:S(2)}) collective-permute-start(bf16[4,128,640]{2,1,0:T(8,128)(2,1)S(1)} %pad_maximum_fusion.refs_9_), channel_id=1, source_target_pairs={{0,192},{4,68},{64,128},{68,4},{128,64},{132,196},{192,0},{196,132... | collective-permute-start | bytes 1966088 | tf_op jit(solution)/shard_map/ppermute | solution.py:291
  80.9 6.6 %collective-permute-start.22 = (bf16[2,16,5632]{2,1,0:T(8,128)(2,1)S(1)}, bf16[2,16,5632]{2,1,0:T(8,128)(2,1)S(1)}, u32[]{:S(2)}, u32[]{:S(2)}) collective-permute-start(bf16[2,16,5632]{2,1,0:T(8,128)(2,1)S(1)} %constant_dynamic-slice_fusion), channel_id=1, source_target_pairs={{0,8},{4,60},{8,16},{12,4},{16,24},{20,12},{24,32},{28,20},{32,40}... | collective-permute-start | bytes 1081352 | tf_op jit(solution)/shard_map/ppermute | solution.py:287
  81.0 12.3 %collective-permute-start.20 = (bf16[4,16,5632]{2,1,0:T(8,128)(2,1)}, bf16[4,16,5632]{2,1,0:T(8,128)(2,1)}, u32[]{:S(2)}, u32[]{:S(2)}) collective-permute-start(bf16[4,16,5632]{2,1,0:T(8,128)(2,1)} %collective-permute-done.14.refs_3_), channel_id=1, source_target_pairs={{0,4},{4,0},{1,5},{5,1},{2,6},{6,2},{3,7},{7,3},{8,12},{12,8},{9,1... | collective-permute-start | bytes 2162696 | tf_op jit(solution)/shard_map/ppermute | solution.py:42
  82.5 10.8 %collective-permute-start.21 = (bf16[4,16,5632]{2,1,0:T(8,128)(2,1)}, bf16[4,16,5632]{2,1,0:T(8,128)(2,1)}, u32[]{:S(2)}, u32[]{:S(2)}) collective-permute-start(bf16[4,16,5632]{2,1,0:T(8,128)(2,1)} %collective-permute-done.19.refs_5_), channel_id=1, source_target_pairs={{0,4},{4,0},{1,5},{5,1},{2,6},{6,2},{3,7},{7,3},{8,12},{12,8},{9,1... | collective-permute-start | bytes 2162696 | tf_op jit(solution)/shard_map/ppermute | solution.py:42
  82.6 10.0 %collective-permute-start.24 = (bf16[4,128,640]{2,1,0:T(8,128)(2,1)}, bf16[4,128,640]{2,1,0:T(8,128)(2,1)}, u32[]{:S(2)}, u32[]{:S(2)}) collective-permute-start(bf16[4,128,640]{2,1,0:T(8,128)(2,1)} %collective-permute-done.15.refs_10_), channel_id=1, source_target_pairs={{0,192},{4,68},{64,128},{68,4},{128,64},{132,196},{192,0},{196,132... | collective-permute-start | bytes 1966088 | tf_op jit(solution)/shard_map/ppermute | solution.py:291
  82.6 10.7 %collective-permute-start.25 = (bf16[4,128,640]{2,1,0:T(8,128)(2,1)S(1)}, bf16[4,128,640]{2,1,0:T(8,128)(2,1)}, u32[]{:S(2)}, u32[]{:S(2)}) collective-permute-start(bf16[4,128,640]{2,1,0:T(8,128)(2,1)S(1)} %collective-permute-done.17.refs_14_), channel_id=1, source_target_pairs={{0,3},{4,5},{1,2},{5,4},{2,1},{6,7},{3,0},{7,6},{8,11},{12,13},{9,... | collective-permute-start | bytes 1966088 | tf_op jit(solution)/shard_map/ppermute | solution.py:292
  87.6 5.8 %collective-permute-start.23 = (bf16[2,16,5632]{2,1,0:T(8,128)(2,1)S(1)}, bf16[2,16,5632]{2,1,0:T(8,128)(2,1)}, u32[]{:S(2)}, u32[]{:S(2)}) collective-permute-start(bf16[2,16,5632]{2,1,0:T(8,128)(2,1)S(1)} %collective-permute-done.22.refs_7_), channel_id=1, source_target_pairs={{0,4},{4,0},{1,5},{5,1},{2,6},{6,2},{3,7},{7,3},{8,12},{12,8},{9,1... | collective-permute-start | bytes 1081352 | tf_op jit(solution)/shard_map/ppermute | solution.py:42
  108.7 13.4 %all-to-all-start = ((f32[16,8,384]{2,1,0:T(8,128)}), f32[16,8,384]{2,1,0:T(8,128)S(1)}, u32[]{:S(2)}, u32[]{:S(2)}) async-start(f32[16,8,384]{2,1,0:T(8,128)} %row_maxima.1), calls=%async_computation | async-start | bytes 393216 | tf_op jit(solution)/shard_map/all_to_all | solution.py:372
  122.8 11.3 %all-to-all-start.1 = ((f32[4,32,128]{2,1,0:T(8,128)}), f32[4,32,128]{2,1,0:T(8,128)S(1)}, u32[]{:S(2)}, u32[]{:S(2)}) async-start(f32[4,32,128]{2,1,0:T(8,128)} %broadcast_in_dim.8), calls=%async_computation.1 | async-start | bytes 131072 | tf_op jit(solution)/shard_map/all_to_all | solution.py:375
  (2 other events, 1.4 us)
